TPU v7x, 32 devices: a whole 2x2x4 slice. The times are simulated.
32 devices in a mesh: videos: 2 (over y), rows: 4 (over z), cols: 4 (over x, core).
Axes of the slice: x: 2, y: 2, z: 4, core: 2. Of those that a mesh axis runs over, the one named last changes fastest.
Arguments:
- hidden: bfloat16 [2, 16, 128, 384], P('videos', 'rows', 'cols'), parts along dimension 0, may hold values from -40 to 40
- frame_cache: bfloat16 [2, 2, 16, 128, 384], P('videos', None, 'rows', 'cols'), parts along dimension 0, may hold values from -6 to 6
- shortcut: bfloat16 [2, 16, 128, 384], P('videos', 'rows', 'cols'), parts along dimension 0, may hold values from -40 to 40
- gain_one: float32 [384], replicated, may hold values from 0.5 to 1.5
- conv_weight: bfloat16 [3, 3, 3, 384, 384], replicated, may hold values from -0.0625 to 0.0625
- conv_bias: float32 [384], replicated, may hold values from -2 to 2
- gain_two: float32 [384], replicated, may hold values from 0.5 to 1.5
- query_weight: bfloat16 [384, 384], replicated, may hold values from -1 to 1
- query_bias: float32 [384], replicated, may hold values from -3 to 3
- key_weight: bfloat16 [384, 384], replicated, may hold values from -1 to 1
- value_weight: bfloat16 [384, 384], replicated, may hold values from -0.3125 to 0.3125
- value_bias: float32 [384], replicated, may hold values from -3 to 3
- out_weight: bfloat16 [384, 384], replicated, may hold values from -0.3125 to 0.3125
- out_bias: float32 [384], replicated, may hold values from -2 to 2
Outputs:
- decoded: bfloat16 [2, 16, 128, 384], P('videos', 'rows', 'cols'), parts along dimension 0
There are 2 independent parts, one for each index of `videos`. A program takes and returns all parts, laid end to end along the dimension named above; an argument that names none is the same for every part. Nothing has to cross between parts.
All inputs are finite; a program needn't handle non-finite values.
Results may differ from a plain program's by a relative error of at most 0.0065.
Values may be sent and summed in bfloat16 or wider, within the bound.
No kernel may reach another device: no remote copies, remote signals or barrier semaphores. Data moves between devices by JAX's collectives and lax.ppermute only.
A program may use at most 128 MiB of HBM per device.

v0:
```python
import jax
import jax.numpy as jnp
from jax import lax
from jax.sharding import PartitionSpec as P

norm_epsilon = 1e-06


def padded(cells, sides, width):
    for axis, dim in sides:
        count = lax.axis_size(axis)
        ends = count - 1
        head = lax.slice_in_dim(cells, 0, width, axis=dim)
        tail = lax.slice_in_dim(cells, cells.shape[dim] - width, cells.shape[dim], axis=dim)
        cells = jnp.concatenate(
            [
                lax.ppermute(tail, axis, [(i, (i + 1) % count) for i in range(ends)]),
                cells,
                lax.ppermute(head, axis, [((i + 1) % count, i) for i in range(ends)]),
            ],
            axis=dim,
        )
    return cells


def normalize(field_rows, gain):
    mean_square = jnp.mean(field_rows * field_rows, axis=1, keepdims=True)
    return field_rows * lax.rsqrt(mean_square + norm_epsilon) * gain


def per_device(
    hidden,
    frame_cache,
    shortcut,
    gain_one,
    conv_weight,
    conv_bias,
    gain_two,
    query_weight,
    query_bias,
    key_weight,
    value_weight,
    value_bias,
    out_weight,
    out_bias,
):
    tile_rows = hidden.shape[1]
    tile_cols = hidden.shape[2]
    channels = hidden.shape[3]
    current = hidden[0].reshape(tile_rows * tile_cols, channels).astype(jnp.float32)
    activated = jax.nn.silu(normalize(current, gain_one)).astype(jnp.bfloat16)
    stacked = jnp.concatenate(
        [frame_cache[0], activated.reshape(1, tile_rows, tile_cols, channels)], axis=0
    )
    rimmed = padded(stacked, (("rows", 1), ("cols", 2)), 1)
    convolved = (
        lax.conv_general_dilated(
            rimmed[None],
            conv_weight,
            (1, 1, 1),
            "VALID",
            dimension_numbers=("NDHWC", "DHWIO", "NDHWC"),
            preferred_element_type=jnp.float32,
        )[0, 0]
        + conv_bias
    )
    mixed = (
        (shortcut[0].astype(jnp.float32) + convolved)
        .astype(jnp.bfloat16)
        .reshape(tile_rows * tile_cols, channels)
    )
    normed = normalize(mixed.astype(jnp.float32), gain_two).astype(jnp.bfloat16)
    queries = (
        jnp.dot(normed, query_weight, preferred_element_type=jnp.float32) + query_bias
    ).astype(jnp.bfloat16)
    score_scale = float(channels) ** (-0.5)
    query_count = queries.shape[0]
    piece = lax.all_gather(normed, ("rows", "cols"), axis=0, tiled=True)
    key_rows = jnp.dot(piece, key_weight, preferred_element_type=jnp.float32).astype(jnp.bfloat16)
    value_rows = (
        jnp.dot(piece, value_weight, preferred_element_type=jnp.float32) + value_bias
    ).astype(jnp.bfloat16)
    running_max = jnp.full((query_count,), -1e30, jnp.float32)
    scores = (
        jnp.einsum("qc,kc->qk", queries, key_rows, preferred_element_type=jnp.float32) * score_scale
    )
    new_max = jnp.maximum(running_max, jnp.max(scores, axis=1))
    expos = jnp.exp(scores - new_max[:, None])
    new_sum = jnp.sum(expos, axis=1)
    new_weighted = jnp.dot(
        expos.astype(jnp.bfloat16), value_rows, preferred_element_type=jnp.float32
    )
    attended = (new_weighted / new_sum[:, None]).astype(jnp.bfloat16)
    projected = jnp.dot(attended, out_weight, preferred_element_type=jnp.float32) + out_bias
    decoded = (mixed.astype(jnp.float32) + projected).astype(jnp.bfloat16)
    return decoded.reshape(1, tile_rows, tile_cols, channels)


def solution(mesh):
    placed = (
        P("videos", "rows", "cols", None),
        P("videos", None, "rows", "cols", None),
        P("videos", "rows", "cols", None),
        P(),
        P(),
        P(),
        P(),
        P(),
        P(),
        P(),
        P(),
        P(),
        P(),
        P(),
    )
    return jax.shard_map(
        per_device,
        mesh=mesh,
        in_specs=placed,
        out_specs=P("videos", "rows", "cols", None),
        check_vma=False,
    )
```

profile of v0, /device:TPU:0, one launch (start us, length us, event | category | flops | bytes accessed | tf_op | source)
XLA Modules:
  0.0 91.4 jit_solution(13943314025765096930)
XLA Ops:
  6.5 0.0 copy-start
  6.5 0.0 all-gather.2.cloned.1.call-start
  6.5 1.0 %fusion.18 = f32[4,32]{1,0:T(4,128)S(1)} fusion(bf16[1,4,32,384]{3,2,1,0:T(8,128)(2,1)} %param.14), kind=kLoop, calls=%fused_computation.28 | loop fusion | flops 147328 | bytes 98816 | tf_op jit(solution)/shard_map/reduce_sum | solution.py:27
  7.6 1.0 %fusion.25 = bf16[1,4,32,384]{3,2,1,0:T(8,128)(2,1)S(1)} fusion(bf16[1,4,32,384]{3,2,1,0:T(8,128)(2,1)} %param.14, f32[384]{0:T(512)} %param.17, f32[4,32]{1,0:T(4,128)S(1)} %add_rsqrt_fusion.1), kind=kLoop, calls=%fused_computation.35 | loop fusion | flops 393216 | bytes 198656 | tf_op jit(solution)/shard_map/convert_element_type | solution.py:51
  8.6 0.9 pad_maximum_fusion.1
  9.5 5.0 %collective-permute-start = (bf16[3,1,32,384]{3,2,1,0:T(8,128)(2,1)S(1)}, bf16[3,1,32,384]{3,2,1,0:T(8,128)(2,1)S(1)}, u32[]{:S(2)}, u32[]{:S(2)}) collective-permute-start(bf16[3,1,32,384]{3,2,1,0:T(8,128)(2,1)S(1)} %get-tuple-element.9), channel_id=1, source_target_pairs={{0,4},{4,8},{8,12},{1,5},{5,9},{9,13},{2,6},{6,10},{10,14},{3,7},{... | collective-permute-start | bytes 221192 | tf_op jit(solution)/shard_map/ppermute | solution.py:17
  14.4 1.3 %collective-permute-start.1 = (bf16[3,1,32,384]{3,2,1,0:T(8,128)(2,1)S(1)}, bf16[3,1,32,384]{3,2,1,0:T(8,128)(2,1)S(1)}, u32[]{:S(2)}, u32[]{:S(2)}) collective-permute-start(bf16[3,1,32,384]{3,2,1,0:T(8,128)(2,1)S(1)} %get-tuple-element.10), channel_id=1, source_target_pairs={{4,0},{8,4},{12,8},{5,1},{9,5},{13,9},{6,2},{10,6},{14,10},{7,3},{... | collective-permute-start | bytes 221192 | tf_op jit(solution)/shard_map/ppermute | solution.py:19
  15.7 0.7 collective-permute-done
  16.4 4.3 %collective-permute-done.1 = bf16[3,1,32,384]{3,2,1,0:T(8,128)(2,1)S(1)} collective-permute-done((bf16[3,1,32,384]{3,2,1,0:T(8,128)(2,1)S(1)}, bf16[3,1,32,384]{3,2,1,0:T(8,128)(2,1)S(1)}, u32[]{:S(2)}, u32[]{:S(2)}) %collective-permute-start.1) | collective-permute-done | bytes 73760 | tf_op jit(solution)/shard_map/ppermute | solution.py:19
  20.7 0.9 pad_maximum_fusion.5
  21.6 1.3 %collective-permute-start.2 = (bf16[3,6,1,384]{3,2,1,0:T(2,128)(2,1)S(1)}, bf16[3,6,1,384]{3,2,1,0:T(2,128)(2,1)S(1)}, u32[]{:S(2)}, u32[]{:S(2)}) collective-permute-start(bf16[3,6,1,384]{3,2,1,0:T(2,128)(2,1)S(1)} %get-tuple-element.7), channel_id=1, source_target_pairs={{0,1},{1,2},{2,3},{4,5},{5,6},{6,7},{8,9},{9,10},{10,11},{12,13},{... | collective-permute-start | bytes 41480 | tf_op jit(solution)/shard_map/ppermute | solution.py:17
  22.9 1.3 %collective-permute-start.3 = (bf16[3,6,1,384]{3,2,1,0:T(2,128)(2,1)S(1)}, bf16[3,6,1,384]{3,2,1,0:T(2,128)(2,1)S(1)}, u32[]{:S(2)}, u32[]{:S(2)}) collective-permute-start(bf16[3,6,1,384]{3,2,1,0:T(2,128)(2,1)S(1)} %get-tuple-element.8), channel_id=1, source_target_pairs={{1,0},{2,1},{3,2},{5,4},{6,5},{7,6},{9,8},{10,9},{11,10},{13,12},{... | collective-permute-start | bytes 41480 | tf_op jit(solution)/shard_map/ppermute | solution.py:19
  24.2 0.0 collective-permute-done.2
  24.2 3.5 %collective-permute-done.3 = bf16[3,6,1,384]{3,2,1,0:T(2,128)(2,1)S(1)} collective-permute-done((bf16[3,6,1,384]{3,2,1,0:T(2,128)(2,1)S(1)}, bf16[3,6,1,384]{3,2,1,0:T(2,128)(2,1)S(1)}, u32[]{:S(2)}, u32[]{:S(2)}) %collective-permute-start.3) | collective-permute-done | bytes 13856 | tf_op jit(solution)/shard_map/ppermute | solution.py:19
  27.7 1.2 %maximum_bitcast_fusion = bf16[3,6,1,34,384]{4,3,1,0,2:T(8,128)(2,1)S(1)} fusion(bf16[3,6,1,384]{3,2,1,0:T(2,128)(2,1)S(1)} %collective-permute-done.3, bf16[3,1,32,384]{3,2,1,0:T(8,128)(2,1)S(1)} %collective-permute-done.1, bf16[1,4,32,384]{3,2,1,0:T(8,128)(2,1)S(1)} %fusion.25, bf16[2,4,32,384]{3,2,1,0:T(8,128)(2,1)} %bitcast.40, ...), kind=kLoop, calls=%fused_computation.22 | loop fusion | flops 2820096 | bytes 940032 | tf_op jit(solution)/shard_map/broadcast_in_dim | solution.py:58
  28.9 0.1 copy.48
  29.0 0.0 copy-start.10
  29.0 0.1 pad.clone
  29.1 0.1 copy.41
  29.2 0.1 slice.18
  29.3 0.4 copy-done.10
  29.7 0.0 copy-start.1
  29.7 0.0 copy-start.4
  29.7 5.2 %convolution_select_fusion = f32[1,4,8,5,384]{4,2,3,1,0:T(8,128)S(1)} fusion(bf16[3,3,3,384,384]{4,3,2,1,0:T(8,128)(2,1)} %param.18, bf16[3,6,1,7,2,384]{5,3,4,1,0,2:T(8,128)(2,1)S(1)} %slice.18, bf16[3,6,1,8,5,384]{5,3,4,1,0,2:T(8,128)(2,1)S(1)} %copy.41, pred[8,5]{0,1:T(8,128)(4,1)S(1)} %copy-done.10), kind=kOutput, calls=%fused_computation.9 | convolution fusion | flops 1276403712 | bytes 8954920 | tf_op jit(solution)/shard_map/conv_general_dilated | solution.py:57
  34.9 0.0 copy-start.5
  34.9 0.0 copy-start.3
  34.9 0.0 copy-start.6
  34.9 0.1 copy.42
  35.0 0.0 copy-done.1
  35.0 0.0 copy-done.4
  35.1 0.1 multiply_reduce_fusion
  35.2 0.1 rsqrt.21
  35.3 0.3 copy-done.5
  35.6 0.7 fusion.27
  36.3 0.0 all-gather.2.cloned.1.call-update
  36.3 0.0 copy-done.3
  36.3 0.0 copy-done.6
  36.3 1.1 %fusion.3 = bf16[128,384]{1,0:T(8,128)(2,1)S(1)} fusion(bf16[128,384]{1,0:T(8,128)(2,1)} %get-tuple-element.5, bf16[384,384]{1,0:T(8,128)(2,1)S(1)} %copy-done.3, f32[384]{0:T(512)S(1)} %copy-done.6), kind=kOutput, calls=%fused_computation.10 | convolution fusion | flops 37847040 | bytes 493056 | tf_op jit(solution)/shard_map/dot_general | solution.py:74
  37.4 0.0 copy-start.9
  37.5 40.1 %all-gather.2.cloned.1.call-done = bf16[2048,384]{1,0:T(8,128)(2,1)} async-done(((bf16[128,384]{1,0:T(8,128)(2,1)}), bf16[2048,384]{1,0:T(8,128)(2,1)}) %all-gather.2.cloned.1.call-update) | async-done | bytes 1572880 | tf_op jit(solution)/shard_map/all_gather | solution.py:78
  77.6 0.0 copy-done
  77.6 0.0 copy-start.8
  77.6 3.1 %fusion.36 = (f32[128]{0:T(128)S(1)}, f32[128,2048]{1,0:T(8,128)S(1)}) fusion(bf16[128,384]{1,0:T(8,128)(2,1)S(1)} %fusion.3, bf16[2048,384]{1,0:T(8,128)(2,1)} %all-gather.2.cloned.1.call-done, bf16[384,384]{1,0:T(8,128)(2,1)S(1)} %copy-done), kind=kOutput, calls=%fused_computation.57 | convolution fusion | flops 806616960 | bytes 3015168 | tf_op jit(solution)/shard_map/qc,kc->qk/dot_general | solution.py:85
  80.7 0.3 fusion.7
  81.0 0.0 copy-done.9
  81.1 0.0 copy-done.8
  81.1 0.0 copy-start.2
  81.1 0.0 copy-start.7
  81.1 2.6 %fusion.6 = bf16[128,384]{1,0:T(8,128)(2,1)S(1)} fusion(bf16[2048,384]{1,0:T(8,128)(2,1)S(1)} %copy-done.8, bf16[384,384]{1,0:T(8,128)(2,1)} %param.24, f32[384]{0:T(512)S(1)} %copy-done.9, f32[128,2048]{1,0:T(8,128)S(1)} %get-tuple-element.12, f32[128]{0:T(128)S(1)} %broadcast_maximum_fusion, f32[128]{0:T(128)S(1)} %fusion.7), kind=kOutput, calls=%fused_computation.13 | convolution fusion | flops 807501824 | bytes 3017216 | tf_op jit(solution)/shard_map/dot_general | solution.py:90
  83.7 0.0 copy-done.2
  83.7 0.0 copy-done.7
  83.7 0.9 fusion.4
  (5 shorter events, 0.1 us)
Async XLA Ops:
  6.5 71.1 %copy-start = (bf16[384,384]{1,0:T(8,128)(2,1)S(1)}, bf16[384,384]{1,0:T(8,128)(2,1)}, u32[]{:S(2)}) copy-start(bf16[384,384]{1,0:T(8,128)(2,1)} %param.23) | copy-start | bytes 884740
  6.5 71.1 %all-gather.2.cloned.1.call-start = ((), (), s32[]{:S(2)}) async-start(), calls=%async_computation | async-start | bytes 1671168 | tf_op jit(solution)/shard_map/all_gather | solution.py:78
  9.5 6.9 %collective-permute-start = (bf16[3,1,32,384]{3,2,1,0:T(8,128)(2,1)S(1)}, bf16[3,1,32,384]{3,2,1,0:T(8,128)(2,1)S(1)}, u32[]{:S(2)}, u32[]{:S(2)}) collective-permute-start(bf16[3,1,32,384]{3,2,1,0:T(8,128)(2,1)S(1)} %get-tuple-element.9), channel_id=1, source_target_pairs={{0,4},{4,8},{8,12},{1,5},{5,9},{9,13},{2,6},{6,10},{10,14},{3,7},{... | collective-permute-start | bytes 221192 | tf_op jit(solution)/shard_map/ppermute | solution.py:17
  14.4 6.2 %collective-permute-start.1 = (bf16[3,1,32,384]{3,2,1,0:T(8,128)(2,1)S(1)}, bf16[3,1,32,384]{3,2,1,0:T(8,128)(2,1)S(1)}, u32[]{:S(2)}, u32[]{:S(2)}) collective-permute-start(bf16[3,1,32,384]{3,2,1,0:T(8,128)(2,1)S(1)} %get-tuple-element.10), channel_id=1, source_target_pairs={{4,0},{8,4},{12,8},{5,1},{9,5},{13,9},{6,2},{10,6},{14,10},{7,3},{... | collective-permute-start | bytes 221192 | tf_op jit(solution)/shard_map/ppermute | solution.py:19
  21.6 2.6 %collective-permute-start.2 = (bf16[3,6,1,384]{3,2,1,0:T(2,128)(2,1)S(1)}, bf16[3,6,1,384]{3,2,1,0:T(2,128)(2,1)S(1)}, u32[]{:S(2)}, u32[]{:S(2)}) collective-permute-start(bf16[3,6,1,384]{3,2,1,0:T(2,128)(2,1)S(1)} %get-tuple-element.7), channel_id=1, source_target_pairs={{0,1},{1,2},{2,3},{4,5},{5,6},{6,7},{8,9},{9,10},{10,11},{12,13},{... | collective-permute-start | bytes 41480 | tf_op jit(solution)/shard_map/ppermute | solution.py:17
  22.9 4.8 %collective-permute-start.3 = (bf16[3,6,1,384]{3,2,1,0:T(2,128)(2,1)S(1)}, bf16[3,6,1,384]{3,2,1,0:T(2,128)(2,1)S(1)}, u32[]{:S(2)}, u32[]{:S(2)}) collective-permute-start(bf16[3,6,1,384]{3,2,1,0:T(2,128)(2,1)S(1)} %get-tuple-element.8), channel_id=1, source_target_pairs={{1,0},{2,1},{3,2},{5,4},{6,5},{7,6},{9,8},{10,9},{11,10},{13,12},{... | collective-permute-start | bytes 41480 | tf_op jit(solution)/shard_map/ppermute | solution.py:19
  29.0 0.7 copy-start.10
  29.7 5.4 %copy-start.1 = (bf16[1,4,32,384]{3,2,1,0:T(8,128)(2,1)S(1)}, bf16[1,4,32,384]{3,2,1,0:T(8,128)(2,1)}, u32[]{:S(2)}) copy-start(bf16[1,4,32,384]{3,2,1,0:T(8,128)(2,1)} %param.16) | copy-start | bytes 294916
  29.7 5.4 %copy-start.4 = (f32[384]{0:T(512)S(1)}, f32[384]{0:T(512)}, u32[]{:S(2)}) copy-start(f32[384]{0:T(512)} %param.19) | copy-start | bytes 4612
  34.9 0.7 copy-start.5
  34.9 1.4 %copy-start.3 = (bf16[384,384]{1,0:T(8,128)(2,1)S(1)}, bf16[384,384]{1,0:T(8,128)(2,1)}, u32[]{:S(2)}) copy-start(bf16[384,384]{1,0:T(8,128)(2,1)} %param.21) | copy-start | bytes 884740
  34.9 1.4 %copy-start.6 = (f32[384]{0:T(512)S(1)}, f32[384]{0:T(512)}, u32[]{:S(2)}) copy-start(f32[384]{0:T(512)} %param.22) | copy-start | bytes 4612
  37.4 43.6 %copy-start.9 = (f32[384]{0:T(512)S(1)}, f32[384]{0:T(512)}, u32[]{:S(2)}) copy-start(f32[384]{0:T(512)} %param.25) | copy-start | bytes 4612
  77.6 3.5 %copy-start.8 = (bf16[2048,384]{1,0:T(8,128)(2,1)S(1)}, bf16[2048,384]{1,0:T(8,128)(2,1)}, u32[]{:S(2)}) copy-start(bf16[2048,384]{1,0:T(8,128)(2,1)} %all-gather.2.cloned.1.call-done) | copy-start | bytes 4718596
  81.1 2.6 %copy-start.2 = (bf16[384,384]{1,0:T(8,128)(2,1)S(1)}, bf16[384,384]{1,0:T(8,128)(2,1)}, u32[]{:S(2)}) copy-start(bf16[384,384]{1,0:T(8,128)(2,1)} %param.26) | copy-start | bytes 884740
  81.1 2.6 %copy-start.7 = (f32[384]{0:T(512)S(1)}, f32[384]{0:T(512)}, u32[]{:S(2)}) copy-start(f32[384]{0:T(512)} %param.27) | copy-start | bytes 4612
Sparse Core Ops, SparseCore 0:
  36.4 41.1 all-gather.1
where the time goes:
time: 91.8 us; the launch traced here: 91.4 us
  waiting for transfers between devices  48.6 us (53%)
  between operations  13.7 us (15%)
  matrix products  12.9 us (14%)
  starting transfers between devices  8.84 us (10%)
  other arithmetic  6.13 us (7%)
  local copies, waits for them, and re-layouts  1.27 us (1%)
    all_gather x1, waiting for transfers between devices, per_device(): piece = lax.all_gather(normed, ('rows', 'cols'), axis=0, tiled=True)  40.1 us
    ppermute x2, waiting for transfers between devices, padded(): lax.ppermute(head, axis, [((i + 1) % count, i) for i in range(ends)])  7.79 us
    ppermute x2, starting transfers between devices, padded(): lax.ppermute(tail, axis, [(i, (i + 1) % count) for i in range(ends)])  6.25 us
    conv_general_dilated x1, matrix products, per_device(): lax.conv_general_dilated(rimmed[None], conv_weight, (1, 1, 1), 'VALID', d...  5.21 us
    dot_general x1, matrix products, per_device(): jnp.einsum('qc,kc->qk', queries, key_rows, preferred_element_type=jnp.flo...  3.13 us
    ppermute x2, starting transfers between devices, padded(): lax.ppermute(head, axis, [((i + 1) % count, i) for i in range(ends)])  2.58 us
    dot_general x1, matrix products, per_device(): jnp.dot(expos.astype(jnp.bfloat16), value_rows, preferred_element_type=jn...  2.56 us
  transfers between devices with their start and end apart: 5, of which 4 were waited for; matrix products, arithmetic and copies ran while one was open for 1% of the time, Pallas kernels for 0%

commit v1 on v0

v1 whole, which is shorter than its diff:
```python
import functools

import jax
import jax.numpy as jnp
from jax import lax
from jax.experimental import pallas as pl
from jax.experimental.pallas import tpu as pltpu
from jax.sharding import PartitionSpec as P

norm_epsilon = 1e-06
stat_lanes = 128
f32 = jnp.float32
bf16 = jnp.bfloat16

VMEM = pl.BlockSpec(memory_space=pltpu.VMEM)
SMEM = pl.BlockSpec(memory_space=pltpu.SMEM)
ANY = pl.BlockSpec(memory_space=pl.ANY)


def near_pairs(count, first):
    pairs = []
    for i in range(first, count - 1, 2):
        pairs += [(i, i + 1), (i + 1, i)]
    return pairs


def far_pairs(count, step, stride=1):
    xor = count & (count - 1) == 0
    pairs = []
    for i in range(count):
        j = i ^ step if xor else (i + step) % count
        pairs += [(i * stride + k, j * stride + k) for k in range(stride)]
    return pairs


def normalize(cells, gain):
    mean_square = jnp.mean(cells * cells, axis=-1, keepdims=True)
    return cells * lax.rsqrt(mean_square + norm_epsilon) * gain


def activate(cells, gain):
    scaled = normalize(cells, gain)
    return scaled * (1.0 / (1.0 + jnp.exp(-scaled)))


def conv_kernel(
    tile_rows,
    tile_cols,
    channels,
    parity,
    cache,
    hidden,
    shortcut,
    row_a,
    row_b,
    col_a,
    col_b,
    gain_one,
    conv_bias,
    gain_two,
    weight,
    normed,
    mixed,
    held,
    stack,
    sems,
):
    copies = [
        pltpu.make_async_copy(weight.at[i], held.at[i], sems.at[i]) for i in range(9)
    ]
    for copy in copies:
        copy.start()
    row_even = parity[0] == 0
    col_even = parity[1] == 0
    place = lax.broadcasted_iota(jnp.int32, (tile_cols, channels), 0)
    reach = tile_rows + 2
    first = col_a[...].astype(f32)
    second = col_b[...].astype(f32)
    left_all = jnp.where(col_even, second, first)
    right_all = jnp.where(col_even, first, second)
    gain = gain_one[...]
    for f in range(3):
        left_rows = left_all[f * reach : (f + 1) * reach]
        right_rows = right_all[f * reach : (f + 1) * reach]
        if f == 2:
            left_rows = activate(left_rows, gain)
            right_rows = activate(right_rows, gain)
        for r in range(reach):
            if r == 0 or r == reach - 1:
                one, two = row_a[f].astype(f32), row_b[f].astype(f32)
                row = jnp.where(row_even, two, one) if r == 0 else jnp.where(row_even, one, two)
            elif f < 2:
                row = cache[0, f, r - 1].astype(f32)
            else:
                row = hidden[0, r - 1].astype(f32)
            if f == 2:
                row = activate(row, gain)
            from_left = jnp.where(place == 0, left_rows[r : r + 1], pltpu.roll(row, 1, 0))
            from_right = jnp.where(
                place == tile_cols - 1, right_rows[r : r + 1], pltpu.roll(row, tile_cols - 1, 0)
            )
            rows = pl.ds(r * tile_cols, tile_cols)
            stack[f, rows, 0:channels] = from_left.astype(bf16)
            stack[f, rows, channels : 2 * channels] = row.astype(bf16)
            stack[f, rows, 2 * channels : 3 * channels] = from_right.astype(bf16)
    total = jnp.zeros((tile_rows * tile_cols, channels), f32)
    for f in range(3):
        for a in range(3):
            copies[3 * f + a].wait()
            total += jnp.dot(
                stack[f, a * tile_cols : (a + tile_rows) * tile_cols, :],
                held[3 * f + a],
                preferred_element_type=f32,
            )
    convolved = total + conv_bias[...]
    residual = shortcut[...].astype(f32)
    kept = (residual + convolved).astype(bf16)
    mixed[...] = kept
    normed[...] = normalize(kept.astype(f32), gain_two[...]).astype(bf16)


def query_kernel(score_scale, parts, refs_in_out):
    sources = refs_in_out[:parts]
    query_weight, query_bias, key_weight, out = refs_in_out[parts:]
    at = 0
    for source in sources:
        rows = source.shape[0]
        queries = (
            jnp.dot(source[...], query_weight[...], preferred_element_type=f32) + query_bias[...]
        ).astype(bf16)
        turned = lax.dot_general(
            queries, key_weight[...], (((1,), (1,)), ((), ())), preferred_element_type=f32
        )
        out[at : at + rows] = (turned * score_scale).astype(bf16)
        at += rows


def pack(values, log_sum):
    lane = lax.broadcasted_iota(jnp.int32, (values.shape[0], stat_lanes), 1)
    high = log_sum.astype(bf16).astype(f32)
    rest = log_sum - high
    middle = rest.astype(bf16).astype(f32)
    low = rest - middle
    stats = jnp.where(
        lane == 0, high, jnp.where(lane == 1, middle, jnp.where(lane == 2, low, 0.0))
    )
    return values.astype(bf16), stats.astype(bf16)


def attend_kernel(blocks, kept_rows, chunk, *refs):
    queries = refs[0]
    keys = refs[1 : 1 + blocks]
    kept, kept_log, sent = refs[1 + blocks :]
    channels = queries.shape[1]
    for at in range(0, queries.shape[0], chunk):
        own = queries[at : at + chunk]
        scores = [
            lax.dot_general(own, key[...], (((1,), (1,)), ((), ())), preferred_element_type=f32)
            for key in keys
        ]
        top = functools.reduce(jnp.maximum, [jnp.max(s, axis=1, keepdims=True) for s in scores])
        expos = [jnp.exp(s - top) for s in scores]
        total = sum(jnp.sum(e, axis=1, keepdims=True) for e in expos)
        weighted = sum(
            jnp.dot(e.astype(bf16), key[...], preferred_element_type=f32)
            for e, key in zip(expos, keys)
        )
        mean = weighted / total
        log_sum = top + jnp.log(total)
        if at < kept_rows:
            kept[at : at + chunk] = mean
            kept_log[at : at + chunk] = jnp.broadcast_to(log_sum, (chunk, stat_lanes))
        else:
            to = at - kept_rows
            values, stats = pack(mean, log_sum)
            sent[to : to + chunk, 0:channels] = values
            sent[to : to + chunk, channels : channels + stat_lanes] = stats


def unpack(ref, rows):
    channels = ref.shape[1] - stat_lanes
    values = ref[rows, 0:channels].astype(f32)
    log_sum = jnp.sum(ref[rows, channels : channels + stat_lanes].astype(f32), axis=1, keepdims=True)
    return values, log_sum


def merge(parts):
    top = functools.reduce(jnp.maximum, [log_sum for _, log_sum in parts])
    scales = [jnp.exp(log_sum - top) for _, log_sum in parts]
    total = sum(scales)
    mean = sum(values * scale for (values, _), scale in zip(parts, scales)) / total
    return mean, top + jnp.log(total)


def chip_kernel(tile, kept, kept_log, received, own, own_log, *sent):
    for block in range(1 + len(sent)):
        rows = pl.ds(block * tile, tile)
        mean, log_sum = merge(
            [(kept[rows, :], kept_log[rows, 0:1]), unpack(received, rows)]
        )
        if block == 0:
            own[...] = mean
            own_log[...] = jnp.broadcast_to(log_sum, (tile, stat_lanes))
        else:
            channels = mean.shape[1]
            values, stats = pack(mean, log_sum)
            sent[block - 1][:, 0:channels] = values
            sent[block - 1][:, channels : channels + stat_lanes] = stats


def final_kernel(tile, others, *refs):
    own, own_log = refs[:2]
    received = refs[2 : 2 + others]
    mixed, value_weight, value_bias, out_weight, out_bias, decoded = refs[2 + others :]
    parts = [(own[...], own_log[:, 0:1])] + [unpack(ref, pl.ds(0, tile)) for ref in received]
    mean, _ = merge(parts)
    attended = (
        jnp.dot(mean.astype(bf16), value_weight[...], preferred_element_type=f32) + value_bias[...]
    ).astype(bf16)
    projected = jnp.dot(attended, out_weight[...], preferred_element_type=f32) + out_bias[...]
    decoded[...] = (mixed[...].astype(f32) + projected).astype(bf16)


def shape(dims, dtype):
    return jax.ShapeDtypeStruct(dims, dtype)


def per_device(
    hidden,
    frame_cache,
    shortcut,
    gain_one,
    conv_weight,
    conv_bias,
    gain_two,
    query_weight,
    query_bias,
    key_weight,
    value_weight,
    value_bias,
    out_weight,
    out_bias,
):
    _, tile_rows, tile_cols, channels = hidden.shape
    tile = tile_rows * tile_cols
    row_count, col_count = lax.axis_size("rows"), lax.axis_size("cols")
    chip_count = col_count // 2
    row_even = lax.axis_index("rows") % 2 == 0
    col_even = lax.axis_index("cols") % 2 == 0
    parity = jnp.stack([lax.axis_index("rows") % 2, lax.axis_index("cols") % 2]).astype(jnp.int32)
    row_vector = lambda v: v.reshape(1, channels)

    frames = jnp.concatenate([frame_cache[0], hidden], axis=0)
    top, bottom = frames[:, 0], frames[:, tile_rows - 1]
    row_a = lax.ppermute(jnp.where(row_even, bottom, top), "rows", near_pairs(row_count, 0))
    row_b = lax.ppermute(jnp.where(row_even, top, bottom), "rows", near_pairs(row_count, 1))
    above = jnp.where(row_even, row_b, row_a)
    below = jnp.where(row_even, row_a, row_b)
    edges = []
    for at in (0, tile_cols - 1):
        edges.append(
            jnp.concatenate(
                [above[:, at][:, None], frames[:, :, at], below[:, at][:, None]], axis=1
            ).reshape(3 * (tile_rows + 2), channels)
        )
    col_a = lax.ppermute(jnp.where(col_even, edges[1], edges[0]), "cols", near_pairs(col_count, 0))
    col_b = lax.ppermute(jnp.where(col_even, edges[0], edges[1]), "cols", near_pairs(col_count, 1))

    normed, mixed = pl.pallas_call(
        functools.partial(conv_kernel, tile_rows, tile_cols, channels),
        out_shape=(shape((tile, channels), bf16), shape((tile, channels), bf16)),
        in_specs=[SMEM] + [VMEM] * 10 + [ANY],
        out_specs=(VMEM, VMEM),
        scratch_shapes=[
            pltpu.VMEM((9, 3 * channels, channels), bf16),
            pltpu.VMEM((3, (tile_rows + 2) * tile_cols, 3 * channels), bf16),
            pltpu.SemaphoreType.DMA((9,)),
        ],
        name="conv",
    )(
        parity,
        frame_cache,
        hidden,
        shortcut.reshape(tile, channels),
        row_a,
        row_b,
        col_a,
        col_b,
        row_vector(gain_one),
        row_vector(conv_bias),
        row_vector(gain_two),
        conv_weight.reshape(9, 3 * channels, channels),
    )

    key_blocks = [normed] + [
        lax.ppermute(normed, "rows", far_pairs(row_count, step))
        for step in range(row_count - 1, 0, -1)
    ]
    query_blocks = jnp.concatenate(
        [normed]
        + [
            lax.ppermute(normed, "cols", far_pairs(chip_count, step, 2))
            for step in range(1, chip_count)
        ],
        axis=0,
    )
    other_queries = lax.ppermute(query_blocks, "cols", near_pairs(col_count, 0))
    query_rows = 2 * chip_count * tile
    queries = pl.pallas_call(
        lambda *refs: query_kernel(float(channels) ** (-0.5), 2, refs),
        out_shape=shape((query_rows, channels), bf16),
        in_specs=[VMEM] * 5,
        out_specs=VMEM,
        name="queries",
    )(query_blocks, other_queries, query_weight, row_vector(query_bias), key_weight)

    kept_rows = chip_count * tile
    kept, kept_log, sent = pl.pallas_call(
        functools.partial(attend_kernel, row_count, kept_rows, tile),
        out_shape=(
            shape((kept_rows, channels), f32),
            shape((kept_rows, stat_lanes), f32),
            shape((kept_rows, channels + stat_lanes), bf16),
        ),
        in_specs=[VMEM] * (1 + row_count),
        out_specs=(VMEM, VMEM, VMEM),
        name="attend",
    )(queries, *key_blocks)
    received = lax.ppermute(sent, "cols", near_pairs(col_count, 0))

    packed = shape((tile, channels + stat_lanes), bf16)
    own, own_log, *results = pl.pallas_call(
        functools.partial(chip_kernel, tile),
        out_shape=(shape((tile, channels), f32), shape((tile, stat_lanes), f32))
        + (packed,) * (chip_count - 1),
        in_specs=[VMEM] * 3,
        out_specs=(VMEM,) * (chip_count + 1),
        name="chip",
    )(kept, kept_log, received)
    returned = [
        lax.ppermute(
            result, "cols", [(j, i) for i, j in far_pairs(chip_count, step, 2)]
        )
        for step, result in enumerate(results, 1)
    ]
    decoded = pl.pallas_call(
        functools.partial(final_kernel, tile, chip_count - 1),
        out_shape=shape((tile, channels), bf16),
        in_specs=[VMEM] * (2 + chip_count - 1 + 5),
        out_specs=VMEM,
        name="final",
    )(
        own,
        own_log,
        *returned,
        mixed,
        value_weight,
        row_vector(value_bias),
        out_weight,
        row_vector(out_bias),
    )
    return decoded.reshape(1, tile_rows, tile_cols, channels)


def solution(mesh):
    placed = (
        P("videos", "rows", "cols", None),
        P("videos", None, "rows", "cols", None),
        P("videos", "rows", "cols", None),
        P(),
        P(),
        P(),
        P(),
        P(),
        P(),
        P(),
        P(),
        P(),
        P(),
        P(),
    )
    return jax.shard_map(
        per_device,
        mesh=mesh,
        in_specs=placed,
        out_specs=P("videos", "rows", "cols", None),
        check_vma=False,
    )
```

time: 91.8 us -> 59.6 us (0.65)
  waiting for transfers between devices: 48.6 us -> 10.5 us
  Pallas kernels: 0 us -> 17.3 us
  between operations: 13.7 us -> 0.17 us
  matrix products: 12.9 us -> 0 us
  local copies, waits for them, and re-layouts: 1.27 us -> 11.4 us
  starting transfers between devices: 8.84 us -> 17.4 us
  other arithmetic: 6.13 us -> 2.35 us
    all_gather x1 -> x0, waiting for transfers between devices: 40.1 us -> none  [per_device(): piece = lax.all_gather(normed, ('rows', 'cols'), axis=0, tiled=True)]
    pallas_call x0 -> x5, Pallas kernels: none -> 17.3 us  [the longest x1 5.88 us: per_device(): pl.pallas_call(functools.partial(conv_kernel, tile_rows, tile_cols, chann...]
    ppermute x4 -> x11, starting transfers between devices: 8.84 us -> 17.4 us  [the longest x3 7.05 us: per_device(): lax.ppermute(normed, 'rows', far_pairs(row_count, step))]
    dot_general x4 -> x0, matrix products: 7.65 us -> none  [the longest x1 3.13 us: per_device(): jnp.einsum('qc,kc->qk', queries, key_rows, preferred_element_type=jnp.flo...]
    reshape x0 -> x6, local copies, waits for them, and re-layouts: none -> 5.49 us  [per_device(): row_vector = lambda v: v.reshape(1, channels)]
    conv_general_dilated x1 -> x0, matrix products: 5.21 us -> none  [per_device(): lax.conv_general_dilated(rimmed[None], conv_weight, (1, 1, 1), 'VALID', d...]
    unnamed x24 -> x30, local copies, waits for them, and re-layouts: 0.86 us -> 5.8 us
    ppermute x4 -> x11, waiting for transfers between devices: 8.46 us -> 10.5 us  [the longest x1 3.1 us: per_device(): lax.ppermute(result, 'cols', [(j, i) for i, j in far_pairs(chip_count, st...]
  transfers between devices with their start and end apart: 5 -> 11, of which waited for: 4 -> 5; matrix products, arithmetic and copies ran while one was open for 1% -> 13% of each run, Pallas kernels for 0% -> 5%
where the time goes in v1:
time: 59.6 us; the launch traced here: 59.1 us
  starting transfers between devices  17.4 us (29%)
  Pallas kernels  17.3 us (29%)
  local copies, waits for them, and re-layouts  11.4 us (19%)
  waiting for transfers between devices  10.5 us (18%)
  other arithmetic  2.35 us (4%)
    ppermute x3, starting transfers between devices, per_device(): lax.ppermute(normed, 'rows', far_pairs(row_count, step))  7.05 us
    pallas_call x1, Pallas kernels, per_device(): pl.pallas_call(functools.partial(conv_kernel, tile_rows, tile_cols, chann...  5.88 us
    unnamed x30, local copies, waits for them, and re-layouts  5.8 us
    reshape x6, local copies, waits for them, and re-layouts, per_device(): row_vector = lambda v: v.reshape(1, channels)  5.49 us
    pallas_call x1, Pallas kernels, per_device(): pl.pallas_call(functools.partial(attend_kernel, row_count, kept_rows, til...  3.96 us
    ppermute x1, starting transfers between devices, per_device(): lax.ppermute(normed, 'cols', far_pairs(chip_count, step, 2))  3.43 us
    ppermute x1, starting transfers between devices, per_device(): lax.ppermute(jnp.where(row_even, bottom, top), 'rows', near_pairs(row_cou...  3.12 us
    ppermute x1, waiting for transfers between devices, per_device(): lax.ppermute(result, 'cols', [(j, i) for i, j in far_pairs(chip_count, st...  3.1 us
  transfers between devices with their start and end apart: 11, of which 5 were waited for; matrix products, arithmetic and copies ran while one was open for 13% of the time, Pallas kernels for 5%

profile of v1, /device:TPU:0, one launch (start us, length us, event | category | flops | bytes accessed | tf_op | source)
XLA Modules:
  0.0 59.1 jit_solution(14642707983863704109)
XLA Ops:
  0.0 0.0 copy-start.11
  0.0 0.0 copy-start.12
  0.0 0.0 copy-start.13
  0.0 1.0 %copy.41 = bf16[1,2,4,32,384]{4,3,1,2,0:T(8,128)(2,1)S(1)} copy(bf16[1,2,4,32,384]{4,3,2,1,0:T(8,128)(2,1)} %cache.1) | data formatting | bytes 393216 | tf_op args[1]
  1.0 0.8 %select_bitcast_fusion = (bf16[3,32,384]{2,1,0:T(8,128)(2,1)S(1)}, bf16[3,32,384]{2,1,0:T(8,128)(2,1)S(1)}) fusion(pred[]{:T(512)S(6)} %eq.11, bf16[1,4,32,384]{3,2,0,1:T(8,128)(2,1)} %bitcast.20, bf16[2,4,32,384]{3,2,0,1:T(8,128)(2,1)S(1)} %bitcast.18), kind=kLoop, calls=%fused_computation.9 | loop fusion | flops 221184 | bytes 442369 | tf_op jit(solution)/shard_map/jit(_where)/select_n | solution.py:256
  1.8 3.1 %collective-permute-start = (bf16[3,32,384]{2,1,0:T(8,128)(2,1)S(1)}, bf16[3,32,384]{2,1,0:T(8,128)(2,1)S(1)}, u32[]{:S(2)}, u32[]{:S(2)}) collective-permute-start(bf16[3,32,384]{2,1,0:T(8,128)(2,1)S(1)} %get-tuple-element.24), channel_id=1, source_target_pairs={{0,4},{4,0},{8,12},{12,8},{1,5},{5,1},{9,13},{13,9},{2,6},{6,2},{1... | collective-permute-start | bytes 221192 | tf_op jit(solution)/shard_map/ppermute | solution.py:255
  5.0 0.7 %collective-permute-start.1 = (bf16[3,32,384]{2,1,0:T(8,128)(2,1)S(1)}, bf16[3,32,384]{2,1,0:T(8,128)(2,1)S(1)}, u32[]{:S(2)}, u32[]{:S(2)}) collective-permute-start(bf16[3,32,384]{2,1,0:T(8,128)(2,1)S(1)} %get-tuple-element.23), channel_id=1, source_target_pairs={{4,8},{8,4},{5,9},{9,5},{6,10},{10,6},{7,11},{11,7},{20,24},{24,20... | collective-permute-start | bytes 221192 | tf_op jit(solution)/shard_map/ppermute | solution.py:256
  5.6 0.8 %fusion.2 = (bf16[3,4,1,384]{3,2,0,1:T(2,128)(2,1)S(1)}, bf16[3,4,1,384]{3,2,0,1:T(2,128)(2,1)S(1)}) fusion(bf16[2,4,32,384]{3,2,0,1:T(8,128)(2,1)S(1)} %bitcast.19, bf16[1,4,32,384]{3,2,0,1:T(8,128)(2,1)} %bitcast.21), kind=kLoop, calls=%fused_computation.13 | loop fusion | flops 36864 | bytes 313344 | tf_op jit(solution)/shard_map/concatenate | solution.py:253
  6.5 0.8 %collective-permute-done.row_a = bf16[3,32,384]{2,1,0:T(8,128)(2,1)S(1)} collective-permute-done((bf16[3,32,384]{2,1,0:T(8,128)(2,1)S(1)}, bf16[3,32,384]{2,1,0:T(8,128)(2,1)S(1)}, u32[]{:S(2)}, u32[]{:S(2)}) %collective-permute-start) | collective-permute-done | bytes 73760 | tf_op jit(solution)/shard_map/ppermute | solution.py:255
  7.3 0.0 copy-start.1
  7.3 0.0 collective-permute-done.1.row_b
  7.3 0.0 copy-start.2
  7.4 0.1 collective-permute-start.2
  7.5 0.7 %collective-permute-start.3 = (bf16[18,384]{1,0:T(8,128)(2,1)S(1)}, bf16[18,384]{1,0:T(8,128)(2,1)S(1)}, u32[]{:S(2)}, u32[]{:S(2)}) collective-permute-start(bf16[18,384]{1,0:T(8,128)(2,1)S(1)} %select_n.75), channel_id=1, source_target_pairs={{1,2},{2,1},{5,6},{6,5},{9,10},{10,9},{13,14},{14,13},{17,18},{18,... | collective-permute-start | bytes 41480 | tf_op jit(solution)/shard_map/ppermute | solution.py:267
  8.2 0.7 %pad_add_fusion.parity = s32[2]{0:T(128)} fusion(s32[1]{0:T(128)} %bitcast.1, s32[1]{0:T(128)} %bitcast), kind=kLoop, calls=%fused_computation.23 | loop fusion | flops 2 | bytes 16 | tf_op jit(solution)/shard_map/stack | solution.py:250
  8.8 1.3 %reshape.38.gain_one = f32[1,384]{1,0:T(1,128)} reshape(f32[384]{0:T(512)} %param.17) | data formatting | bytes 3072 | tf_op jit(solution)/shard_map/reshape | solution.py:251
  10.1 1.3 %reshape.39.conv_bias = f32[1,384]{1,0:T(1,128)} reshape(f32[384]{0:T(512)} %param.19) | data formatting | bytes 3072 | tf_op jit(solution)/shard_map/reshape | solution.py:251
  11.4 1.2 %reshape.40.gain_two = f32[1,384]{1,0:T(1,128)} reshape(f32[384]{0:T(512)} %param.20) | data formatting | bytes 3072 | tf_op jit(solution)/shard_map/reshape | solution.py:251
  12.6 0.0 collective-permute-done.2.col_a
  12.6 0.0 copy-start.9
  12.6 0.0 collective-permute-done.3.col_b
  12.6 0.0 copy-start.10
  12.6 0.0 copy-done.1
  12.6 0.0 copy-done.2
  12.7 0.6 copy-done.9
  13.2 0.0 copy-done.10
  13.2 5.9 %conv.1 = (bf16[128,384]{1,0:T(8,128)(2,1)}, bf16[128,384]{1,0:T(8,128)(2,1)}) custom-call(s32[2]{0:T(128)} %pad_add_fusion.parity, bf16[1,2,4,32,384]{4,3,2,1,0:T(8,128)(2,1)} %cache.1, bf16[1,4,32,384]{3,2,1,0:T(8,128)(2,1)} %hidden.1, bf16[128,384]{1,0:T(8,128)(2,1)} %bitcast.22, bf16[3,32,384]{2,1,0:T(8,128)(2,1)} %copy-done.1, ...), custom_call_target="tpu_custom_call" | custom-call | tf_op jit(solution)/shard_map/conv/pallas_call | solution.py:269
  19.1 3.4 %collective-permute-start.4 = (bf16[128,384]{1,0:T(8,128)(2,1)}, bf16[128,384]{1,0:T(8,128)(2,1)S(1)}, u32[]{:S(2)}, u32[]{:S(2)}) collective-permute-start(bf16[128,384]{1,0:T(8,128)(2,1)} %get-tuple-element.13.refs_1_), channel_id=1, source_target_pairs={{0,2},{1,3},{2,0},{3,1},{4,6},{5,7},{6,4},{7,5},{8,10},{9,11},{10,... | collective-permute-start | bytes 294920 | tf_op jit(solution)/shard_map/ppermute | solution.py:302
  22.5 0.9 %constant_dynamic-update-slice_fusion.1 = bf16[256,384]{1,0:T(8,128)(2,1)S(1)} fusion(bf16[128,384]{1,0:T(8,128)(2,1)} %get-tuple-element.13.refs_1_), kind=kLoop, calls=%fused_computation.22 | loop fusion | bytes 196608
  23.5 1.9 %collective-permute-done.4 = bf16[128,384]{1,0:T(8,128)(2,1)S(1)} collective-permute-done((bf16[128,384]{1,0:T(8,128)(2,1)}, bf16[128,384]{1,0:T(8,128)(2,1)S(1)}, u32[]{:S(2)}, u32[]{:S(2)}) %collective-permute-start.4) | collective-permute-done | bytes 98336 | tf_op jit(solution)/shard_map/ppermute | solution.py:302
  25.4 0.0 copy-start
  25.5 0.9 %collective-permute-start.5 = (bf16[256,384]{1,0:T(8,128)(2,1)S(1)}, bf16[256,384]{1,0:T(8,128)(2,1)S(1)}, u32[]{:S(2)}, u32[]{:S(2)}) collective-permute-start(bf16[256,384]{1,0:T(8,128)(2,1)S(1)} %constant_dynamic-update-slice_fusion.refs_0_), channel_id=1, source_target_pairs={{0,1},{1,0},{2,3},{3,2},{4,5},{5,4},{6,7},{7,6},{8,9},{9,8},{10,11... | collective-permute-start | bytes 589832 | tf_op jit(solution)/shard_map/ppermute | solution.py:307
  26.3 4.0 %collective-permute-start.6 = (bf16[128,384]{1,0:T(8,128)(2,1)}, bf16[128,384]{1,0:T(8,128)(2,1)S(1)}, u32[]{:S(2)}, u32[]{:S(2)}) collective-permute-start(bf16[128,384]{1,0:T(8,128)(2,1)} %get-tuple-element.13.refs_1_), channel_id=1, source_target_pairs={{0,12},{4,8},{8,4},{12,0},{1,13},{5,9},{9,5},{13,1},{2,14},{6,10},... | collective-permute-start | bytes 294920 | tf_op jit(solution)/shard_map/ppermute | solution.py:296
  30.4 2.5 %collective-permute-start.7 = (bf16[128,384]{1,0:T(8,128)(2,1)}, bf16[128,384]{1,0:T(8,128)(2,1)S(1)}, u32[]{:S(2)}, u32[]{:S(2)}) collective-permute-start(bf16[128,384]{1,0:T(8,128)(2,1)} %get-tuple-element.13.refs_1_), channel_id=1, source_target_pairs={{0,8},{4,12},{8,0},{12,4},{1,9},{5,13},{9,1},{13,5},{2,10},{6,14},... | collective-permute-start | bytes 294920 | tf_op jit(solution)/shard_map/ppermute | solution.py:296
  32.8 0.6 collective-permute-start.8
  33.4 0.0 copy-done.11
  33.4 0.6 reshape.42.refs_3_
  34.0 0.0 collective-permute-done.5.refs_1_
  34.0 0.0 copy-done
  34.0 0.0 copy-start.4
  34.0 0.7 %copy-done.4 = bf16[256,384]{1,0:T(8,128)(2,1)} copy-done((bf16[256,384]{1,0:T(8,128)(2,1)}, bf16[256,384]{1,0:T(8,128)(2,1)S(1)}, u32[]{:S(2)}) %copy-start.4) | copy-done | bytes 196632
  34.6 2.8 %queries.1.refs_0_ = bf16[512,384]{1,0:T(8,128)(2,1)} custom-call(bf16[256,384]{1,0:T(8,128)(2,1)} %copy-done, bf16[256,384]{1,0:T(8,128)(2,1)} %copy-done.4, bf16[384,384]{1,0:T(8,128)(2,1)} %refs_2_.1, f32[1,384]{1,0:T(1,128)} %reshape.42.refs_3_, bf16[384,384]{1,0:T(8,128)(2,1)} %refs_4_.2), custom_call_target="tpu_custom_call" | custom-call | tf_op jit(solution)/shard_map/queries/pallas_call | solution.py:309
  37.5 0.0 collective-permute-done.6.refs_2_
  37.5 0.0 copy-start.6
  37.5 2.9 %collective-permute-done.7.refs_3_ = bf16[128,384]{1,0:T(8,128)(2,1)S(1)} collective-permute-done((bf16[128,384]{1,0:T(8,128)(2,1)}, bf16[128,384]{1,0:T(8,128)(2,1)S(1)}, u32[]{:S(2)}, u32[]{:S(2)}) %collective-permute-start.7) | collective-permute-done | bytes 98336 | tf_op jit(solution)/shard_map/ppermute | solution.py:296
  40.3 0.0 copy-start.7
  40.3 0.0 collective-permute-done.8.refs_4_
  40.3 0.0 copy-done.6
  40.4 0.6 %copy-done.7 = bf16[128,384]{1,0:T(8,128)(2,1)} copy-done((bf16[128,384]{1,0:T(8,128)(2,1)}, bf16[128,384]{1,0:T(8,128)(2,1)S(1)}, u32[]{:S(2)}) %copy-start.7) | copy-done | bytes 98328
  41.0 0.0 copy-start.8
  41.0 0.6 %copy-done.8 = bf16[128,384]{1,0:T(8,128)(2,1)} copy-done((bf16[128,384]{1,0:T(8,128)(2,1)}, bf16[128,384]{1,0:T(8,128)(2,1)S(1)}, u32[]{:S(2)}) %copy-start.8) | copy-done | bytes 98328
  41.6 4.0 %attend.1 = (f32[256,384]{1,0:T(8,128)}, f32[256,128]{1,0:T(8,128)}, bf16[256,512]{1,0:T(8,128)(2,1)}) custom-call(bf16[512,384]{1,0:T(8,128)(2,1)} %queries.1.refs_0_, bf16[128,384]{1,0:T(8,128)(2,1)} %get-tuple-element.13.refs_1_, bf16[128,384]{1,0:T(8,128)(2,1)} %copy-done.6, bf16[128,384]{1,0:T(8,128)(2,1)} %copy-done.7, bf16[128,384]{1,0:T(8,128)(2,1)} %copy-done.8), custom_call_target="tpu_custom_call" | custom-call | tf_op jit(solution)/shard_map/attend/pallas_call | solution.py:318
  45.6 0.0 collective-permute-start.9
  45.6 1.7 %collective-permute-done.9.received = bf16[256,512]{1,0:T(8,128)(2,1)S(1)} collective-permute-done((bf16[256,512]{1,0:T(8,128)(2,1)}, bf16[256,512]{1,0:T(8,128)(2,1)S(1)}, u32[]{:S(2)}, u32[]{:S(2)}) %collective-permute-start.9) | collective-permute-done | bytes 262176 | tf_op jit(solution)/shard_map/ppermute | solution.py:329
  47.3 0.7 %copy-done.3 = bf16[256,512]{1,0:T(8,128)(2,1)} copy-done((bf16[256,512]{1,0:T(8,128)(2,1)}, bf16[256,512]{1,0:T(8,128)(2,1)S(1)}, u32[]{:S(2)}) %copy-start.3) | copy-done | bytes 262168
  48.0 2.1 %chip.1 = (f32[128,384]{1,0:T(8,128)}, f32[128,128]{1,0:T(8,128)}, bf16[128,512]{1,0:T(8,128)(2,1)}) custom-call(f32[256,384]{1,0:T(8,128)} %get-tuple-element.14.kept, f32[256,128]{1,0:T(8,128)} %get-tuple-element.15.kept_log, bf16[256,512]{1,0:T(8,128)(2,1)} %copy-done.3), custom_call_target="tpu_custom_call" | custom-call | tf_op jit(solution)/shard_map/chip/pallas_call | solution.py:332
  50.2 1.5 %collective-permute-start.10 = (bf16[128,512]{1,0:T(8,128)(2,1)}, bf16[128,512]{1,0:T(8,128)(2,1)S(1)}, u32[]{:S(2)}, u32[]{:S(2)}) collective-permute-start(bf16[128,512]{1,0:T(8,128)(2,1)} %get-tuple-element.19), channel_id=1, source_target_pairs={{2,0},{3,1},{0,2},{1,3},{6,4},{7,5},{4,6},{5,7},{10,8},{11,9},{8,1... | collective-permute-start | bytes 393224 | tf_op jit(solution)/shard_map/ppermute | solution.py:341
  51.7 0.0 copy-done.12
  51.7 0.6 reshape.43.refs_5_
  52.2 0.0 copy-done.13
  52.2 0.6 reshape.44.refs_7_
  52.8 3.1 %collective-permute-done.10.refs_2_ = bf16[128,512]{1,0:T(8,128)(2,1)S(1)} collective-permute-done((bf16[128,512]{1,0:T(8,128)(2,1)}, bf16[128,512]{1,0:T(8,128)(2,1)S(1)}, u32[]{:S(2)}, u32[]{:S(2)}) %collective-permute-start.10) | collective-permute-done | bytes 131104 | tf_op jit(solution)/shard_map/ppermute | solution.py:341
  55.9 0.6 %copy-done.5 = bf16[128,512]{1,0:T(8,128)(2,1)} copy-done((bf16[128,512]{1,0:T(8,128)(2,1)}, bf16[128,512]{1,0:T(8,128)(2,1)S(1)}, u32[]{:S(2)}) %copy-start.5) | copy-done | bytes 131096
  56.6 2.5 %final.1 = bf16[128,384]{1,0:T(8,128)(2,1)} custom-call(f32[128,384]{1,0:T(8,128)} %get-tuple-element.17.refs_0_, f32[128,128]{1,0:T(8,128)} %get-tuple-element.18.refs_1_, bf16[128,512]{1,0:T(8,128)(2,1)} %copy-done.5, bf16[128,384]{1,0:T(8,128)(2,1)} %get-tuple-element.20.refs_3_, bf16[384,384]{1,0:T(8,128)(2,1)} %refs_4_.3, f32[1,384]{1,0:T(1,128)} %reshape.43.refs_5_, ...), custom_call_target="tpu_custom_call" | custom-call | tf_op jit(solution)/shard_map/final/pallas_call | solution.py:346
  (9 shorter events, 0.1 us)
Async XLA Ops:
  0.0 33.4 %copy-start.11 = (f32[384]{0:T(512)S(1)}, f32[384]{0:T(512)}, u32[]{:S(2)}) copy-start(f32[384]{0:T(512)} %param.22) | copy-start | bytes 4612
  0.0 51.7 %copy-start.12 = (f32[384]{0:T(512)S(1)}, f32[384]{0:T(512)}, u32[]{:S(2)}) copy-start(f32[384]{0:T(512)} %param.25) | copy-start | bytes 4612
  0.0 52.2 %copy-start.13 = (f32[384]{0:T(512)S(1)}, f32[384]{0:T(512)}, u32[]{:S(2)}) copy-start(f32[384]{0:T(512)} %param.27) | copy-start | bytes 4612
  1.8 5.5 %collective-permute-start = (bf16[3,32,384]{2,1,0:T(8,128)(2,1)S(1)}, bf16[3,32,384]{2,1,0:T(8,128)(2,1)S(1)}, u32[]{:S(2)}, u32[]{:S(2)}) collective-permute-start(bf16[3,32,384]{2,1,0:T(8,128)(2,1)S(1)} %get-tuple-element.24), channel_id=1, source_target_pairs={{0,4},{4,0},{8,12},{12,8},{1,5},{5,1},{9,13},{13,9},{2,6},{6,2},{1... | collective-permute-start | bytes 221192 | tf_op jit(solution)/shard_map/ppermute | solution.py:255
  5.0 2.3 %collective-permute-start.1 = (bf16[3,32,384]{2,1,0:T(8,128)(2,1)S(1)}, bf16[3,32,384]{2,1,0:T(8,128)(2,1)S(1)}, u32[]{:S(2)}, u32[]{:S(2)}) collective-permute-start(bf16[3,32,384]{2,1,0:T(8,128)(2,1)S(1)} %get-tuple-element.23), channel_id=1, source_target_pairs={{4,8},{8,4},{5,9},{9,5},{6,10},{10,6},{7,11},{11,7},{20,24},{24,20... | collective-permute-start | bytes 221192 | tf_op jit(solution)/shard_map/ppermute | solution.py:256
  7.3 5.3 %copy-start.1 = (bf16[3,32,384]{2,1,0:T(8,128)(2,1)}, bf16[3,32,384]{2,1,0:T(8,128)(2,1)S(1)}, u32[]{:S(2)}) copy-start(bf16[3,32,384]{2,1,0:T(8,128)(2,1)S(1)} %collective-permute-done.row_a) | copy-start | bytes 221188
  7.3 5.3 %copy-start.2 = (bf16[3,32,384]{2,1,0:T(8,128)(2,1)}, bf16[3,32,384]{2,1,0:T(8,128)(2,1)S(1)}, u32[]{:S(2)}) copy-start(bf16[3,32,384]{2,1,0:T(8,128)(2,1)S(1)} %collective-permute-done.1.row_b) | copy-start | bytes 221188
  7.4 5.2 %collective-permute-start.2 = (bf16[18,384]{1,0:T(8,128)(2,1)S(1)}, bf16[18,384]{1,0:T(8,128)(2,1)S(1)}, u32[]{:S(2)}, u32[]{:S(2)}) collective-permute-start(bf16[18,384]{1,0:T(8,128)(2,1)S(1)} %select_n.73), channel_id=1, source_target_pairs={{0,1},{1,0},{2,3},{3,2},{4,5},{5,4},{6,7},{7,6},{8,9},{9,8},{10,11... | collective-permute-start | bytes 41480 | tf_op jit(solution)/shard_map/ppermute | solution.py:266
  7.5 5.1 %collective-permute-start.3 = (bf16[18,384]{1,0:T(8,128)(2,1)S(1)}, bf16[18,384]{1,0:T(8,128)(2,1)S(1)}, u32[]{:S(2)}, u32[]{:S(2)}) collective-permute-start(bf16[18,384]{1,0:T(8,128)(2,1)S(1)} %select_n.75), channel_id=1, source_target_pairs={{1,2},{2,1},{5,6},{6,5},{9,10},{10,9},{13,14},{14,13},{17,18},{18,... | collective-permute-start | bytes 41480 | tf_op jit(solution)/shard_map/ppermute | solution.py:267
  12.6 0.6 %copy-start.9 = (bf16[18,384]{1,0:T(8,128)(2,1)}, bf16[18,384]{1,0:T(8,128)(2,1)S(1)}, u32[]{:S(2)}) copy-start(bf16[18,384]{1,0:T(8,128)(2,1)S(1)} %collective-permute-done.2.col_a) | copy-start | bytes 41476
  12.6 0.6 %copy-start.10 = (bf16[18,384]{1,0:T(8,128)(2,1)}, bf16[18,384]{1,0:T(8,128)(2,1)S(1)}, u32[]{:S(2)}) copy-start(bf16[18,384]{1,0:T(8,128)(2,1)S(1)} %collective-permute-done.3.col_b) | copy-start | bytes 41476
  19.1 6.3 %collective-permute-start.4 = (bf16[128,384]{1,0:T(8,128)(2,1)}, bf16[128,384]{1,0:T(8,128)(2,1)S(1)}, u32[]{:S(2)}, u32[]{:S(2)}) collective-permute-start(bf16[128,384]{1,0:T(8,128)(2,1)} %get-tuple-element.13.refs_1_), channel_id=1, source_target_pairs={{0,2},{1,3},{2,0},{3,1},{4,6},{5,7},{6,4},{7,5},{8,10},{9,11},{10,... | collective-permute-start | bytes 294920 | tf_op jit(solution)/shard_map/ppermute | solution.py:302
  25.4 8.5 %copy-start = (bf16[256,384]{1,0:T(8,128)(2,1)}, bf16[256,384]{1,0:T(8,128)(2,1)S(1)}, u32[]{:S(2)}) copy-start(bf16[256,384]{1,0:T(8,128)(2,1)S(1)} %constant_dynamic-update-slice_fusion.refs_0_) | copy-start | bytes 589828
  25.5 8.5 %collective-permute-start.5 = (bf16[256,384]{1,0:T(8,128)(2,1)S(1)}, bf16[256,384]{1,0:T(8,128)(2,1)S(1)}, u32[]{:S(2)}, u32[]{:S(2)}) collective-permute-start(bf16[256,384]{1,0:T(8,128)(2,1)S(1)} %constant_dynamic-update-slice_fusion.refs_0_), channel_id=1, source_target_pairs={{0,1},{1,0},{2,3},{3,2},{4,5},{5,4},{6,7},{7,6},{8,9},{9,8},{10,11... | collective-permute-start | bytes 589832 | tf_op jit(solution)/shard_map/ppermute | solution.py:307
  26.3 11.2 %collective-permute-start.6 = (bf16[128,384]{1,0:T(8,128)(2,1)}, bf16[128,384]{1,0:T(8,128)(2,1)S(1)}, u32[]{:S(2)}, u32[]{:S(2)}) collective-permute-start(bf16[128,384]{1,0:T(8,128)(2,1)} %get-tuple-element.13.refs_1_), channel_id=1, source_target_pairs={{0,12},{4,8},{8,4},{12,0},{1,13},{5,9},{9,5},{13,1},{2,14},{6,10},... | collective-permute-start | bytes 294920 | tf_op jit(solution)/shard_map/ppermute | solution.py:296
  30.4 10.0 %collective-permute-start.7 = (bf16[128,384]{1,0:T(8,128)(2,1)}, bf16[128,384]{1,0:T(8,128)(2,1)S(1)}, u32[]{:S(2)}, u32[]{:S(2)}) collective-permute-start(bf16[128,384]{1,0:T(8,128)(2,1)} %get-tuple-element.13.refs_1_), channel_id=1, source_target_pairs={{0,8},{4,12},{8,0},{12,4},{1,9},{5,13},{9,1},{13,5},{2,10},{6,14},... | collective-permute-start | bytes 294920 | tf_op jit(solution)/shard_map/ppermute | solution.py:296
  32.8 7.5 %collective-permute-start.8 = (bf16[128,384]{1,0:T(8,128)(2,1)}, bf16[128,384]{1,0:T(8,128)(2,1)S(1)}, u32[]{:S(2)}, u32[]{:S(2)}) collective-permute-start(bf16[128,384]{1,0:T(8,128)(2,1)} %get-tuple-element.13.refs_1_), channel_id=1, source_target_pairs={{0,4},{4,0},{8,12},{12,8},{1,5},{5,1},{9,13},{13,9},{2,6},{6,2},{1... | collective-permute-start | bytes 294920 | tf_op jit(solution)/shard_map/ppermute | solution.py:296
  34.0 0.7 %copy-start.4 = (bf16[256,384]{1,0:T(8,128)(2,1)}, bf16[256,384]{1,0:T(8,128)(2,1)S(1)}, u32[]{:S(2)}) copy-start(bf16[256,384]{1,0:T(8,128)(2,1)S(1)} %collective-permute-done.5.refs_1_) | copy-start | bytes 589828
  37.5 2.9 %copy-start.6 = (bf16[128,384]{1,0:T(8,128)(2,1)}, bf16[128,384]{1,0:T(8,128)(2,1)S(1)}, u32[]{:S(2)}) copy-start(bf16[128,384]{1,0:T(8,128)(2,1)S(1)} %collective-permute-done.6.refs_2_) | copy-start | bytes 294916
  40.3 0.6 %copy-start.7 = (bf16[128,384]{1,0:T(8,128)(2,1)}, bf16[128,384]{1,0:T(8,128)(2,1)S(1)}, u32[]{:S(2)}) copy-start(bf16[128,384]{1,0:T(8,128)(2,1)S(1)} %collective-permute-done.7.refs_3_) | copy-start | bytes 294916
  41.0 0.6 %copy-start.8 = (bf16[128,384]{1,0:T(8,128)(2,1)}, bf16[128,384]{1,0:T(8,128)(2,1)S(1)}, u32[]{:S(2)}) copy-start(bf16[128,384]{1,0:T(8,128)(2,1)S(1)} %collective-permute-done.8.refs_4_) | copy-start | bytes 294916
  45.6 1.7 %collective-permute-start.9 = (bf16[256,512]{1,0:T(8,128)(2,1)}, bf16[256,512]{1,0:T(8,128)(2,1)S(1)}, u32[]{:S(2)}, u32[]{:S(2)}) collective-permute-start(bf16[256,512]{1,0:T(8,128)(2,1)} %get-tuple-element.16), channel_id=1, source_target_pairs={{0,1},{1,0},{2,3},{3,2},{4,5},{5,4},{6,7},{7,6},{8,9},{9,8},{10,11... | collective-permute-start | bytes 786440 | tf_op jit(solution)/shard_map/ppermute | solution.py:329
  47.3 0.7 %copy-start.3 = (bf16[256,512]{1,0:T(8,128)(2,1)}, bf16[256,512]{1,0:T(8,128)(2,1)S(1)}, u32[]{:S(2)}) copy-start(bf16[256,512]{1,0:T(8,128)(2,1)S(1)} %collective-permute-done.9.received) | copy-start | bytes 786436
  50.2 5.7 %collective-permute-start.10 = (bf16[128,512]{1,0:T(8,128)(2,1)}, bf16[128,512]{1,0:T(8,128)(2,1)S(1)}, u32[]{:S(2)}, u32[]{:S(2)}) collective-permute-start(bf16[128,512]{1,0:T(8,128)(2,1)} %get-tuple-element.19), channel_id=1, source_target_pairs={{2,0},{3,1},{0,2},{1,3},{6,4},{7,5},{4,6},{5,7},{10,8},{11,9},{8,1... | collective-permute-start | bytes 393224 | tf_op jit(solution)/shard_map/ppermute | solution.py:341
  55.9 0.7 %copy-start.5 = (bf16[128,512]{1,0:T(8,128)(2,1)}, bf16[128,512]{1,0:T(8,128)(2,1)S(1)}, u32[]{:S(2)}) copy-start(bf16[128,512]{1,0:T(8,128)(2,1)S(1)} %collective-permute-done.10.refs_2_) | copy-start | bytes 393220

commit v2 on v1

--- a/solution.py
+++ b/solution.py
@@ -7,11 +7,14 @@
 from jax.experimental.pallas import tpu as pltpu
 from jax.sharding import PartitionSpec as P
 
+
 norm_epsilon = 1e-06
 stat_lanes = 128
 f32 = jnp.float32
 bf16 = jnp.bfloat16
 
+small_grant = 24 * 1024 * 1024
+stage_cost = pl.CostEstimate(flops=10**10, bytes_accessed=10**7, transcendentals=0)
 VMEM = pl.BlockSpec(memory_space=pltpu.VMEM)
 SMEM = pl.BlockSpec(memory_space=pltpu.SMEM)
 ANY = pl.BlockSpec(memory_space=pl.ANY)
@@ -38,16 +41,52 @@
     return cells * lax.rsqrt(mean_square + norm_epsilon) * gain
 
 
+def line(ref):
+    return ref[...].reshape(1, ref.shape[0])
+
+
 def activate(cells, gain):
     scaled = normalize(cells, gain)
     return scaled * (1.0 / (1.0 + jnp.exp(-scaled)))
+
+
+def rows_kernel(tile_rows, cache, hidden, row_a, row_b, sems):
+    odd = lax.rem(lax.axis_index("rows"), 2)
+    copies = []
+    for out, at in ((row_a, (1 - odd) * (tile_rows - 1)), (row_b, odd * (tile_rows - 1))):
+        for f in range(3):
+            source = cache.at[0, f, at] if f < 2 else hidden.at[0, at]
+            copies.append(pltpu.make_async_copy(source, out.at[f], sems.at[len(copies)]))
+    for copy in copies:
+        copy.start()
+    for copy in copies:
+        copy.wait()
+
+
+def cols_kernel(tile_rows, tile_cols, cache, hidden, row_a, row_b, col_a, col_b):
+    row_even = lax.rem(lax.axis_index("rows"), 2) == 0
+    col_even = lax.rem(lax.axis_index("cols"), 2) == 0
+    first, last = pl.ds(0, 1), pl.ds(tile_cols - 1, 1)
+    near, far = [], []
+
+    def add(pick):
+        left, right = pick(first).astype(f32), pick(last).astype(f32)
+        near.append(jnp.where(col_even, right, left))
+        far.append(jnp.where(col_even, left, right))
+
+    for f in range(3):
+        add(lambda at: jnp.where(row_even, row_b[f, at].astype(f32), row_a[f, at].astype(f32)))
+        for r in range(tile_rows):
+            add(lambda at: cache[0, f, r, at] if f < 2 else hidden[0, r, at])
+        add(lambda at: jnp.where(row_even, row_a[f, at].astype(f32), row_b[f, at].astype(f32)))
+    col_a[...] = jnp.concatenate(near, axis=0).astype(bf16)
+    col_b[...] = jnp.concatenate(far, axis=0).astype(bf16)
 
 
 def conv_kernel(
     tile_rows,
     tile_cols,
     channels,
-    parity,
     cache,
     hidden,
     shortcut,
@@ -61,24 +100,17 @@
     weight,
     normed,
     mixed,
-    held,
     stack,
-    sems,
 ):
-    copies = [
-        pltpu.make_async_copy(weight.at[i], held.at[i], sems.at[i]) for i in range(9)
-    ]
-    for copy in copies:
-        copy.start()
-    row_even = parity[0] == 0
-    col_even = parity[1] == 0
+    row_even = lax.rem(lax.axis_index("rows"), 2) == 0
+    col_even = lax.rem(lax.axis_index("cols"), 2) == 0
     place = lax.broadcasted_iota(jnp.int32, (tile_cols, channels), 0)
     reach = tile_rows + 2
     first = col_a[...].astype(f32)
     second = col_b[...].astype(f32)
     left_all = jnp.where(col_even, second, first)
     right_all = jnp.where(col_even, first, second)
-    gain = gain_one[...]
+    gain = line(gain_one)
     for f in range(3):
         left_rows = left_all[f * reach : (f + 1) * reach]
         right_rows = right_all[f * reach : (f + 1) * reach]
@@ -106,27 +138,26 @@
     total = jnp.zeros((tile_rows * tile_cols, channels), f32)
     for f in range(3):
         for a in range(3):
-            copies[3 * f + a].wait()
             total += jnp.dot(
                 stack[f, a * tile_cols : (a + tile_rows) * tile_cols, :],
-                held[3 * f + a],
+                weight[f, a].reshape(3 * channels, channels),
                 preferred_element_type=f32,
             )
-    convolved = total + conv_bias[...]
+    convolved = total + line(conv_bias)
     residual = shortcut[...].astype(f32)
     kept = (residual + convolved).astype(bf16)
     mixed[...] = kept
-    normed[...] = normalize(kept.astype(f32), gain_two[...]).astype(bf16)
-
-
-def query_kernel(score_scale, parts, refs_in_out):
-    sources = refs_in_out[:parts]
-    query_weight, query_bias, key_weight, out = refs_in_out[parts:]
+    normed[...] = normalize(kept.astype(f32), line(gain_two)).astype(bf16)
+
+
+def query_kernel(score_scale, parts, *refs):
+    sources = refs[:parts]
+    query_weight, query_bias, key_weight, out = refs[parts:]
     at = 0
     for source in sources:
         rows = source.shape[0]
         queries = (
-            jnp.dot(source[...], query_weight[...], preferred_element_type=f32) + query_bias[...]
+            jnp.dot(source[...], query_weight[...], preferred_element_type=f32) + line(query_bias)
         ).astype(bf16)
         turned = lax.dot_general(
             queries, key_weight[...], (((1,), (1,)), ((), ())), preferred_element_type=f32
@@ -215,14 +246,21 @@
     parts = [(own[...], own_log[:, 0:1])] + [unpack(ref, pl.ds(0, tile)) for ref in received]
     mean, _ = merge(parts)
     attended = (
-        jnp.dot(mean.astype(bf16), value_weight[...], preferred_element_type=f32) + value_bias[...]
+        jnp.dot(mean.astype(bf16), value_weight[...], preferred_element_type=f32) + line(value_bias)
     ).astype(bf16)
-    projected = jnp.dot(attended, out_weight[...], preferred_element_type=f32) + out_bias[...]
+    projected = jnp.dot(attended, out_weight[...], preferred_element_type=f32) + line(out_bias)
     decoded[...] = (mixed[...].astype(f32) + projected).astype(bf16)
 
 
-def shape(dims, dtype):
-    return jax.ShapeDtypeStruct(dims, dtype)
+def call(kernel, out_shape, *operands, scratch_shapes=()):
+    return pl.pallas_call(
+        kernel,
+        out_shape=out_shape,
+        in_specs=[VMEM] * len(operands),
+        out_specs=jax.tree.map(lambda _: VMEM, out_shape),
+        scratch_shapes=scratch_shapes,
+        compiler_params=pltpu.CompilerParams(vmem_limit_bytes=small_grant),
+    )(*[pltpu.with_memory_space_constraint(operand, pltpu.VMEM) for operand in operands])
 
 
 def per_device(
@@ -245,40 +283,36 @@
     tile = tile_rows * tile_cols
     row_count, col_count = lax.axis_size("rows"), lax.axis_size("cols")
     chip_count = col_count // 2
-    row_even = lax.axis_index("rows") % 2 == 0
-    col_even = lax.axis_index("cols") % 2 == 0
-    parity = jnp.stack([lax.axis_index("rows") % 2, lax.axis_index("cols") % 2]).astype(jnp.int32)
-    row_vector = lambda v: v.reshape(1, channels)
-
-    frames = jnp.concatenate([frame_cache[0], hidden], axis=0)
-    top, bottom = frames[:, 0], frames[:, tile_rows - 1]
-    row_a = lax.ppermute(jnp.where(row_even, bottom, top), "rows", near_pairs(row_count, 0))
-    row_b = lax.ppermute(jnp.where(row_even, top, bottom), "rows", near_pairs(row_count, 1))
-    above = jnp.where(row_even, row_b, row_a)
-    below = jnp.where(row_even, row_a, row_b)
-    edges = []
-    for at in (0, tile_cols - 1):
-        edges.append(
-            jnp.concatenate(
-                [above[:, at][:, None], frames[:, :, at], below[:, at][:, None]], axis=1
-            ).reshape(3 * (tile_rows + 2), channels)
-        )
-    col_a = lax.ppermute(jnp.where(col_even, edges[1], edges[0]), "cols", near_pairs(col_count, 0))
-    col_b = lax.ppermute(jnp.where(col_even, edges[0], edges[1]), "cols", near_pairs(col_count, 1))
-
-    normed, mixed = pl.pallas_call(
+    wide = pltpu.VMEM((tile, channels), bf16)
+
+    edge_rows = pltpu.VMEM((3, tile_cols, channels), bf16)
+    row_a, row_b = pl.pallas_call(
+        functools.partial(rows_kernel, tile_rows),
+        out_shape=(edge_rows, edge_rows),
+        in_specs=[ANY, ANY],
+        out_specs=(VMEM, VMEM),
+        scratch_shapes=[pltpu.SemaphoreType.DMA((6,))],
+        compiler_params=pltpu.CompilerParams(vmem_limit_bytes=small_grant),
+        cost_estimate=stage_cost,
+        name="edge_rows",
+    )(*[pltpu.with_memory_space_constraint(v, pltpu.HBM) for v in (frame_cache, hidden)])
+    row_a = lax.ppermute(row_a, "rows", near_pairs(row_count, 0))
+    row_b = lax.ppermute(row_b, "rows", near_pairs(row_count, 1))
+    edge_cols = pltpu.VMEM((3 * (tile_rows + 2), channels), bf16)
+    col_a, col_b = call(
+        functools.partial(cols_kernel, tile_rows, tile_cols),
+        (edge_cols, edge_cols),
+        frame_cache,
+        hidden,
+        row_a,
+        row_b,
+    )
+    col_a = lax.ppermute(col_a, "cols", near_pairs(col_count, 0))
+    col_b = lax.ppermute(col_b, "cols", near_pairs(col_count, 1))
+
+    normed, mixed = call(
         functools.partial(conv_kernel, tile_rows, tile_cols, channels),
-        out_shape=(shape((tile, channels), bf16), shape((tile, channels), bf16)),
-        in_specs=[SMEM] + [VMEM] * 10 + [ANY],
-        out_specs=(VMEM, VMEM),
-        scratch_shapes=[
-            pltpu.VMEM((9, 3 * channels, channels), bf16),
-            pltpu.VMEM((3, (tile_rows + 2) * tile_cols, 3 * channels), bf16),
-            pltpu.SemaphoreType.DMA((9,)),
-        ],
-        name="conv",
-    )(
-        parity,
+        (wide, wide),
         frame_cache,
         hidden,
         shortcut.reshape(tile, channels),
@@ -286,78 +320,73 @@
         row_b,
         col_a,
         col_b,
-        row_vector(gain_one),
-        row_vector(conv_bias),
-        row_vector(gain_two),
-        conv_weight.reshape(9, 3 * channels, channels),
-    )
-
-    key_blocks = [normed] + [
-        lax.ppermute(normed, "rows", far_pairs(row_count, step))
-        for step in range(row_count - 1, 0, -1)
-    ]
-    query_blocks = jnp.concatenate(
-        [normed]
-        + [
-            lax.ppermute(normed, "cols", far_pairs(chip_count, step, 2))
-            for step in range(1, chip_count)
+        gain_one,
+        conv_bias,
+        gain_two,
+        conv_weight,
+        scratch_shapes=[
+            pltpu.VMEM((3, (tile_rows + 2) * tile_cols, 3 * channels), bf16),
         ],
-        axis=0,
-    )
-    other_queries = lax.ppermute(query_blocks, "cols", near_pairs(col_count, 0))
-    query_rows = 2 * chip_count * tile
-    queries = pl.pallas_call(
-        lambda *refs: query_kernel(float(channels) ** (-0.5), 2, refs),
-        out_shape=shape((query_rows, channels), bf16),
-        in_specs=[VMEM] * 5,
-        out_specs=VMEM,
-        name="queries",
-    )(query_blocks, other_queries, query_weight, row_vector(query_bias), key_weight)
+    )
+
+    key_blocks = [normed]
+    for step in range(row_count - 1, 0, -1):
+        key_blocks.append(lax.ppermute(normed, "rows", far_pairs(row_count, step)))
+    near_queries = [normed]
+    for step in range(1, chip_count):
+        near_queries.append(lax.ppermute(normed, "cols", far_pairs(chip_count, step, 2)))
+    other_queries = []
+    for block in near_queries:
+        other_queries.append(lax.ppermute(block, "cols", near_pairs(col_count, 0)))
+    queries = call(
+        functools.partial(query_kernel, float(channels) ** (-0.5), 2 * chip_count),
+        pltpu.VMEM((2 * chip_count * tile, channels), bf16),
+        *near_queries,
+        *other_queries,
+        query_weight,
+        query_bias,
+        key_weight,
+    )
 
     kept_rows = chip_count * tile
-    kept, kept_log, sent = pl.pallas_call(
+    kept, kept_log, sent = call(
         functools.partial(attend_kernel, row_count, kept_rows, tile),
-        out_shape=(
-            shape((kept_rows, channels), f32),
-            shape((kept_rows, stat_lanes), f32),
-            shape((kept_rows, channels + stat_lanes), bf16),
+        (
+            pltpu.VMEM((kept_rows, channels), f32),
+            pltpu.VMEM((kept_rows, stat_lanes), f32),
+            pltpu.VMEM((kept_rows, channels + stat_lanes), bf16),
         ),
-        in_specs=[VMEM] * (1 + row_count),
-        out_specs=(VMEM, VMEM, VMEM),
-        name="attend",
-    )(queries, *key_blocks)
+        queries,
+        *key_blocks,
+    )
     received = lax.ppermute(sent, "cols", near_pairs(col_count, 0))
 
-    packed = shape((tile, channels + stat_lanes), bf16)
-    own, own_log, *results = pl.pallas_call(
+    packed = pltpu.VMEM((tile, channels + stat_lanes), bf16)
+    own, own_log, *results = call(
         functools.partial(chip_kernel, tile),
-        out_shape=(shape((tile, channels), f32), shape((tile, stat_lanes), f32))
+        (pltpu.VMEM((tile, channels), f32), pltpu.VMEM((tile, stat_lanes), f32))
         + (packed,) * (chip_count - 1),
-        in_specs=[VMEM] * 3,
-        out_specs=(VMEM,) * (chip_count + 1),
-        name="chip",
-    )(kept, kept_log, received)
+        kept,
+        kept_log,
+        received,
+    )
     returned = [
         lax.ppermute(
             result, "cols", [(j, i) for i, j in far_pairs(chip_count, step, 2)]
         )
         for step, result in enumerate(results, 1)
     ]
-    decoded = pl.pallas_call(
+    decoded = call(
         functools.partial(final_kernel, tile, chip_count - 1),
-        out_shape=shape((tile, channels), bf16),
-        in_specs=[VMEM] * (2 + chip_count - 1 + 5),
-        out_specs=VMEM,
-        name="final",
-    )(
+        jax.ShapeDtypeStruct((tile, channels), bf16),
         own,
         own_log,
         *returned,
         mixed,
         value_weight,
-        row_vector(value_bias),
+        value_bias,
         out_weight,
-        row_vector(out_bias),
+        out_bias,
     )
     return decoded.reshape(1, tile_rows, tile_cols, channels)
 

time: 59.6 us -> 45.6 us (0.77)
  local copies, waits for them, and re-layouts: 11.4 us -> 0.07 us
  Pallas kernels: 17.3 us -> 7.78 us
  waiting for transfers between devices: 10.5 us -> 17.7 us
  other arithmetic: 2.35 us -> 0 us
  starting transfers between devices: 17.4 us -> 19.7 us
    pallas_call x5 -> x7, Pallas kernels: 17.3 us -> 7.78 us  [the longest x6 6.78 us: call(): pl.pallas_call(kernel, out_shape=out_shape, in_specs=[VMEM] * len(operand...]
    unnamed x30 -> x28, local copies, waits for them, and re-layouts: 5.8 us -> 0.07 us
    reshape x6 -> x0, local copies, waits for them, and re-layouts: 5.49 us -> none  [per_device(): row_vector = lambda v: v.reshape(1, channels)]
    ppermute x8 -> x9, waiting for transfers between devices: 3.72 us -> 8.41 us  [the longest x3 6.22 us: per_device(): key_blocks.append(lax.ppermute(normed, 'rows', far_pairs(row_count, step)))]
    ppermute x1, starting transfers between devices: 3.43 us -> 5.89 us  [per_device(): lax.ppermute(normed, 'cols', far_pairs(chip_count, step, 2))]
    ppermute x1, waiting for transfers between devices: 3.1 us -> 4.54 us  [per_device(): lax.ppermute(result, 'cols', [(j, i) for i, j in far_pairs(chip_count, st...]
    ppermute x1, waiting for transfers between devices: 1.94 us -> 3.25 us  [per_device(): lax.ppermute(normed, 'cols', far_pairs(chip_count, step, 2))]
    select_n x3 -> x0, other arithmetic: 0.91 us -> none  [the longest x1 0.84 us: per_device(): jnp.where(row_even, top, bottom)]
  transfers between devices with their start and end apart: 11 -> 12, of which waited for: 5 -> 6; matrix products, arithmetic and copies ran while one was open for 13% -> 0% of each run, Pallas kernels for 5% -> 2%
where the time goes in v2:
time: 45.6 us; the launch traced here: 45.5 us
  starting transfers between devices  19.7 us (43%)
  waiting for transfers between devices  17.7 us (39%)
  Pallas kernels  7.78 us (17%)
    ppermute x3, starting transfers between devices, per_device(): key_blocks.append(lax.ppermute(normed, 'rows', far_pairs(row_count, step)))  8.09 us
    pallas_call x6, Pallas kernels, call(): pl.pallas_call(kernel, out_shape=out_shape, in_specs=[VMEM] * len(operand...  6.78 us
    ppermute x3, waiting for transfers between devices, per_device(): key_blocks.append(lax.ppermute(normed, 'rows', far_pairs(row_count, step)))  6.22 us
    ppermute x1, starting transfers between devices, per_device(): lax.ppermute(normed, 'cols', far_pairs(chip_count, step, 2))  5.89 us
    ppermute x1, waiting for transfers between devices, per_device(): lax.ppermute(result, 'cols', [(j, i) for i, j in far_pairs(chip_count, st...  4.54 us
    ppermute x1, waiting for transfers between devices, per_device(): lax.ppermute(normed, 'cols', far_pairs(chip_count, step, 2))  3.25 us
    ppermute x1, starting transfers between devices, per_device(): row_a = lax.ppermute(row_a, 'rows', near_pairs(row_count, 0))  3.13 us
    ppermute x1, waiting for transfers between devices, per_device(): row_a = lax.ppermute(row_a, 'rows', near_pairs(row_count, 0))  1.67 us
  transfers between devices with their start and end apart: 12, of which 6 were waited for; matrix products, arithmetic and copies ran while one was open for 0% of the time, Pallas kernels for 2%

profile of v2, /device:TPU:0, one launch (start us, length us, event | category | flops | bytes accessed | tf_op | source)
XLA Modules:
  0.0 45.5 jit_solution(17346799960801756529)
XLA Ops:
  0.0 0.0 copy-start.1
  0.0 0.0 copy-start.2
  0.0 0.0 copy-start.13
  0.0 0.0 copy-start.12
  0.0 0.0 copy-start
  0.0 0.0 copy-start.11
  0.0 0.0 copy-start.7
  0.0 1.0 %edge_rows.1 = (bf16[3,32,384]{2,1,0:T(8,128)(2,1)S(1)}, bf16[3,32,384]{2,1,0:T(8,128)(2,1)S(1)}) custom-call(bf16[1,2,4,32,384]{4,3,2,1,0:T(8,128)(2,1)} %cache.5, bf16[1,4,32,384]{3,2,1,0:T(8,128)(2,1)} %hidden.5), custom_call_target="tpu_custom_call" | custom-call | flops 10000000000 | bytes 10000000 | tf_op jit(solution)/shard_map/edge_rows/pallas_call | solution.py:289
  1.0 0.0 copy-start.3
  1.1 0.0 copy-start.4
  1.1 0.0 copy-start.8
  1.1 0.0 copy-start.5
  1.1 0.0 copy-start.6
  1.1 0.0 copy-start.9
  1.1 0.0 copy-start.10
  1.1 3.1 %collective-permute-start = (bf16[3,32,384]{2,1,0:T(8,128)(2,1)S(1)}, bf16[3,32,384]{2,1,0:T(8,128)(2,1)S(1)}, u32[]{:S(2)}, u32[]{:S(2)}) collective-permute-start(bf16[3,32,384]{2,1,0:T(8,128)(2,1)S(1)} %get-tuple-element.17), channel_id=1, source_target_pairs={{0,4},{4,0},{8,12},{12,8},{1,5},{5,1},{9,13},{13,9},{2,6},{6,2},{1... | collective-permute-start | bytes 221192 | tf_op jit(solution)/shard_map/ppermute | solution.py:299
  4.3 0.7 %collective-permute-start.1 = (bf16[3,32,384]{2,1,0:T(8,128)(2,1)S(1)}, bf16[3,32,384]{2,1,0:T(8,128)(2,1)S(1)}, u32[]{:S(2)}, u32[]{:S(2)}) collective-permute-start(bf16[3,32,384]{2,1,0:T(8,128)(2,1)S(1)} %get-tuple-element.18), channel_id=1, source_target_pairs={{4,8},{8,4},{5,9},{9,5},{6,10},{10,6},{7,11},{11,7},{20,24},{24,20... | collective-permute-start | bytes 221192 | tf_op jit(solution)/shard_map/ppermute | solution.py:300
  4.9 1.7 %collective-permute-done.row_a = bf16[3,32,384]{2,1,0:T(8,128)(2,1)S(1)} collective-permute-done((bf16[3,32,384]{2,1,0:T(8,128)(2,1)S(1)}, bf16[3,32,384]{2,1,0:T(8,128)(2,1)S(1)}, u32[]{:S(2)}, u32[]{:S(2)}) %collective-permute-start) | collective-permute-done | bytes 73760 | tf_op jit(solution)/shard_map/ppermute | solution.py:299
  6.6 0.0 collective-permute-done.1.row_b
  6.6 0.0 copy-done.1
  6.6 0.0 copy-done.2
  6.6 0.1 shard_map.136
  6.7 0.1 collective-permute-start.2
  6.8 0.7 %collective-permute-start.3 = (bf16[18,384]{1,0:T(8,128)(2,1)S(1)}, bf16[18,384]{1,0:T(8,128)(2,1)S(1)}, u32[]{:S(2)}, u32[]{:S(2)}) collective-permute-start(bf16[18,384]{1,0:T(8,128)(2,1)S(1)} %get-tuple-element.20), channel_id=1, source_target_pairs={{1,2},{2,1},{5,6},{6,5},{9,10},{10,9},{13,14},{14,13},{17,18},{18,... | collective-permute-start | bytes 41480 | tf_op jit(solution)/shard_map/ppermute | solution.py:311
  7.5 0.5 %collective-permute-done.2.col_a = bf16[18,384]{1,0:T(8,128)(2,1)S(1)} collective-permute-done((bf16[18,384]{1,0:T(8,128)(2,1)S(1)}, bf16[18,384]{1,0:T(8,128)(2,1)S(1)}, u32[]{:S(2)}, u32[]{:S(2)}) %collective-permute-start.2) | collective-permute-done | bytes 13856 | tf_op jit(solution)/shard_map/ppermute | solution.py:310
  8.0 0.0 collective-permute-done.3.col_b
  8.0 0.0 copy-done.13
  8.0 0.0 copy-done.12
  8.0 0.0 copy-done
  8.0 0.0 copy-done.11
  8.0 0.0 copy-done.7
  8.0 1.9 %shard_map.137 = (bf16[128,384]{1,0:T(8,128)(2,1)S(1)}, bf16[128,384]{1,0:T(8,128)(2,1)S(1)}) custom-call(bf16[1,2,4,32,384]{4,3,2,1,0:T(8,128)(2,1)S(1)} %copy-done.1, bf16[1,4,32,384]{3,2,1,0:T(8,128)(2,1)S(1)} %copy-done.2, bf16[128,384]{1,0:T(8,128)(2,1)S(1)} %bitcast.2, bf16[3,32,384]{2,1,0:T(8,128)(2,1)S(1)} %collective-permute-done.row_a, ...), custom_call_target="tpu_custom_call" | custom-call | tf_op jit(solution)/shard_map/pallas_call | solution.py:256
  9.9 5.9 %collective-permute-start.4 = (bf16[128,384]{1,0:T(8,128)(2,1)S(1)}, bf16[128,384]{1,0:T(8,128)(2,1)S(1)}, u32[]{:S(2)}, u32[]{:S(2)}) collective-permute-start(bf16[128,384]{1,0:T(8,128)(2,1)S(1)} %get-tuple-element.21.refs_0_.refs_1_), channel_id=1, source_target_pairs={{0,2},{1,3},{2,0},{3,1},{4,6},{5,7},{6,4},{7,5},{8,10},{9,11},{10,... | collective-permute-start | bytes 294920 | tf_op jit(solution)/shard_map/ppermute | solution.py:337
  15.8 0.0 collective-permute-start.5
  15.8 3.2 %collective-permute-done.4.refs_1_ = bf16[128,384]{1,0:T(8,128)(2,1)S(1)} collective-permute-done((bf16[128,384]{1,0:T(8,128)(2,1)S(1)}, bf16[128,384]{1,0:T(8,128)(2,1)S(1)}, u32[]{:S(2)}, u32[]{:S(2)}) %collective-permute-start.4) | collective-permute-done | bytes 98336 | tf_op jit(solution)/shard_map/ppermute | solution.py:337
  19.1 0.0 collective-permute-start.6
  19.1 5.2 %collective-permute-start.9 = (bf16[128,384]{1,0:T(8,128)(2,1)S(1)}, bf16[128,384]{1,0:T(8,128)(2,1)S(1)}, u32[]{:S(2)}, u32[]{:S(2)}) collective-permute-start(bf16[128,384]{1,0:T(8,128)(2,1)S(1)} %get-tuple-element.21.refs_0_.refs_1_), channel_id=1, source_target_pairs={{0,4},{4,0},{8,12},{12,8},{1,5},{5,1},{9,13},{13,9},{2,6},{6,2},{1... | collective-permute-start | bytes 294920 | tf_op jit(solution)/shard_map/ppermute | solution.py:334
  24.3 1.4 %collective-permute-start.8 = (bf16[128,384]{1,0:T(8,128)(2,1)S(1)}, bf16[128,384]{1,0:T(8,128)(2,1)S(1)}, u32[]{:S(2)}, u32[]{:S(2)}) collective-permute-start(bf16[128,384]{1,0:T(8,128)(2,1)S(1)} %get-tuple-element.21.refs_0_.refs_1_), channel_id=1, source_target_pairs={{0,8},{4,12},{8,0},{12,4},{1,9},{5,13},{9,1},{13,5},{2,10},{6,14},... | collective-permute-start | bytes 294920 | tf_op jit(solution)/shard_map/ppermute | solution.py:334
  25.7 1.5 %collective-permute-start.7 = (bf16[128,384]{1,0:T(8,128)(2,1)S(1)}, bf16[128,384]{1,0:T(8,128)(2,1)S(1)}, u32[]{:S(2)}, u32[]{:S(2)}) collective-permute-start(bf16[128,384]{1,0:T(8,128)(2,1)S(1)} %get-tuple-element.21.refs_0_.refs_1_), channel_id=1, source_target_pairs={{0,12},{4,8},{8,4},{12,0},{1,13},{5,9},{9,5},{13,1},{2,14},{6,10},... | collective-permute-start | bytes 294920 | tf_op jit(solution)/shard_map/ppermute | solution.py:334
  27.2 0.0 collective-permute-done.5.refs_2_
  27.2 0.0 collective-permute-done.6.refs_3_
  27.2 0.0 copy-done.3
  27.2 0.0 copy-done.4
  27.2 0.0 copy-done.8
  27.2 1.1 %shard_map.138.refs_0_ = bf16[512,384]{1,0:T(8,128)(2,1)S(1)} custom-call(bf16[128,384]{1,0:T(8,128)(2,1)S(1)} %get-tuple-element.21.refs_0_.refs_1_, bf16[128,384]{1,0:T(8,128)(2,1)S(1)} %collective-permute-done.4.refs_1_, bf16[128,384]{1,0:T(8,128)(2,1)S(1)} %collective-permute-done.5.refs_2_, bf16[128,384]{1,0:T(8,128)(2,1)S(1)} %collective-permute-done.6.refs_3_, ...), custom_call_target="tpu_custom_call" | custom-call | tf_op jit(solution)/shard_map/pallas_call | solution.py:256
  28.4 0.0 collective-permute-done.9.refs_4_
  28.4 6.2 %collective-permute-done.8.refs_3_ = bf16[128,384]{1,0:T(8,128)(2,1)S(1)} collective-permute-done((bf16[128,384]{1,0:T(8,128)(2,1)S(1)}, bf16[128,384]{1,0:T(8,128)(2,1)S(1)}, u32[]{:S(2)}, u32[]{:S(2)}) %collective-permute-start.8) | collective-permute-done | bytes 98336 | tf_op jit(solution)/shard_map/ppermute | solution.py:334
  34.6 0.0 collective-permute-done.7.refs_2_
  34.6 2.1 %shard_map.139 = (f32[256,384]{1,0:T(8,128)S(1)}, f32[256,128]{1,0:T(8,128)S(1)}, bf16[256,512]{1,0:T(8,128)(2,1)S(1)}) custom-call(bf16[512,384]{1,0:T(8,128)(2,1)S(1)} %shard_map.138.refs_0_, bf16[128,384]{1,0:T(8,128)(2,1)S(1)} %get-tuple-element.21.refs_0_.refs_1_, bf16[128,384]{1,0:T(8,128)(2,1)S(1)} %collective-permute-done.7.refs_2_, ...), custom_call_target="tpu_custom_call" | custom-call | tf_op jit(solution)/shard_map/pallas_call | solution.py:256
  36.7 0.1 collective-permute-start.10
  36.8 1.5 %collective-permute-done.10.received = bf16[256,512]{1,0:T(8,128)(2,1)S(1)} collective-permute-done((bf16[256,512]{1,0:T(8,128)(2,1)S(1)}, bf16[256,512]{1,0:T(8,128)(2,1)S(1)}, u32[]{:S(2)}, u32[]{:S(2)}) %collective-permute-start.10) | collective-permute-done | bytes 262176 | tf_op jit(solution)/shard_map/ppermute | solution.py:362
  38.3 0.3 shard_map.140
  38.6 1.1 %collective-permute-start.11 = (bf16[128,512]{1,0:T(8,128)(2,1)S(1)}, bf16[128,512]{1,0:T(8,128)(2,1)S(1)}, u32[]{:S(2)}, u32[]{:S(2)}) collective-permute-start(bf16[128,512]{1,0:T(8,128)(2,1)S(1)} %get-tuple-element.27), channel_id=1, source_target_pairs={{2,0},{3,1},{0,2},{1,3},{6,4},{7,5},{4,6},{5,7},{10,8},{11,9},{8,1... | collective-permute-start | bytes 393224 | tf_op jit(solution)/shard_map/ppermute | solution.py:374
  39.7 4.5 %collective-permute-done.11.refs_2_ = bf16[128,512]{1,0:T(8,128)(2,1)S(1)} collective-permute-done((bf16[128,512]{1,0:T(8,128)(2,1)S(1)}, bf16[128,512]{1,0:T(8,128)(2,1)S(1)}, u32[]{:S(2)}, u32[]{:S(2)}) %collective-permute-start.11) | collective-permute-done | bytes 131104 | tf_op jit(solution)/shard_map/ppermute | solution.py:374
  44.2 0.0 copy-done.5
  44.2 0.0 copy-done.6
  44.2 0.0 copy-done.9
  44.2 0.0 copy-done.10
  44.2 1.2 %shard_map.141 = bf16[128,384]{1,0:T(8,128)(2,1)} custom-call(f32[128,384]{1,0:T(8,128)S(1)} %get-tuple-element.25.refs_0_, f32[128,128]{1,0:T(8,128)S(1)} %get-tuple-element.26.refs_1_, bf16[128,512]{1,0:T(8,128)(2,1)S(1)} %collective-permute-done.11.refs_2_, bf16[128,384]{1,0:T(8,128)(2,1)S(1)} %get-tuple-element.28.refs_3_, ...), custom_call_target="tpu_custom_call" | custom-call | tf_op jit(solution)/shard_map/pallas_call | solution.py:256
Async XLA Ops:
  0.0 6.6 %copy-start.1 = (bf16[1,2,4,32,384]{4,3,2,1,0:T(8,128)(2,1)S(1)}, bf16[1,2,4,32,384]{4,3,2,1,0:T(8,128)(2,1)}, u32[]{:S(2)}) copy-start(bf16[1,2,4,32,384]{4,3,2,1,0:T(8,128)(2,1)} %cache.5) | copy-start | bytes 589828
  0.0 6.6 %copy-start.2 = (bf16[1,4,32,384]{3,2,1,0:T(8,128)(2,1)S(1)}, bf16[1,4,32,384]{3,2,1,0:T(8,128)(2,1)}, u32[]{:S(2)}) copy-start(bf16[1,4,32,384]{3,2,1,0:T(8,128)(2,1)} %hidden.5) | copy-start | bytes 294916
  0.0 8.0 %copy-start.13 = (f32[384]{0:T(512)S(1)}, f32[384]{0:T(512)}, u32[]{:S(2)}) copy-start(f32[384]{0:T(512)} %gain_two.1) | copy-start | bytes 4612
  0.0 8.0 %copy-start.12 = (f32[384]{0:T(512)S(1)}, f32[384]{0:T(512)}, u32[]{:S(2)}) copy-start(f32[384]{0:T(512)} %conv_bias.1) | copy-start | bytes 4612
  0.0 8.0 %copy-start = (bf16[3,3,3,384,384]{4,3,2,1,0:T(8,128)(2,1)S(1)}, bf16[3,3,3,384,384]{4,3,2,1,0:T(8,128)(2,1)}, u32[]{:S(2)}) copy-start(bf16[3,3,3,384,384]{4,3,2,1,0:T(8,128)(2,1)} %weight.1) | copy-start | bytes 23887876
  0.0 8.0 %copy-start.11 = (f32[384]{0:T(512)S(1)}, f32[384]{0:T(512)}, u32[]{:S(2)}) copy-start(f32[384]{0:T(512)} %gain_one.1) | copy-start | bytes 4612
  0.0 8.0 %copy-start.7 = (bf16[1,4,32,384]{3,2,1,0:T(8,128)(2,1)S(1)}, bf16[1,4,32,384]{3,2,1,0:T(8,128)(2,1)}, u32[]{:S(2)}) copy-start(bf16[1,4,32,384]{3,2,1,0:T(8,128)(2,1)} %param.16) | copy-start | bytes 294916
  1.0 26.2 %copy-start.3 = (bf16[384,384]{1,0:T(8,128)(2,1)S(1)}, bf16[384,384]{1,0:T(8,128)(2,1)}, u32[]{:S(2)}) copy-start(bf16[384,384]{1,0:T(8,128)(2,1)} %refs_4_.2) | copy-start | bytes 884740
  1.1 26.1 %copy-start.4 = (bf16[384,384]{1,0:T(8,128)(2,1)S(1)}, bf16[384,384]{1,0:T(8,128)(2,1)}, u32[]{:S(2)}) copy-start(bf16[384,384]{1,0:T(8,128)(2,1)} %refs_6_.2) | copy-start | bytes 884740
  1.1 26.1 %copy-start.8 = (f32[384]{0:T(512)S(1)}, f32[384]{0:T(512)}, u32[]{:S(2)}) copy-start(f32[384]{0:T(512)} %refs_5_.2) | copy-start | bytes 4612
  1.1 43.1 %copy-start.5 = (bf16[384,384]{1,0:T(8,128)(2,1)S(1)}, bf16[384,384]{1,0:T(8,128)(2,1)}, u32[]{:S(2)}) copy-start(bf16[384,384]{1,0:T(8,128)(2,1)} %refs_4_.3) | copy-start | bytes 884740
  1.1 43.1 %copy-start.6 = (bf16[384,384]{1,0:T(8,128)(2,1)S(1)}, bf16[384,384]{1,0:T(8,128)(2,1)}, u32[]{:S(2)}) copy-start(bf16[384,384]{1,0:T(8,128)(2,1)} %refs_6_.3) | copy-start | bytes 884740
  1.1 43.1 %copy-start.9 = (f32[384]{0:T(512)S(1)}, f32[384]{0:T(512)}, u32[]{:S(2)}) copy-start(f32[384]{0:T(512)} %refs_5_.3) | copy-start | bytes 4612
  1.1 43.1 %copy-start.10 = (f32[384]{0:T(512)S(1)}, f32[384]{0:T(512)}, u32[]{:S(2)}) copy-start(f32[384]{0:T(512)} %refs_7_.1) | copy-start | bytes 4612
  1.1 5.5 %collective-permute-start = (bf16[3,32,384]{2,1,0:T(8,128)(2,1)S(1)}, bf16[3,32,384]{2,1,0:T(8,128)(2,1)S(1)}, u32[]{:S(2)}, u32[]{:S(2)}) collective-permute-start(bf16[3,32,384]{2,1,0:T(8,128)(2,1)S(1)} %get-tuple-element.17), channel_id=1, source_target_pairs={{0,4},{4,0},{8,12},{12,8},{1,5},{5,1},{9,13},{13,9},{2,6},{6,2},{1... | collective-permute-start | bytes 221192 | tf_op jit(solution)/shard_map/ppermute | solution.py:299
  4.3 2.3 %collective-permute-start.1 = (bf16[3,32,384]{2,1,0:T(8,128)(2,1)S(1)}, bf16[3,32,384]{2,1,0:T(8,128)(2,1)S(1)}, u32[]{:S(2)}, u32[]{:S(2)}) collective-permute-start(bf16[3,32,384]{2,1,0:T(8,128)(2,1)S(1)} %get-tuple-element.18), channel_id=1, source_target_pairs={{4,8},{8,4},{5,9},{9,5},{6,10},{10,6},{7,11},{11,7},{20,24},{24,20... | collective-permute-start | bytes 221192 | tf_op jit(solution)/shard_map/ppermute | solution.py:300
  6.7 1.3 %collective-permute-start.2 = (bf16[18,384]{1,0:T(8,128)(2,1)S(1)}, bf16[18,384]{1,0:T(8,128)(2,1)S(1)}, u32[]{:S(2)}, u32[]{:S(2)}) collective-permute-start(bf16[18,384]{1,0:T(8,128)(2,1)S(1)} %get-tuple-element.19), channel_id=1, source_target_pairs={{0,1},{1,0},{2,3},{3,2},{4,5},{5,4},{6,7},{7,6},{8,9},{9,8},{10,11... | collective-permute-start | bytes 41480 | tf_op jit(solution)/shard_map/ppermute | solution.py:310
  6.8 1.2 %collective-permute-start.3 = (bf16[18,384]{1,0:T(8,128)(2,1)S(1)}, bf16[18,384]{1,0:T(8,128)(2,1)S(1)}, u32[]{:S(2)}, u32[]{:S(2)}) collective-permute-start(bf16[18,384]{1,0:T(8,128)(2,1)S(1)} %get-tuple-element.20), channel_id=1, source_target_pairs={{1,2},{2,1},{5,6},{6,5},{9,10},{10,9},{13,14},{14,13},{17,18},{18,... | collective-permute-start | bytes 41480 | tf_op jit(solution)/shard_map/ppermute | solution.py:311
  9.9 9.1 %collective-permute-start.4 = (bf16[128,384]{1,0:T(8,128)(2,1)S(1)}, bf16[128,384]{1,0:T(8,128)(2,1)S(1)}, u32[]{:S(2)}, u32[]{:S(2)}) collective-permute-start(bf16[128,384]{1,0:T(8,128)(2,1)S(1)} %get-tuple-element.21.refs_0_.refs_1_), channel_id=1, source_target_pairs={{0,2},{1,3},{2,0},{3,1},{4,6},{5,7},{6,4},{7,5},{8,10},{9,11},{10,... | collective-permute-start | bytes 294920 | tf_op jit(solution)/shard_map/ppermute | solution.py:337
  15.8 11.4 %collective-permute-start.5 = (bf16[128,384]{1,0:T(8,128)(2,1)S(1)}, bf16[128,384]{1,0:T(8,128)(2,1)S(1)}, u32[]{:S(2)}, u32[]{:S(2)}) collective-permute-start(bf16[128,384]{1,0:T(8,128)(2,1)S(1)} %get-tuple-element.21.refs_0_.refs_1_), channel_id=1, source_target_pairs={{0,1},{1,0},{2,3},{3,2},{4,5},{5,4},{6,7},{7,6},{8,9},{9,8},{10,11... | collective-permute-start | bytes 294920 | tf_op jit(solution)/shard_map/ppermute | solution.py:340
  19.1 8.1 %collective-permute-start.6 = (bf16[128,384]{1,0:T(8,128)(2,1)S(1)}, bf16[128,384]{1,0:T(8,128)(2,1)S(1)}, u32[]{:S(2)}, u32[]{:S(2)}) collective-permute-start(bf16[128,384]{1,0:T(8,128)(2,1)S(1)} %collective-permute-done.4.refs_1_), channel_id=1, source_target_pairs={{0,1},{1,0},{2,3},{3,2},{4,5},{5,4},{6,7},{7,6},{8,9},{9,8},{10,11... | collective-permute-start | bytes 294920 | tf_op jit(solution)/shard_map/ppermute | solution.py:340
  19.1 9.3 %collective-permute-start.9 = (bf16[128,384]{1,0:T(8,128)(2,1)S(1)}, bf16[128,384]{1,0:T(8,128)(2,1)S(1)}, u32[]{:S(2)}, u32[]{:S(2)}) collective-permute-start(bf16[128,384]{1,0:T(8,128)(2,1)S(1)} %get-tuple-element.21.refs_0_.refs_1_), channel_id=1, source_target_pairs={{0,4},{4,0},{8,12},{12,8},{1,5},{5,1},{9,13},{13,9},{2,6},{6,2},{1... | collective-permute-start | bytes 294920 | tf_op jit(solution)/shard_map/ppermute | solution.py:334
  24.3 10.3 %collective-permute-start.8 = (bf16[128,384]{1,0:T(8,128)(2,1)S(1)}, bf16[128,384]{1,0:T(8,128)(2,1)S(1)}, u32[]{:S(2)}, u32[]{:S(2)}) collective-permute-start(bf16[128,384]{1,0:T(8,128)(2,1)S(1)} %get-tuple-element.21.refs_0_.refs_1_), channel_id=1, source_target_pairs={{0,8},{4,12},{8,0},{12,4},{1,9},{5,13},{9,1},{13,5},{2,10},{6,14},... | collective-permute-start | bytes 294920 | tf_op jit(solution)/shard_map/ppermute | solution.py:334
  25.7 8.9 %collective-permute-start.7 = (bf16[128,384]{1,0:T(8,128)(2,1)S(1)}, bf16[128,384]{1,0:T(8,128)(2,1)S(1)}, u32[]{:S(2)}, u32[]{:S(2)}) collective-permute-start(bf16[128,384]{1,0:T(8,128)(2,1)S(1)} %get-tuple-element.21.refs_0_.refs_1_), channel_id=1, source_target_pairs={{0,12},{4,8},{8,4},{12,0},{1,13},{5,9},{9,5},{13,1},{2,14},{6,10},... | collective-permute-start | bytes 294920 | tf_op jit(solution)/shard_map/ppermute | solution.py:334
  36.7 1.6 %collective-permute-start.10 = (bf16[256,512]{1,0:T(8,128)(2,1)S(1)}, bf16[256,512]{1,0:T(8,128)(2,1)S(1)}, u32[]{:S(2)}, u32[]{:S(2)}) collective-permute-start(bf16[256,512]{1,0:T(8,128)(2,1)S(1)} %get-tuple-element.24), channel_id=1, source_target_pairs={{0,1},{1,0},{2,3},{3,2},{4,5},{5,4},{6,7},{7,6},{8,9},{9,8},{10,11... | collective-permute-start | bytes 786440 | tf_op jit(solution)/shard_map/ppermute | solution.py:362
  38.6 5.6 %collective-permute-start.11 = (bf16[128,512]{1,0:T(8,128)(2,1)S(1)}, bf16[128,512]{1,0:T(8,128)(2,1)S(1)}, u32[]{:S(2)}, u32[]{:S(2)}) collective-permute-start(bf16[128,512]{1,0:T(8,128)(2,1)S(1)} %get-tuple-element.27), channel_id=1, source_target_pairs={{2,0},{3,1},{0,2},{1,3},{6,4},{7,5},{4,6},{5,7},{10,8},{11,9},{8,1... | collective-permute-start | bytes 393224 | tf_op jit(solution)/shard_map/ppermute | solution.py:374

commit v3 on v2

--- a/solution.py
+++ b/solution.py
@@ -178,34 +178,57 @@
     return values.astype(bf16), stats.astype(bf16)
 
 
-def attend_kernel(blocks, kept_rows, chunk, *refs):
-    queries = refs[0]
-    keys = refs[1 : 1 + blocks]
-    kept, kept_log, sent = refs[1 + blocks :]
+def weigh(own, keys, state=None):
+    scores = [
+        lax.dot_general(own, key[...], (((1,), (1,)), ((), ())), preferred_element_type=f32)
+        for key in keys
+    ]
+    tops = [jnp.max(s, axis=1, keepdims=True) for s in scores]
+    top = functools.reduce(jnp.maximum, tops if state is None else tops + [state[0]])
+    expos = [jnp.exp(s - top) for s in scores]
+    total = sum(jnp.sum(e, axis=1, keepdims=True) for e in expos)
+    weighted = sum(
+        jnp.dot(e.astype(bf16), key[...], preferred_element_type=f32)
+        for e, key in zip(expos, keys)
+    )
+    if state is not None:
+        scale = jnp.exp(state[0] - top)
+        total += state[1] * scale
+        weighted += state[2] * scale
+    return top, total, weighted
+
+
+def early_kernel(tile, blocks, *refs):
+    queries, keys = refs[0], refs[1 : 1 + blocks]
+    tops, totals, weights = refs[1 + blocks :]
+    for at in range(0, queries.shape[0], tile):
+        rows = pl.ds(at, tile)
+        top, total, weighted = weigh(queries[rows, :], keys)
+        tops[rows, :] = jnp.broadcast_to(top, (tile, stat_lanes))
+        totals[rows, :] = jnp.broadcast_to(total, (tile, stat_lanes))
+        weights[rows, :] = weighted
+
+
+def late_kernel(tile, blocks, first, *refs):
+    queries, tops, totals, weights = refs[:4]
+    keys, outs = refs[4 : 4 + blocks], list(refs[4 + blocks :])
     channels = queries.shape[1]
-    for at in range(0, queries.shape[0], chunk):
-        own = queries[at : at + chunk]
-        scores = [
-            lax.dot_general(own, key[...], (((1,), (1,)), ((), ())), preferred_element_type=f32)
-            for key in keys
-        ]
-        top = functools.reduce(jnp.maximum, [jnp.max(s, axis=1, keepdims=True) for s in scores])
-        expos = [jnp.exp(s - top) for s in scores]
-        total = sum(jnp.sum(e, axis=1, keepdims=True) for e in expos)
-        weighted = sum(
-            jnp.dot(e.astype(bf16), key[...], preferred_element_type=f32)
-            for e, key in zip(expos, keys)
-        )
-        mean = weighted / total
-        log_sum = top + jnp.log(total)
-        if at < kept_rows:
-            kept[at : at + chunk] = mean
-            kept_log[at : at + chunk] = jnp.broadcast_to(log_sum, (chunk, stat_lanes))
+    block = first
+    while outs:
+        rows = pl.ds(block * tile, tile)
+        state = (tops[rows, 0:1], totals[rows, 0:1], weights[rows, :])
+        top, total, weighted = weigh(queries[rows, :], keys, state)
+        mean, log_sum = weighted / total, top + jnp.log(total)
+        if block == 0:
+            own, own_log = outs.pop(0), outs.pop(0)
+            own[...] = mean
+            own_log[...] = jnp.broadcast_to(log_sum, (tile, stat_lanes))
         else:
-            to = at - kept_rows
+            out = outs.pop(0)
             values, stats = pack(mean, log_sum)
-            sent[to : to + chunk, 0:channels] = values
-            sent[to : to + chunk, channels : channels + stat_lanes] = stats
+            out[:, 0:channels] = values
+            out[:, channels : channels + stat_lanes] = stats
+        block += 1
 
 
 def unpack(ref, rows):
@@ -221,22 +244,6 @@
     total = sum(scales)
     mean = sum(values * scale for (values, _), scale in zip(parts, scales)) / total
     return mean, top + jnp.log(total)
-
-
-def chip_kernel(tile, kept, kept_log, received, own, own_log, *sent):
-    for block in range(1 + len(sent)):
-        rows = pl.ds(block * tile, tile)
-        mean, log_sum = merge(
-            [(kept[rows, :], kept_log[rows, 0:1]), unpack(received, rows)]
-        )
-        if block == 0:
-            own[...] = mean
-            own_log[...] = jnp.broadcast_to(log_sum, (tile, stat_lanes))
-        else:
-            channels = mean.shape[1]
-            values, stats = pack(mean, log_sum)
-            sent[block - 1][:, 0:channels] = values
-            sent[block - 1][:, channels : channels + stat_lanes] = stats
 
 
 def final_kernel(tile, others, *refs):
@@ -329,53 +336,55 @@
         ],
     )
 
-    key_blocks = [normed]
+    partners = near_pairs(col_count, 0)
+    arrived = {0: normed}
     for step in range(row_count - 1, 0, -1):
-        key_blocks.append(lax.ppermute(normed, "rows", far_pairs(row_count, step)))
-    near_queries = [normed]
+        arrived[step] = lax.ppermute(normed, "rows", far_pairs(row_count, step))
+    query_blocks = [normed]
     for step in range(1, chip_count):
-        near_queries.append(lax.ppermute(normed, "cols", far_pairs(chip_count, step, 2)))
-    other_queries = []
-    for block in near_queries:
-        other_queries.append(lax.ppermute(block, "cols", near_pairs(col_count, 0)))
+        query_blocks.append(lax.ppermute(normed, "cols", far_pairs(chip_count, step, 2)))
+    keys = {}
+    for step, block in arrived.items():
+        keys[step] = [block, lax.ppermute(block, "cols", partners)]
+    early = keys[0] + keys[row_count - 1]
+    late = [key for step in range(1, row_count - 1) for key in keys[step]]
+
+    query_rows = chip_count * tile
     queries = call(
-        functools.partial(query_kernel, float(channels) ** (-0.5), 2 * chip_count),
-        pltpu.VMEM((2 * chip_count * tile, channels), bf16),
-        *near_queries,
-        *other_queries,
+        functools.partial(query_kernel, float(channels) ** (-0.5), chip_count),
+        pltpu.VMEM((query_rows, channels), bf16),
+        *query_blocks,
         query_weight,
         query_bias,
         key_weight,
     )
-
-    kept_rows = chip_count * tile
-    kept, kept_log, sent = call(
-        functools.partial(attend_kernel, row_count, kept_rows, tile),
-        (
-            pltpu.VMEM((kept_rows, channels), f32),
-            pltpu.VMEM((kept_rows, stat_lanes), f32),
-            pltpu.VMEM((kept_rows, channels + stat_lanes), bf16),
-        ),
+    stat = pltpu.VMEM((query_rows, stat_lanes), f32)
+    state = call(
+        functools.partial(early_kernel, tile, len(early)),
+        (stat, stat, pltpu.VMEM((query_rows, channels), f32)),
         queries,
-        *key_blocks,
-    )
-    received = lax.ppermute(sent, "cols", near_pairs(col_count, 0))
-
+        *early,
+    )
     packed = pltpu.VMEM((tile, channels + stat_lanes), bf16)
-    own, own_log, *results = call(
-        functools.partial(chip_kernel, tile),
-        (pltpu.VMEM((tile, channels), f32), pltpu.VMEM((tile, stat_lanes), f32))
-        + (packed,) * (chip_count - 1),
-        kept,
-        kept_log,
-        received,
-    )
-    returned = [
-        lax.ppermute(
-            result, "cols", [(j, i) for i, j in far_pairs(chip_count, step, 2)]
+    results = call(
+        functools.partial(late_kernel, tile, len(late), 1),
+        (packed,) * (chip_count - 1),
+        queries,
+        *state,
+        *late,
+    )
+    returned = []
+    for step, result in enumerate(results, 1):
+        returned.append(
+            lax.ppermute(result, "cols", [(j, i) for i, j in far_pairs(chip_count, step, 2)])
         )
-        for step, result in enumerate(results, 1)
-    ]
+    own, own_log = call(
+        functools.partial(late_kernel, tile, len(late), 0),
+        (pltpu.VMEM((tile, channels), f32), pltpu.VMEM((tile, stat_lanes), f32)),
+        queries,
+        *state,
+        *late,
+    )
     decoded = call(
         functools.partial(final_kernel, tile, chip_count - 1),
         jax.ShapeDtypeStruct((tile, channels), bf16),

time: 45.6 us -> 35.3 us (0.77)
  waiting for transfers between devices: 17.7 us -> 5.8 us
  starting transfers between devices: 19.7 us -> 21.6 us
    ppermute x6 -> x7, waiting for transfers between devices: 7.75 us -> 0.02 us  [the longest x4 0.01 us: per_device(): keys[step] = [block, lax.ppermute(block, 'cols', partners)]]
    ppermute x1, waiting for transfers between devices: 3.25 us -> 0.27 us  [per_device(): lax.ppermute(normed, 'cols', far_pairs(chip_count, step, 2))]
    ppermute x6 -> x7, starting transfers between devices: 8.17 us -> 10.1 us  [the longest x3 7.24 us: per_device(): arrived[step] = lax.ppermute(normed, 'rows', far_pairs(row_count, step))]
    ppermute x1, waiting for transfers between devices: 4.54 us -> 3.34 us  [per_device(): lax.ppermute(result, 'cols', [(j, i) for i, j in far_pairs(chip_count, st...]
    ppermute x1, starting transfers between devices: 5.89 us -> 5.39 us  [per_device(): lax.ppermute(normed, 'cols', far_pairs(chip_count, step, 2))]
    ppermute x1, starting transfers between devices: 1.07 us -> 1.55 us  [per_device(): lax.ppermute(result, 'cols', [(j, i) for i, j in far_pairs(chip_count, st...]
    pallas_call x6 -> x7, Pallas kernels: 6.78 us -> 6.53 us  [call(): pl.pallas_call(kernel, out_shape=out_shape, in_specs=[VMEM] * len(operand...]
  transfers between devices with their start and end apart: 12 -> 13, of which waited for: 6 -> 4; matrix products, arithmetic and copies ran while one was open for 0% -> 0% of each run, Pallas kernels for 2% -> 7%
where the time goes in v3:
time: 35.3 us; the launch traced here: 35.2 us
  starting transfers between devices  21.6 us (61%)
  Pallas kernels  7.53 us (21%)
  waiting for transfers between devices  5.8 us (16%)
    ppermute x3, starting transfers between devices, per_device(): arrived[step] = lax.ppermute(normed, 'rows', far_pairs(row_count, step))  7.24 us
    pallas_call x7, Pallas kernels, call(): pl.pallas_call(kernel, out_shape=out_shape, in_specs=[VMEM] * len(operand...  6.53 us
    ppermute x1, starting transfers between devices, per_device(): lax.ppermute(normed, 'cols', far_pairs(chip_count, step, 2))  5.39 us
    ppermute x1, waiting for transfers between devices, per_device(): lax.ppermute(result, 'cols', [(j, i) for i, j in far_pairs(chip_count, st...  3.34 us
    ppermute x1, starting transfers between devices, per_device(): row_a = lax.ppermute(row_a, 'rows', near_pairs(row_count, 0))  3.13 us
    ppermute x4, starting transfers between devices, per_device(): keys[step] = [block, lax.ppermute(block, 'cols', partners)]  2.86 us
    ppermute x1, waiting for transfers between devices, per_device(): row_a = lax.ppermute(row_a, 'rows', near_pairs(row_count, 0))  1.67 us
    ppermute x1, starting transfers between devices, per_device(): lax.ppermute(result, 'cols', [(j, i) for i, j in far_pairs(chip_count, st...  1.55 us
  transfers between devices with their start and end apart: 13, of which 4 were waited for; matrix products, arithmetic and copies ran while one was open for 0% of the time, Pallas kernels for 7%

profile of v3, /device:TPU:0, one launch (start us, length us, event | category | flops | bytes accessed | tf_op | source)
XLA Modules:
  0.0 35.2 jit_solution(2130950299127754187)
XLA Ops:
  0.0 0.0 copy-start.1
  0.0 0.0 copy-start.2
  0.0 0.0 copy-start.13
  0.0 0.0 copy-start.12
  0.0 0.0 copy-start
  0.0 0.0 copy-start.11
  0.0 0.0 copy-start.7
  0.0 1.0 %edge_rows.1 = (bf16[3,32,384]{2,1,0:T(8,128)(2,1)S(1)}, bf16[3,32,384]{2,1,0:T(8,128)(2,1)S(1)}) custom-call(bf16[1,2,4,32,384]{4,3,2,1,0:T(8,128)(2,1)} %cache.5, bf16[1,4,32,384]{3,2,1,0:T(8,128)(2,1)} %hidden.5), custom_call_target="tpu_custom_call" | custom-call | flops 10000000000 | bytes 10000000 | tf_op jit(solution)/shard_map/edge_rows/pallas_call | solution.py:296
  1.0 0.0 copy-start.3
  1.1 0.0 copy-start.4
  1.1 0.0 copy-start.8
  1.1 0.0 copy-start.5
  1.1 0.0 copy-start.6
  1.1 0.0 copy-start.9
  1.1 0.0 copy-start.10
  1.1 3.1 %collective-permute-start = (bf16[3,32,384]{2,1,0:T(8,128)(2,1)S(1)}, bf16[3,32,384]{2,1,0:T(8,128)(2,1)S(1)}, u32[]{:S(2)}, u32[]{:S(2)}) collective-permute-start(bf16[3,32,384]{2,1,0:T(8,128)(2,1)S(1)} %get-tuple-element.16), channel_id=1, source_target_pairs={{0,4},{4,0},{8,12},{12,8},{1,5},{5,1},{9,13},{13,9},{2,6},{6,2},{1... | collective-permute-start | bytes 221192 | tf_op jit(solution)/shard_map/ppermute | solution.py:306
  4.3 0.7 %collective-permute-start.1 = (bf16[3,32,384]{2,1,0:T(8,128)(2,1)S(1)}, bf16[3,32,384]{2,1,0:T(8,128)(2,1)S(1)}, u32[]{:S(2)}, u32[]{:S(2)}) collective-permute-start(bf16[3,32,384]{2,1,0:T(8,128)(2,1)S(1)} %get-tuple-element.17), channel_id=1, source_target_pairs={{4,8},{8,4},{5,9},{9,5},{6,10},{10,6},{7,11},{11,7},{20,24},{24,20... | collective-permute-start | bytes 221192 | tf_op jit(solution)/shard_map/ppermute | solution.py:307
  4.9 1.7 %collective-permute-done.row_a = bf16[3,32,384]{2,1,0:T(8,128)(2,1)S(1)} collective-permute-done((bf16[3,32,384]{2,1,0:T(8,128)(2,1)S(1)}, bf16[3,32,384]{2,1,0:T(8,128)(2,1)S(1)}, u32[]{:S(2)}, u32[]{:S(2)}) %collective-permute-start) | collective-permute-done | bytes 73760 | tf_op jit(solution)/shard_map/ppermute | solution.py:306
  6.6 0.0 collective-permute-done.1.row_b
  6.6 0.0 copy-done.1
  6.6 0.0 copy-done.2
  6.6 0.1 shard_map.136
  6.7 0.1 collective-permute-start.2
  6.8 0.7 %collective-permute-start.3 = (bf16[18,384]{1,0:T(8,128)(2,1)S(1)}, bf16[18,384]{1,0:T(8,128)(2,1)S(1)}, u32[]{:S(2)}, u32[]{:S(2)}) collective-permute-start(bf16[18,384]{1,0:T(8,128)(2,1)S(1)} %get-tuple-element.19), channel_id=1, source_target_pairs={{1,2},{2,1},{5,6},{6,5},{9,10},{10,9},{13,14},{14,13},{17,18},{18,... | collective-permute-start | bytes 41480 | tf_op jit(solution)/shard_map/ppermute | solution.py:318
  7.5 0.5 %collective-permute-done.2.col_a = bf16[18,384]{1,0:T(8,128)(2,1)S(1)} collective-permute-done((bf16[18,384]{1,0:T(8,128)(2,1)S(1)}, bf16[18,384]{1,0:T(8,128)(2,1)S(1)}, u32[]{:S(2)}, u32[]{:S(2)}) %collective-permute-start.2) | collective-permute-done | bytes 13856 | tf_op jit(solution)/shard_map/ppermute | solution.py:317
  8.0 0.0 collective-permute-done.3.col_b
  8.0 0.0 copy-done.13
  8.0 0.0 copy-done.12
  8.0 0.0 copy-done
  8.0 0.0 copy-done.11
  8.0 0.0 copy-done.7
  8.0 1.9 %shard_map.137 = (bf16[128,384]{1,0:T(8,128)(2,1)S(1)}, bf16[128,384]{1,0:T(8,128)(2,1)S(1)}) custom-call(bf16[1,2,4,32,384]{4,3,2,1,0:T(8,128)(2,1)S(1)} %copy-done.1, bf16[1,4,32,384]{3,2,1,0:T(8,128)(2,1)S(1)} %copy-done.2, bf16[128,384]{1,0:T(8,128)(2,1)S(1)} %bitcast.2, bf16[3,32,384]{2,1,0:T(8,128)(2,1)S(1)} %collective-permute-done.row_a, ...), custom_call_target="tpu_custom_call" | custom-call | tf_op jit(solution)/shard_map/pallas_call | solution.py:263
  9.9 4.1 %collective-permute-start.6 = (bf16[128,384]{1,0:T(8,128)(2,1)S(1)}, bf16[128,384]{1,0:T(8,128)(2,1)S(1)}, u32[]{:S(2)}, u32[]{:S(2)}) collective-permute-start(bf16[128,384]{1,0:T(8,128)(2,1)S(1)} %get-tuple-element.20.refs_0_.refs_1_), channel_id=1, source_target_pairs={{0,12},{4,8},{8,4},{12,0},{1,13},{5,9},{9,5},{13,1},{2,14},{6,10},... | collective-permute-start | bytes 294920 | tf_op jit(solution)/shard_map/ppermute | solution.py:342
  14.1 2.6 %collective-permute-start.10 = (bf16[128,384]{1,0:T(8,128)(2,1)S(1)}, bf16[128,384]{1,0:T(8,128)(2,1)S(1)}, u32[]{:S(2)}, u32[]{:S(2)}) collective-permute-start(bf16[128,384]{1,0:T(8,128)(2,1)S(1)} %get-tuple-element.20.refs_0_.refs_1_), channel_id=1, source_target_pairs={{0,8},{4,12},{8,0},{12,4},{1,9},{5,13},{9,1},{13,5},{2,10},{6,14},... | collective-permute-start | bytes 294920 | tf_op jit(solution)/shard_map/ppermute | solution.py:342
  16.7 0.5 %collective-permute-start.8 = (bf16[128,384]{1,0:T(8,128)(2,1)S(1)}, bf16[128,384]{1,0:T(8,128)(2,1)S(1)}, u32[]{:S(2)}, u32[]{:S(2)}) collective-permute-start(bf16[128,384]{1,0:T(8,128)(2,1)S(1)} %get-tuple-element.20.refs_0_.refs_1_), channel_id=1, source_target_pairs={{0,4},{4,0},{8,12},{12,8},{1,5},{5,1},{9,13},{13,9},{2,6},{6,2},{1... | collective-permute-start | bytes 294920 | tf_op jit(solution)/shard_map/ppermute | solution.py:342
  17.2 5.4 %collective-permute-start.4 = (bf16[128,384]{1,0:T(8,128)(2,1)S(1)}, bf16[128,384]{1,0:T(8,128)(2,1)S(1)}, u32[]{:S(2)}, u32[]{:S(2)}) collective-permute-start(bf16[128,384]{1,0:T(8,128)(2,1)S(1)} %get-tuple-element.20.refs_0_.refs_1_), channel_id=1, source_target_pairs={{0,2},{1,3},{2,0},{3,1},{4,6},{5,7},{6,4},{7,5},{8,10},{9,11},{10,... | collective-permute-start | bytes 294920 | tf_op jit(solution)/shard_map/ppermute | solution.py:345
  22.6 0.0 collective-permute-start.5
  22.6 0.0 collective-permute-done.6.refs_3_
  22.6 0.5 %collective-permute-start.7 = (bf16[128,384]{1,0:T(8,128)(2,1)S(1)}, bf16[128,384]{1,0:T(8,128)(2,1)S(1)}, u32[]{:S(2)}, u32[]{:S(2)}) collective-permute-start(bf16[128,384]{1,0:T(8,128)(2,1)S(1)} %collective-permute-done.6.refs_3_), channel_id=1, source_target_pairs={{0,1},{1,0},{2,3},{3,2},{4,5},{5,4},{6,7},{7,6},{8,9},{9,8},{10,11... | collective-permute-start | bytes 294920 | tf_op jit(solution)/shard_map/ppermute | solution.py:348
  23.1 0.0 collective-permute-done.10.refs_6_
  23.1 2.3 %collective-permute-start.11 = (bf16[128,384]{1,0:T(8,128)(2,1)S(1)}, bf16[128,384]{1,0:T(8,128)(2,1)S(1)}, u32[]{:S(2)}, u32[]{:S(2)}) collective-permute-start(bf16[128,384]{1,0:T(8,128)(2,1)S(1)} %collective-permute-done.10.refs_6_), channel_id=1, source_target_pairs={{0,1},{1,0},{2,3},{3,2},{4,5},{5,4},{6,7},{7,6},{8,9},{9,8},{10,11... | collective-permute-start | bytes 294920 | tf_op jit(solution)/shard_map/ppermute | solution.py:348
  25.4 0.0 collective-permute-done.8.refs_4_
  25.4 0.1 collective-permute-start.9
  25.4 0.3 collective-permute-done.4.refs_1_
  25.7 0.0 copy-done.3
  25.7 0.0 copy-done.4
  25.7 0.0 copy-done.8
  25.7 0.6 %shard_map.138.refs_0_ = bf16[256,384]{1,0:T(8,128)(2,1)S(1)} custom-call(bf16[128,384]{1,0:T(8,128)(2,1)S(1)} %get-tuple-element.20.refs_0_.refs_1_, bf16[128,384]{1,0:T(8,128)(2,1)S(1)} %collective-permute-done.4.refs_1_, bf16[384,384]{1,0:T(8,128)(2,1)S(1)} %copy-done.3, f32[384]{0:T(512)S(1)} %copy-done.8, bf16[384,384]{1,0:T(8,128)(2,1)S(1)} %copy-done.4), custom_call_target="tpu_custom_call" | custom-call | tf_op jit(solution)/shard_map/pallas_call | solution.py:263
  26.4 0.0 collective-permute-done.5.refs_2_
  26.4 0.0 collective-permute-done.7.refs_4_
  26.4 1.1 %shard_map.139 = (f32[256,128]{1,0:T(8,128)S(1)}, f32[256,128]{1,0:T(8,128)S(1)}, f32[256,384]{1,0:T(8,128)S(1)}) custom-call(bf16[256,384]{1,0:T(8,128)(2,1)S(1)} %shard_map.138.refs_0_, bf16[128,384]{1,0:T(8,128)(2,1)S(1)} %get-tuple-element.20.refs_0_.refs_1_, bf16[128,384]{1,0:T(8,128)(2,1)S(1)} %collective-permute-done.5.refs_2_, ...), custom_call_target="tpu_custom_call" | custom-call | tf_op jit(solution)/shard_map/pallas_call | solution.py:263
  27.5 0.0 collective-permute-done.11.refs_7_
  27.5 0.0 collective-permute-done.9.refs_5_
  27.5 0.8 %shard_map.141 = bf16[128,512]{1,0:T(8,128)(2,1)S(1)} custom-call(bf16[256,384]{1,0:T(8,128)(2,1)S(1)} %shard_map.138.refs_0_, f32[256,128]{1,0:T(8,128)S(1)} %get-tuple-element.21.refs_1_, f32[256,128]{1,0:T(8,128)S(1)} %get-tuple-element.22.refs_2_, f32[256,384]{1,0:T(8,128)S(1)} %get-tuple-element.23.refs_3_, ...), custom_call_target="tpu_custom_call" | custom-call | tf_op jit(solution)/shard_map/pallas_call | solution.py:263
  28.3 1.5 %collective-permute-start.12 = (bf16[128,512]{1,0:T(8,128)(2,1)S(1)}, bf16[128,512]{1,0:T(8,128)(2,1)S(1)}, u32[]{:S(2)}, u32[]{:S(2)}) collective-permute-start(bf16[128,512]{1,0:T(8,128)(2,1)S(1)} %shard_map.141), channel_id=1, source_target_pairs={{2,0},{3,1},{0,2},{1,3},{6,4},{7,5},{4,6},{5,7},{10,8},{11,9},{8,1... | collective-permute-start | bytes 393224 | tf_op jit(solution)/shard_map/ppermute | solution.py:379
  29.8 0.8 %shard_map.140 = (f32[128,384]{1,0:T(8,128)S(1)}, f32[128,128]{1,0:T(8,128)S(1)}) custom-call(bf16[256,384]{1,0:T(8,128)(2,1)S(1)} %shard_map.138.refs_0_, f32[256,128]{1,0:T(8,128)S(1)} %get-tuple-element.21.refs_1_, f32[256,128]{1,0:T(8,128)S(1)} %get-tuple-element.22.refs_2_, f32[256,384]{1,0:T(8,128)S(1)} %get-tuple-element.23.refs_3_, ...), custom_call_target="tpu_custom_call" | custom-call | tf_op jit(solution)/shard_map/pallas_call | solution.py:263
  30.6 3.3 %collective-permute-done.12.refs_2_ = bf16[128,512]{1,0:T(8,128)(2,1)S(1)} collective-permute-done((bf16[128,512]{1,0:T(8,128)(2,1)S(1)}, bf16[128,512]{1,0:T(8,128)(2,1)S(1)}, u32[]{:S(2)}, u32[]{:S(2)}) %collective-permute-start.12) | collective-permute-done | bytes 131104 | tf_op jit(solution)/shard_map/ppermute | solution.py:379
  34.0 0.0 copy-done.5
  34.0 0.0 copy-done.6
  34.0 0.0 copy-done.9
  34.0 0.0 copy-done.10
  34.0 1.2 %shard_map.142 = bf16[128,384]{1,0:T(8,128)(2,1)} custom-call(f32[128,384]{1,0:T(8,128)S(1)} %get-tuple-element.24.refs_0_, f32[128,128]{1,0:T(8,128)S(1)} %get-tuple-element.25.refs_1_, bf16[128,512]{1,0:T(8,128)(2,1)S(1)} %collective-permute-done.12.refs_2_, bf16[128,384]{1,0:T(8,128)(2,1)S(1)} %get-tuple-element.26.refs_3_, ...), custom_call_target="tpu_custom_call" | custom-call | tf_op jit(solution)/shard_map/pallas_call | solution.py:263
Async XLA Ops:
  0.0 6.6 %copy-start.1 = (bf16[1,2,4,32,384]{4,3,2,1,0:T(8,128)(2,1)S(1)}, bf16[1,2,4,32,384]{4,3,2,1,0:T(8,128)(2,1)}, u32[]{:S(2)}) copy-start(bf16[1,2,4,32,384]{4,3,2,1,0:T(8,128)(2,1)} %cache.5) | copy-start | bytes 589828
  0.0 6.6 %copy-start.2 = (bf16[1,4,32,384]{3,2,1,0:T(8,128)(2,1)S(1)}, bf16[1,4,32,384]{3,2,1,0:T(8,128)(2,1)}, u32[]{:S(2)}) copy-start(bf16[1,4,32,384]{3,2,1,0:T(8,128)(2,1)} %hidden.5) | copy-start | bytes 294916
  0.0 8.0 %copy-start.13 = (f32[384]{0:T(512)S(1)}, f32[384]{0:T(512)}, u32[]{:S(2)}) copy-start(f32[384]{0:T(512)} %gain_two.1) | copy-start | bytes 4612
  0.0 8.0 %copy-start.12 = (f32[384]{0:T(512)S(1)}, f32[384]{0:T(512)}, u32[]{:S(2)}) copy-start(f32[384]{0:T(512)} %conv_bias.1) | copy-start | bytes 4612
  0.0 8.0 %copy-start = (bf16[3,3,3,384,384]{4,3,2,1,0:T(8,128)(2,1)S(1)}, bf16[3,3,3,384,384]{4,3,2,1,0:T(8,128)(2,1)}, u32[]{:S(2)}) copy-start(bf16[3,3,3,384,384]{4,3,2,1,0:T(8,128)(2,1)} %weight.1) | copy-start | bytes 23887876
  0.0 8.0 %copy-start.11 = (f32[384]{0:T(512)S(1)}, f32[384]{0:T(512)}, u32[]{:S(2)}) copy-start(f32[384]{0:T(512)} %gain_one.1) | copy-start | bytes 4612
  0.0 8.0 %copy-start.7 = (bf16[1,4,32,384]{3,2,1,0:T(8,128)(2,1)S(1)}, bf16[1,4,32,384]{3,2,1,0:T(8,128)(2,1)}, u32[]{:S(2)}) copy-start(bf16[1,4,32,384]{3,2,1,0:T(8,128)(2,1)} %param.16) | copy-start | bytes 294916
  1.0 24.7 %copy-start.3 = (bf16[384,384]{1,0:T(8,128)(2,1)S(1)}, bf16[384,384]{1,0:T(8,128)(2,1)}, u32[]{:S(2)}) copy-start(bf16[384,384]{1,0:T(8,128)(2,1)} %refs_2_.1) | copy-start | bytes 884740
  1.1 24.7 %copy-start.4 = (bf16[384,384]{1,0:T(8,128)(2,1)S(1)}, bf16[384,384]{1,0:T(8,128)(2,1)}, u32[]{:S(2)}) copy-start(bf16[384,384]{1,0:T(8,128)(2,1)} %refs_4_.2) | copy-start | bytes 884740
  1.1 24.6 %copy-start.8 = (f32[384]{0:T(512)S(1)}, f32[384]{0:T(512)}, u32[]{:S(2)}) copy-start(f32[384]{0:T(512)} %refs_3_.1) | copy-start | bytes 4612
  1.1 32.9 %copy-start.5 = (bf16[384,384]{1,0:T(8,128)(2,1)S(1)}, bf16[384,384]{1,0:T(8,128)(2,1)}, u32[]{:S(2)}) copy-start(bf16[384,384]{1,0:T(8,128)(2,1)} %refs_4_.3) | copy-start | bytes 884740
  1.1 32.9 %copy-start.6 = (bf16[384,384]{1,0:T(8,128)(2,1)S(1)}, bf16[384,384]{1,0:T(8,128)(2,1)}, u32[]{:S(2)}) copy-start(bf16[384,384]{1,0:T(8,128)(2,1)} %refs_6_.1) | copy-start | bytes 884740
  1.1 32.9 %copy-start.9 = (f32[384]{0:T(512)S(1)}, f32[384]{0:T(512)}, u32[]{:S(2)}) copy-start(f32[384]{0:T(512)} %refs_5_.1) | copy-start | bytes 4612
  1.1 32.9 %copy-start.10 = (f32[384]{0:T(512)S(1)}, f32[384]{0:T(512)}, u32[]{:S(2)}) copy-start(f32[384]{0:T(512)} %refs_7_.1) | copy-start | bytes 4612
  1.1 5.5 %collective-permute-start = (bf16[3,32,384]{2,1,0:T(8,128)(2,1)S(1)}, bf16[3,32,384]{2,1,0:T(8,128)(2,1)S(1)}, u32[]{:S(2)}, u32[]{:S(2)}) collective-permute-start(bf16[3,32,384]{2,1,0:T(8,128)(2,1)S(1)} %get-tuple-element.16), channel_id=1, source_target_pairs={{0,4},{4,0},{8,12},{12,8},{1,5},{5,1},{9,13},{13,9},{2,6},{6,2},{1... | collective-permute-start | bytes 221192 | tf_op jit(solution)/shard_map/ppermute | solution.py:306
  4.3 2.3 %collective-permute-start.1 = (bf16[3,32,384]{2,1,0:T(8,128)(2,1)S(1)}, bf16[3,32,384]{2,1,0:T(8,128)(2,1)S(1)}, u32[]{:S(2)}, u32[]{:S(2)}) collective-permute-start(bf16[3,32,384]{2,1,0:T(8,128)(2,1)S(1)} %get-tuple-element.17), channel_id=1, source_target_pairs={{4,8},{8,4},{5,9},{9,5},{6,10},{10,6},{7,11},{11,7},{20,24},{24,20... | collective-permute-start | bytes 221192 | tf_op jit(solution)/shard_map/ppermute | solution.py:307
  6.7 1.3 %collective-permute-start.2 = (bf16[18,384]{1,0:T(8,128)(2,1)S(1)}, bf16[18,384]{1,0:T(8,128)(2,1)S(1)}, u32[]{:S(2)}, u32[]{:S(2)}) collective-permute-start(bf16[18,384]{1,0:T(8,128)(2,1)S(1)} %get-tuple-element.18), channel_id=1, source_target_pairs={{0,1},{1,0},{2,3},{3,2},{4,5},{5,4},{6,7},{7,6},{8,9},{9,8},{10,11... | collective-permute-start | bytes 41480 | tf_op jit(solution)/shard_map/ppermute | solution.py:317
  6.8 1.2 %collective-permute-start.3 = (bf16[18,384]{1,0:T(8,128)(2,1)S(1)}, bf16[18,384]{1,0:T(8,128)(2,1)S(1)}, u32[]{:S(2)}, u32[]{:S(2)}) collective-permute-start(bf16[18,384]{1,0:T(8,128)(2,1)S(1)} %get-tuple-element.19), channel_id=1, source_target_pairs={{1,2},{2,1},{5,6},{6,5},{9,10},{10,9},{13,14},{14,13},{17,18},{18,... | collective-permute-start | bytes 41480 | tf_op jit(solution)/shard_map/ppermute | solution.py:318
  9.9 12.6 %collective-permute-start.6 = (bf16[128,384]{1,0:T(8,128)(2,1)S(1)}, bf16[128,384]{1,0:T(8,128)(2,1)S(1)}, u32[]{:S(2)}, u32[]{:S(2)}) collective-permute-start(bf16[128,384]{1,0:T(8,128)(2,1)S(1)} %get-tuple-element.20.refs_0_.refs_1_), channel_id=1, source_target_pairs={{0,12},{4,8},{8,4},{12,0},{1,13},{5,9},{9,5},{13,1},{2,14},{6,10},... | collective-permute-start | bytes 294920 | tf_op jit(solution)/shard_map/ppermute | solution.py:342
  14.1 9.0 %collective-permute-start.10 = (bf16[128,384]{1,0:T(8,128)(2,1)S(1)}, bf16[128,384]{1,0:T(8,128)(2,1)S(1)}, u32[]{:S(2)}, u32[]{:S(2)}) collective-permute-start(bf16[128,384]{1,0:T(8,128)(2,1)S(1)} %get-tuple-element.20.refs_0_.refs_1_), channel_id=1, source_target_pairs={{0,8},{4,12},{8,0},{12,4},{1,9},{5,13},{9,1},{13,5},{2,10},{6,14},... | collective-permute-start | bytes 294920 | tf_op jit(solution)/shard_map/ppermute | solution.py:342
  16.7 8.7 %collective-permute-start.8 = (bf16[128,384]{1,0:T(8,128)(2,1)S(1)}, bf16[128,384]{1,0:T(8,128)(2,1)S(1)}, u32[]{:S(2)}, u32[]{:S(2)}) collective-permute-start(bf16[128,384]{1,0:T(8,128)(2,1)S(1)} %get-tuple-element.20.refs_0_.refs_1_), channel_id=1, source_target_pairs={{0,4},{4,0},{8,12},{12,8},{1,5},{5,1},{9,13},{13,9},{2,6},{6,2},{1... | collective-permute-start | bytes 294920 | tf_op jit(solution)/shard_map/ppermute | solution.py:342
  17.2 8.5 %collective-permute-start.4 = (bf16[128,384]{1,0:T(8,128)(2,1)S(1)}, bf16[128,384]{1,0:T(8,128)(2,1)S(1)}, u32[]{:S(2)}, u32[]{:S(2)}) collective-permute-start(bf16[128,384]{1,0:T(8,128)(2,1)S(1)} %get-tuple-element.20.refs_0_.refs_1_), channel_id=1, source_target_pairs={{0,2},{1,3},{2,0},{3,1},{4,6},{5,7},{6,4},{7,5},{8,10},{9,11},{10,... | collective-permute-start | bytes 294920 | tf_op jit(solution)/shard_map/ppermute | solution.py:345
  22.6 3.8 %collective-permute-start.5 = (bf16[128,384]{1,0:T(8,128)(2,1)S(1)}, bf16[128,384]{1,0:T(8,128)(2,1)S(1)}, u32[]{:S(2)}, u32[]{:S(2)}) collective-permute-start(bf16[128,384]{1,0:T(8,128)(2,1)S(1)} %get-tuple-element.20.refs_0_.refs_1_), channel_id=1, source_target_pairs={{0,1},{1,0},{2,3},{3,2},{4,5},{5,4},{6,7},{7,6},{8,9},{9,8},{10,11... | collective-permute-start | bytes 294920 | tf_op jit(solution)/shard_map/ppermute | solution.py:348
  22.6 3.8 %collective-permute-start.7 = (bf16[128,384]{1,0:T(8,128)(2,1)S(1)}, bf16[128,384]{1,0:T(8,128)(2,1)S(1)}, u32[]{:S(2)}, u32[]{:S(2)}) collective-permute-start(bf16[128,384]{1,0:T(8,128)(2,1)S(1)} %collective-permute-done.6.refs_3_), channel_id=1, source_target_pairs={{0,1},{1,0},{2,3},{3,2},{4,5},{5,4},{6,7},{7,6},{8,9},{9,8},{10,11... | collective-permute-start | bytes 294920 | tf_op jit(solution)/shard_map/ppermute | solution.py:348
  23.1 4.4 %collective-permute-start.11 = (bf16[128,384]{1,0:T(8,128)(2,1)S(1)}, bf16[128,384]{1,0:T(8,128)(2,1)S(1)}, u32[]{:S(2)}, u32[]{:S(2)}) collective-permute-start(bf16[128,384]{1,0:T(8,128)(2,1)S(1)} %collective-permute-done.10.refs_6_), channel_id=1, source_target_pairs={{0,1},{1,0},{2,3},{3,2},{4,5},{5,4},{6,7},{7,6},{8,9},{9,8},{10,11... | collective-permute-start | bytes 294920 | tf_op jit(solution)/shard_map/ppermute | solution.py:348
  25.4 2.2 %collective-permute-start.9 = (bf16[128,384]{1,0:T(8,128)(2,1)S(1)}, bf16[128,384]{1,0:T(8,128)(2,1)S(1)}, u32[]{:S(2)}, u32[]{:S(2)}) collective-permute-start(bf16[128,384]{1,0:T(8,128)(2,1)S(1)} %collective-permute-done.8.refs_4_), channel_id=1, source_target_pairs={{0,1},{1,0},{2,3},{3,2},{4,5},{5,4},{6,7},{7,6},{8,9},{9,8},{10,11... | collective-permute-start | bytes 294920 | tf_op jit(solution)/shard_map/ppermute | solution.py:348
  28.3 5.6 %collective-permute-start.12 = (bf16[128,512]{1,0:T(8,128)(2,1)S(1)}, bf16[128,512]{1,0:T(8,128)(2,1)S(1)}, u32[]{:S(2)}, u32[]{:S(2)}) collective-permute-start(bf16[128,512]{1,0:T(8,128)(2,1)S(1)} %shard_map.141), channel_id=1, source_target_pairs={{2,0},{3,1},{0,2},{1,3},{6,4},{7,5},{4,6},{5,7},{10,8},{11,9},{8,1... | collective-permute-start | bytes 393224 | tf_op jit(solution)/shard_map/ppermute | solution.py:379

commit v4 on v3

--- a/solution.py
+++ b/solution.py
@@ -63,9 +63,12 @@
         copy.wait()
 
 
-def cols_kernel(tile_rows, tile_cols, cache, hidden, row_a, row_b, col_a, col_b):
+def cols_kernel(
+    tile_rows, tile_cols, cache, hidden, row_a, row_b, gain_one, weight, inner, outer
+):
     row_even = lax.rem(lax.axis_index("rows"), 2) == 0
-    col_even = lax.rem(lax.axis_index("cols"), 2) == 0
+    col_odd = lax.rem(lax.axis_index("cols"), 2)
+    col_even = col_odd == 0
     first, last = pl.ds(0, 1), pl.ds(tile_cols - 1, 1)
     near, far = [], []
 
@@ -79,8 +82,20 @@
         for r in range(tile_rows):
             add(lambda at: cache[0, f, r, at] if f < 2 else hidden[0, r, at])
         add(lambda at: jnp.where(row_even, row_a[f, at].astype(f32), row_b[f, at].astype(f32)))
-    col_a[...] = jnp.concatenate(near, axis=0).astype(bf16)
-    col_b[...] = jnp.concatenate(far, axis=0).astype(bf16)
+    inner[...] = jnp.concatenate(near, axis=0).astype(bf16)
+    reach = tile_rows + 2
+    side = 2 - 2 * col_odd
+    total = jnp.zeros((outer.shape[0], far[0].shape[1]), f32)
+    spare = [jnp.zeros_like(far[0])] * (outer.shape[0] - tile_rows)
+    for f in range(3):
+        rows = far[f * reach : (f + 1) * reach]
+        if f == 2:
+            live = activate(jnp.concatenate(rows, axis=0), line(gain_one))
+            rows = [live[r : r + 1] for r in range(reach)]
+        for a in range(3):
+            taken = jnp.concatenate(rows[a : a + tile_rows] + spare, axis=0).astype(bf16)
+            total += jnp.dot(taken, weight[f, a, side], preferred_element_type=f32)
+    outer[...] = total
 
 
 def conv_kernel(
@@ -89,34 +104,26 @@
     channels,
     cache,
     hidden,
-    shortcut,
     row_a,
     row_b,
-    col_a,
-    col_b,
+    inner,
     gain_one,
-    conv_bias,
-    gain_two,
     weight,
-    normed,
-    mixed,
+    convolved,
     stack,
 ):
     row_even = lax.rem(lax.axis_index("rows"), 2) == 0
     col_even = lax.rem(lax.axis_index("cols"), 2) == 0
     place = lax.broadcasted_iota(jnp.int32, (tile_cols, channels), 0)
     reach = tile_rows + 2
-    first = col_a[...].astype(f32)
-    second = col_b[...].astype(f32)
-    left_all = jnp.where(col_even, second, first)
-    right_all = jnp.where(col_even, first, second)
+    beside = inner[...].astype(f32)
     gain = line(gain_one)
     for f in range(3):
-        left_rows = left_all[f * reach : (f + 1) * reach]
-        right_rows = right_all[f * reach : (f + 1) * reach]
+        side_rows = beside[f * reach : (f + 1) * reach]
         if f == 2:
-            left_rows = activate(left_rows, gain)
-            right_rows = activate(right_rows, gain)
+            side_rows = activate(side_rows, gain)
+        left_rows = jnp.where(col_even, 0.0, side_rows)
+        right_rows = jnp.where(col_even, side_rows, 0.0)
         for r in range(reach):
             if r == 0 or r == reach - 1:
                 one, two = row_a[f].astype(f32), row_b[f].astype(f32)
@@ -143,11 +150,23 @@
                 weight[f, a].reshape(3 * channels, channels),
                 preferred_element_type=f32,
             )
-    convolved = total + line(conv_bias)
-    residual = shortcut[...].astype(f32)
-    kept = (residual + convolved).astype(bf16)
-    mixed[...] = kept
-    normed[...] = normalize(kept.astype(f32), line(gain_two)).astype(bf16)
+    convolved[...] = total
+
+
+def mix_kernel(
+    tile_rows, tile_cols, convolved, outer, shortcut, conv_bias, gain_two, normed, mixed
+):
+    col_even = lax.rem(lax.axis_index("cols"), 2) == 0
+    channels = shortcut.shape[-1]
+    edge = jnp.where(col_even, 0, tile_cols - 1)
+    place = lax.broadcasted_iota(jnp.int32, (tile_cols, channels), 0)
+    bias, gain = line(conv_bias), line(gain_two)
+    for r in range(tile_rows):
+        rows = pl.ds(r * tile_cols, tile_cols)
+        total = convolved[rows, :] + jnp.where(place == edge, outer[r : r + 1, :], 0.0)
+        kept = (shortcut[0, r].astype(f32) + (total + bias)).astype(bf16)
+        mixed[rows, :] = kept
+        normed[rows, :] = normalize(kept.astype(f32), gain).astype(bf16)
 
 
 def query_kernel(score_scale, parts, *refs):
@@ -305,35 +324,43 @@
     )(*[pltpu.with_memory_space_constraint(v, pltpu.HBM) for v in (frame_cache, hidden)])
     row_a = lax.ppermute(row_a, "rows", near_pairs(row_count, 0))
     row_b = lax.ppermute(row_b, "rows", near_pairs(row_count, 1))
-    edge_cols = pltpu.VMEM((3 * (tile_rows + 2), channels), bf16)
-    col_a, col_b = call(
+    inner, outer = call(
         functools.partial(cols_kernel, tile_rows, tile_cols),
-        (edge_cols, edge_cols),
+        (
+            pltpu.VMEM((3 * (tile_rows + 2), channels), bf16),
+            pltpu.VMEM((-(-tile_rows // 8) * 8, channels), f32),
+        ),
         frame_cache,
         hidden,
         row_a,
         row_b,
-    )
-    col_a = lax.ppermute(col_a, "cols", near_pairs(col_count, 0))
-    col_b = lax.ppermute(col_b, "cols", near_pairs(col_count, 1))
-
-    normed, mixed = call(
+        gain_one,
+        conv_weight,
+    )
+    inner = lax.ppermute(inner, "cols", near_pairs(col_count, 0))
+    outer = lax.ppermute(outer, "cols", near_pairs(col_count, 1))
+    convolved = call(
         functools.partial(conv_kernel, tile_rows, tile_cols, channels),
-        (wide, wide),
+        pltpu.VMEM((tile, channels), f32),
         frame_cache,
         hidden,
-        shortcut.reshape(tile, channels),
         row_a,
         row_b,
-        col_a,
-        col_b,
+        inner,
         gain_one,
-        conv_bias,
-        gain_two,
         conv_weight,
         scratch_shapes=[
             pltpu.VMEM((3, (tile_rows + 2) * tile_cols, 3 * channels), bf16),
         ],
+    )
+    normed, mixed = call(
+        functools.partial(mix_kernel, tile_rows, tile_cols),
+        (wide, wide),
+        convolved,
+        outer,
+        shortcut,
+        conv_bias,
+        gain_two,
     )
 
     partners = near_pairs(col_count, 0)

time: 35.3 us -> 35.2 us (level)
  waiting for transfers between devices: 5.8 us -> 4.8 us
  Pallas kernels: 7.53 us -> 7.97 us
    ppermute x1, starting transfers between devices: 5.39 us -> 3.64 us  [per_device(): lax.ppermute(normed, 'cols', far_pairs(chip_count, step, 2))]
    ppermute x1, starting transfers between devices: 1.55 us -> 2.49 us  [per_device(): lax.ppermute(result, 'cols', [(j, i) for i, j in far_pairs(chip_count, st...]
    ppermute x4, starting transfers between devices: 2.86 us -> 3.72 us  [per_device(): keys[step] = [block, lax.ppermute(block, 'cols', partners)]]
    ppermute x1, waiting for transfers between devices: 3.34 us -> 2.91 us  [per_device(): lax.ppermute(result, 'cols', [(j, i) for i, j in far_pairs(chip_count, st...]
    pallas_call x7 -> x8, Pallas kernels: 6.53 us -> 6.95 us  [call(): pl.pallas_call(kernel, out_shape=out_shape, in_specs=[VMEM] * len(operand...]
  transfers between devices with their start and end apart: 13 -> 13, of which waited for: 4 -> 3; matrix products, arithmetic and copies ran while one was open for 0% -> 0% of each run, Pallas kernels for 7% -> 12%
where the time goes in v4:
time: 35.2 us; the launch traced here: 35 us
  starting transfers between devices  21.9 us (62%)
  Pallas kernels  7.97 us (23%)
  waiting for transfers between devices  4.8 us (14%)
    ppermute x3, starting transfers between devices, per_device(): arrived[step] = lax.ppermute(normed, 'rows', far_pairs(row_count, step))  7.29 us
    pallas_call x8, Pallas kernels, call(): pl.pallas_call(kernel, out_shape=out_shape, in_specs=[VMEM] * len(operand...  6.95 us
    ppermute x4, starting transfers between devices, per_device(): keys[step] = [block, lax.ppermute(block, 'cols', partners)]  3.72 us
    ppermute x1, starting transfers between devices, per_device(): lax.ppermute(normed, 'cols', far_pairs(chip_count, step, 2))  3.64 us
    ppermute x1, starting transfers between devices, per_device(): row_a = lax.ppermute(row_a, 'rows', near_pairs(row_count, 0))  3.13 us
    ppermute x1, waiting for transfers between devices, per_device(): lax.ppermute(result, 'cols', [(j, i) for i, j in far_pairs(chip_count, st...  2.91 us
    ppermute x1, starting transfers between devices, per_device(): lax.ppermute(result, 'cols', [(j, i) for i, j in far_pairs(chip_count, st...  2.49 us
    ppermute x1, waiting for transfers between devices, per_device(): row_a = lax.ppermute(row_a, 'rows', near_pairs(row_count, 0))  1.49 us
  transfers between devices with their start and end apart: 13, of which 3 were waited for; matrix products, arithmetic and copies ran while one was open for 0% of the time, Pallas kernels for 12%

profile of v4, /device:TPU:0, one launch (start us, length us, event | category | flops | bytes accessed | tf_op | source)
XLA Modules:
  0.0 35.0 jit_solution(652288305639304783)
XLA Ops:
  0.0 0.0 copy-start.1
  0.0 0.0 copy-start.2
  0.0 0.0 copy-start
  0.0 0.0 copy-start.8
  0.0 1.0 %edge_rows.1 = (bf16[3,32,384]{2,1,0:T(8,128)(2,1)S(1)}, bf16[3,32,384]{2,1,0:T(8,128)(2,1)S(1)}) custom-call(bf16[1,2,4,32,384]{4,3,2,1,0:T(8,128)(2,1)} %cache.5, bf16[1,4,32,384]{3,2,1,0:T(8,128)(2,1)} %hidden.5), custom_call_target="tpu_custom_call" | custom-call | flops 10000000000 | bytes 10000000 | tf_op jit(solution)/shard_map/edge_rows/pallas_call | solution.py:315
  1.0 3.1 %collective-permute-start = (bf16[3,32,384]{2,1,0:T(8,128)(2,1)S(1)}, bf16[3,32,384]{2,1,0:T(8,128)(2,1)S(1)}, u32[]{:S(2)}, u32[]{:S(2)}) collective-permute-start(bf16[3,32,384]{2,1,0:T(8,128)(2,1)S(1)} %get-tuple-element.16), channel_id=1, source_target_pairs={{0,4},{4,0},{8,12},{12,8},{1,5},{5,1},{9,13},{13,9},{2,6},{6,2},{1... | collective-permute-start | bytes 221192 | tf_op jit(solution)/shard_map/ppermute | solution.py:325
  4.2 0.0 copy-start.7
  4.2 0.0 copy-start.9
  4.2 0.0 copy-start.10
  4.2 0.0 copy-start.3
  4.2 0.0 copy-start.4
  4.2 0.0 copy-start.11
  4.2 0.8 %collective-permute-start.1 = (bf16[3,32,384]{2,1,0:T(8,128)(2,1)S(1)}, bf16[3,32,384]{2,1,0:T(8,128)(2,1)S(1)}, u32[]{:S(2)}, u32[]{:S(2)}) collective-permute-start(bf16[3,32,384]{2,1,0:T(8,128)(2,1)S(1)} %get-tuple-element.17), channel_id=1, source_target_pairs={{4,8},{8,4},{5,9},{9,5},{6,10},{10,6},{7,11},{11,7},{20,24},{24,20... | collective-permute-start | bytes 221192 | tf_op jit(solution)/shard_map/ppermute | solution.py:326
  5.0 1.5 %collective-permute-done.row_a = bf16[3,32,384]{2,1,0:T(8,128)(2,1)S(1)} collective-permute-done((bf16[3,32,384]{2,1,0:T(8,128)(2,1)S(1)}, bf16[3,32,384]{2,1,0:T(8,128)(2,1)S(1)}, u32[]{:S(2)}, u32[]{:S(2)}) %collective-permute-start) | collective-permute-done | bytes 73760 | tf_op jit(solution)/shard_map/ppermute | solution.py:325
  6.5 0.0 collective-permute-done.1.row_b
  6.5 0.0 copy-done.1
  6.5 0.0 copy-done.2
  6.5 0.0 copy-done
  6.5 0.0 copy-done.8
  6.5 0.5 %shard_map.136 = (bf16[18,384]{1,0:T(8,128)(2,1)S(1)}, f32[8,384]{1,0:T(8,128)S(1)}) custom-call(bf16[1,2,4,32,384]{4,3,2,1,0:T(8,128)(2,1)S(1)} %copy-done.1, bf16[1,4,32,384]{3,2,1,0:T(8,128)(2,1)S(1)} %copy-done.2, bf16[3,32,384]{2,1,0:T(8,128)(2,1)S(1)} %collective-permute-done.row_a, bf16[3,32,384]{2,1,0:T(8,128)(2,1)S(1)} %collective-permute-done.1.row_b, ...), custom_call_target="tpu_custom_call" | custom-call | tf_op jit(solution)/shard_map/pallas_call | solution.py:282
  7.0 0.0 copy-start.5
  7.0 0.0 copy-start.6
  7.1 0.0 copy-start.12
  7.1 0.0 copy-start.13
  7.1 0.1 collective-permute-start.2
  7.2 0.8 %collective-permute-start.3 = (f32[8,384]{1,0:T(8,128)S(1)}, f32[8,384]{1,0:T(8,128)S(1)}, u32[]{:S(2)}, u32[]{:S(2)}) collective-permute-start(f32[8,384]{1,0:T(8,128)S(1)} %get-tuple-element.19), channel_id=1, source_target_pairs={{1,2},{2,1},{5,6},{6,5},{9,10},{10,9},{13,14},{14,13},{17,18},{18,... | collective-permute-start | bytes 36872 | tf_op jit(solution)/shard_map/ppermute | solution.py:341
  8.0 0.4 %collective-permute-done.2.inner = bf16[18,384]{1,0:T(8,128)(2,1)S(1)} collective-permute-done((bf16[18,384]{1,0:T(8,128)(2,1)S(1)}, bf16[18,384]{1,0:T(8,128)(2,1)S(1)}, u32[]{:S(2)}, u32[]{:S(2)}) %collective-permute-start.2) | collective-permute-done | bytes 13856 | tf_op jit(solution)/shard_map/ppermute | solution.py:340
  8.3 1.8 %shard_map.137.convolved = f32[128,384]{1,0:T(8,128)S(1)} custom-call(bf16[1,2,4,32,384]{4,3,2,1,0:T(8,128)(2,1)S(1)} %copy-done.1, bf16[1,4,32,384]{3,2,1,0:T(8,128)(2,1)S(1)} %copy-done.2, bf16[3,32,384]{2,1,0:T(8,128)(2,1)S(1)} %collective-permute-done.row_a, bf16[3,32,384]{2,1,0:T(8,128)(2,1)S(1)} %collective-permute-done.1.row_b, ...), custom_call_target="tpu_custom_call" | custom-call | tf_op jit(solution)/shard_map/pallas_call | solution.py:282
  10.1 0.0 collective-permute-done.3.outer
  10.1 0.0 copy-done.7
  10.1 0.0 copy-done.9
  10.2 0.0 copy-done.10
  10.2 0.2 shard_map.138
  10.3 4.1 %collective-permute-start.6 = (bf16[128,384]{1,0:T(8,128)(2,1)S(1)}, bf16[128,384]{1,0:T(8,128)(2,1)S(1)}, u32[]{:S(2)}, u32[]{:S(2)}) collective-permute-start(bf16[128,384]{1,0:T(8,128)(2,1)S(1)} %get-tuple-element.20.refs_0_.refs_1_), channel_id=1, source_target_pairs={{0,12},{4,8},{8,4},{12,0},{1,13},{5,9},{9,5},{13,1},{2,14},{6,10},... | collective-permute-start | bytes 294920 | tf_op jit(solution)/shard_map/ppermute | solution.py:369
  14.4 2.7 %collective-permute-start.10 = (bf16[128,384]{1,0:T(8,128)(2,1)S(1)}, bf16[128,384]{1,0:T(8,128)(2,1)S(1)}, u32[]{:S(2)}, u32[]{:S(2)}) collective-permute-start(bf16[128,384]{1,0:T(8,128)(2,1)S(1)} %get-tuple-element.20.refs_0_.refs_1_), channel_id=1, source_target_pairs={{0,8},{4,12},{8,0},{12,4},{1,9},{5,13},{9,1},{13,5},{2,10},{6,14},... | collective-permute-start | bytes 294920 | tf_op jit(solution)/shard_map/ppermute | solution.py:369
  17.1 0.5 %collective-permute-start.8 = (bf16[128,384]{1,0:T(8,128)(2,1)S(1)}, bf16[128,384]{1,0:T(8,128)(2,1)S(1)}, u32[]{:S(2)}, u32[]{:S(2)}) collective-permute-start(bf16[128,384]{1,0:T(8,128)(2,1)S(1)} %get-tuple-element.20.refs_0_.refs_1_), channel_id=1, source_target_pairs={{0,4},{4,0},{8,12},{12,8},{1,5},{5,1},{9,13},{13,9},{2,6},{6,2},{1... | collective-permute-start | bytes 294920 | tf_op jit(solution)/shard_map/ppermute | solution.py:369
  17.6 3.6 %collective-permute-start.4 = (bf16[128,384]{1,0:T(8,128)(2,1)S(1)}, bf16[128,384]{1,0:T(8,128)(2,1)S(1)}, u32[]{:S(2)}, u32[]{:S(2)}) collective-permute-start(bf16[128,384]{1,0:T(8,128)(2,1)S(1)} %get-tuple-element.20.refs_0_.refs_1_), channel_id=1, source_target_pairs={{0,2},{1,3},{2,0},{3,1},{4,6},{5,7},{6,4},{7,5},{8,10},{9,11},{10,... | collective-permute-start | bytes 294920 | tf_op jit(solution)/shard_map/ppermute | solution.py:372
  21.3 0.0 collective-permute-start.5
  21.3 0.0 collective-permute-done.6.refs_3_
  21.3 0.5 %collective-permute-start.7 = (bf16[128,384]{1,0:T(8,128)(2,1)S(1)}, bf16[128,384]{1,0:T(8,128)(2,1)S(1)}, u32[]{:S(2)}, u32[]{:S(2)}) collective-permute-start(bf16[128,384]{1,0:T(8,128)(2,1)S(1)} %collective-permute-done.6.refs_3_), channel_id=1, source_target_pairs={{0,1},{1,0},{2,3},{3,2},{4,5},{5,4},{6,7},{7,6},{8,9},{9,8},{10,11... | collective-permute-start | bytes 294920 | tf_op jit(solution)/shard_map/ppermute | solution.py:375
  21.8 0.0 collective-permute-done.10.refs_6_
  21.8 3.2 %collective-permute-start.11 = (bf16[128,384]{1,0:T(8,128)(2,1)S(1)}, bf16[128,384]{1,0:T(8,128)(2,1)S(1)}, u32[]{:S(2)}, u32[]{:S(2)}) collective-permute-start(bf16[128,384]{1,0:T(8,128)(2,1)S(1)} %collective-permute-done.10.refs_6_), channel_id=1, source_target_pairs={{0,1},{1,0},{2,3},{3,2},{4,5},{5,4},{6,7},{7,6},{8,9},{9,8},{10,11... | collective-permute-start | bytes 294920 | tf_op jit(solution)/shard_map/ppermute | solution.py:375
  25.0 0.0 collective-permute-done.8.refs_4_
  25.0 0.0 collective-permute-start.9
  25.0 0.0 collective-permute-done.4.refs_1_
  25.0 0.0 copy-done.3
  25.0 0.0 copy-done.4
  25.0 0.0 copy-done.11
  25.0 0.6 %shard_map.139.refs_0_ = bf16[256,384]{1,0:T(8,128)(2,1)S(1)} custom-call(bf16[128,384]{1,0:T(8,128)(2,1)S(1)} %get-tuple-element.20.refs_0_.refs_1_, bf16[128,384]{1,0:T(8,128)(2,1)S(1)} %collective-permute-done.4.refs_1_, bf16[384,384]{1,0:T(8,128)(2,1)S(1)} %copy-done.3, f32[384]{0:T(512)S(1)} %copy-done.11, bf16[384,384]{1,0:T(8,128)(2,1)S(1)} %copy-done.4), custom_call_target="tpu_custom_call" | custom-call | tf_op jit(solution)/shard_map/pallas_call | solution.py:282
  25.7 0.0 collective-permute-done.5.refs_2_
  25.7 0.0 collective-permute-done.7.refs_4_
  25.7 1.1 %shard_map.140 = (f32[256,128]{1,0:T(8,128)S(1)}, f32[256,128]{1,0:T(8,128)S(1)}, f32[256,384]{1,0:T(8,128)S(1)}) custom-call(bf16[256,384]{1,0:T(8,128)(2,1)S(1)} %shard_map.139.refs_0_, bf16[128,384]{1,0:T(8,128)(2,1)S(1)} %get-tuple-element.20.refs_0_.refs_1_, bf16[128,384]{1,0:T(8,128)(2,1)S(1)} %collective-permute-done.5.refs_2_, ...), custom_call_target="tpu_custom_call" | custom-call | tf_op jit(solution)/shard_map/pallas_call | solution.py:282
  26.8 0.0 collective-permute-done.11.refs_7_
  26.8 0.0 collective-permute-done.9.refs_5_
  26.8 0.8 %shard_map.142 = bf16[128,512]{1,0:T(8,128)(2,1)S(1)} custom-call(bf16[256,384]{1,0:T(8,128)(2,1)S(1)} %shard_map.139.refs_0_, f32[256,128]{1,0:T(8,128)S(1)} %get-tuple-element.21.refs_1_, f32[256,128]{1,0:T(8,128)S(1)} %get-tuple-element.22.refs_2_, f32[256,384]{1,0:T(8,128)S(1)} %get-tuple-element.23.refs_3_, ...), custom_call_target="tpu_custom_call" | custom-call | tf_op jit(solution)/shard_map/pallas_call | solution.py:282
  27.6 2.5 %collective-permute-start.12 = (bf16[128,512]{1,0:T(8,128)(2,1)S(1)}, bf16[128,512]{1,0:T(8,128)(2,1)S(1)}, u32[]{:S(2)}, u32[]{:S(2)}) collective-permute-start(bf16[128,512]{1,0:T(8,128)(2,1)S(1)} %shard_map.142), channel_id=1, source_target_pairs={{2,0},{3,1},{0,2},{1,3},{6,4},{7,5},{4,6},{5,7},{10,8},{11,9},{8,1... | collective-permute-start | bytes 393224 | tf_op jit(solution)/shard_map/ppermute | solution.py:406
  30.1 0.8 %shard_map.141 = (f32[128,384]{1,0:T(8,128)S(1)}, f32[128,128]{1,0:T(8,128)S(1)}) custom-call(bf16[256,384]{1,0:T(8,128)(2,1)S(1)} %shard_map.139.refs_0_, f32[256,128]{1,0:T(8,128)S(1)} %get-tuple-element.21.refs_1_, f32[256,128]{1,0:T(8,128)S(1)} %get-tuple-element.22.refs_2_, f32[256,384]{1,0:T(8,128)S(1)} %get-tuple-element.23.refs_3_, ...), custom_call_target="tpu_custom_call" | custom-call | tf_op jit(solution)/shard_map/pallas_call | solution.py:282
  30.9 2.9 %collective-permute-done.12.refs_2_ = bf16[128,512]{1,0:T(8,128)(2,1)S(1)} collective-permute-done((bf16[128,512]{1,0:T(8,128)(2,1)S(1)}, bf16[128,512]{1,0:T(8,128)(2,1)S(1)}, u32[]{:S(2)}, u32[]{:S(2)}) %collective-permute-start.12) | collective-permute-done | bytes 131104 | tf_op jit(solution)/shard_map/ppermute | solution.py:406
  33.8 0.0 copy-done.5
  33.8 0.0 copy-done.6
  33.8 0.0 copy-done.12
  33.8 0.0 copy-done.13
  33.8 1.2 %shard_map.143 = bf16[128,384]{1,0:T(8,128)(2,1)} custom-call(f32[128,384]{1,0:T(8,128)S(1)} %get-tuple-element.24.refs_0_, f32[128,128]{1,0:T(8,128)S(1)} %get-tuple-element.25.refs_1_, bf16[128,512]{1,0:T(8,128)(2,1)S(1)} %collective-permute-done.12.refs_2_, bf16[128,384]{1,0:T(8,128)(2,1)S(1)} %get-tuple-element.26.refs_3_, ...), custom_call_target="tpu_custom_call" | custom-call | tf_op jit(solution)/shard_map/pallas_call | solution.py:282
Async XLA Ops:
  0.0 6.5 %copy-start.1 = (bf16[1,2,4,32,384]{4,3,2,1,0:T(8,128)(2,1)S(1)}, bf16[1,2,4,32,384]{4,3,2,1,0:T(8,128)(2,1)}, u32[]{:S(2)}) copy-start(bf16[1,2,4,32,384]{4,3,2,1,0:T(8,128)(2,1)} %cache.5) | copy-start | bytes 589828
  0.0 6.5 %copy-start.2 = (bf16[1,4,32,384]{3,2,1,0:T(8,128)(2,1)S(1)}, bf16[1,4,32,384]{3,2,1,0:T(8,128)(2,1)}, u32[]{:S(2)}) copy-start(bf16[1,4,32,384]{3,2,1,0:T(8,128)(2,1)} %hidden.5) | copy-start | bytes 294916
  0.0 6.5 %copy-start = (bf16[3,3,3,384,384]{4,3,2,1,0:T(8,128)(2,1)S(1)}, bf16[3,3,3,384,384]{4,3,2,1,0:T(8,128)(2,1)}, u32[]{:S(2)}) copy-start(bf16[3,3,3,384,384]{4,3,2,1,0:T(8,128)(2,1)} %weight.3) | copy-start | bytes 23887876
  0.0 6.5 %copy-start.8 = (f32[384]{0:T(512)S(1)}, f32[384]{0:T(512)}, u32[]{:S(2)}) copy-start(f32[384]{0:T(512)} %gain_one.3) | copy-start | bytes 4612
  1.0 5.5 %collective-permute-start = (bf16[3,32,384]{2,1,0:T(8,128)(2,1)S(1)}, bf16[3,32,384]{2,1,0:T(8,128)(2,1)S(1)}, u32[]{:S(2)}, u32[]{:S(2)}) collective-permute-start(bf16[3,32,384]{2,1,0:T(8,128)(2,1)S(1)} %get-tuple-element.16), channel_id=1, source_target_pairs={{0,4},{4,0},{8,12},{12,8},{1,5},{5,1},{9,13},{13,9},{2,6},{6,2},{1... | collective-permute-start | bytes 221192 | tf_op jit(solution)/shard_map/ppermute | solution.py:325
  4.2 6.0 %copy-start.7 = (bf16[1,4,32,384]{3,2,1,0:T(8,128)(2,1)S(1)}, bf16[1,4,32,384]{3,2,1,0:T(8,128)(2,1)}, u32[]{:S(2)}) copy-start(bf16[1,4,32,384]{3,2,1,0:T(8,128)(2,1)} %shortcut.1) | copy-start | bytes 294916
  4.2 6.0 %copy-start.9 = (f32[384]{0:T(512)S(1)}, f32[384]{0:T(512)}, u32[]{:S(2)}) copy-start(f32[384]{0:T(512)} %conv_bias.1) | copy-start | bytes 4612
  4.2 6.0 %copy-start.10 = (f32[384]{0:T(512)S(1)}, f32[384]{0:T(512)}, u32[]{:S(2)}) copy-start(f32[384]{0:T(512)} %gain_two.1) | copy-start | bytes 4612
  4.2 20.8 %copy-start.3 = (bf16[384,384]{1,0:T(8,128)(2,1)S(1)}, bf16[384,384]{1,0:T(8,128)(2,1)}, u32[]{:S(2)}) copy-start(bf16[384,384]{1,0:T(8,128)(2,1)} %refs_2_.1) | copy-start | bytes 884740
  4.2 20.8 %copy-start.4 = (bf16[384,384]{1,0:T(8,128)(2,1)S(1)}, bf16[384,384]{1,0:T(8,128)(2,1)}, u32[]{:S(2)}) copy-start(bf16[384,384]{1,0:T(8,128)(2,1)} %refs_4_.2) | copy-start | bytes 884740
  4.2 20.8 %copy-start.11 = (f32[384]{0:T(512)S(1)}, f32[384]{0:T(512)}, u32[]{:S(2)}) copy-start(f32[384]{0:T(512)} %refs_3_.1) | copy-start | bytes 4612
  4.2 2.3 %collective-permute-start.1 = (bf16[3,32,384]{2,1,0:T(8,128)(2,1)S(1)}, bf16[3,32,384]{2,1,0:T(8,128)(2,1)S(1)}, u32[]{:S(2)}, u32[]{:S(2)}) collective-permute-start(bf16[3,32,384]{2,1,0:T(8,128)(2,1)S(1)} %get-tuple-element.17), channel_id=1, source_target_pairs={{4,8},{8,4},{5,9},{9,5},{6,10},{10,6},{7,11},{11,7},{20,24},{24,20... | collective-permute-start | bytes 221192 | tf_op jit(solution)/shard_map/ppermute | solution.py:326
  7.0 26.7 %copy-start.5 = (bf16[384,384]{1,0:T(8,128)(2,1)S(1)}, bf16[384,384]{1,0:T(8,128)(2,1)}, u32[]{:S(2)}) copy-start(bf16[384,384]{1,0:T(8,128)(2,1)} %refs_4_.3) | copy-start | bytes 884740
  7.0 26.7 %copy-start.6 = (bf16[384,384]{1,0:T(8,128)(2,1)S(1)}, bf16[384,384]{1,0:T(8,128)(2,1)}, u32[]{:S(2)}) copy-start(bf16[384,384]{1,0:T(8,128)(2,1)} %refs_6_.1) | copy-start | bytes 884740
  7.1 26.7 %copy-start.12 = (f32[384]{0:T(512)S(1)}, f32[384]{0:T(512)}, u32[]{:S(2)}) copy-start(f32[384]{0:T(512)} %refs_5_.1) | copy-start | bytes 4612
  7.1 26.7 %copy-start.13 = (f32[384]{0:T(512)S(1)}, f32[384]{0:T(512)}, u32[]{:S(2)}) copy-start(f32[384]{0:T(512)} %refs_7_.1) | copy-start | bytes 4612
  7.1 1.3 %collective-permute-start.2 = (bf16[18,384]{1,0:T(8,128)(2,1)S(1)}, bf16[18,384]{1,0:T(8,128)(2,1)S(1)}, u32[]{:S(2)}, u32[]{:S(2)}) collective-permute-start(bf16[18,384]{1,0:T(8,128)(2,1)S(1)} %get-tuple-element.18), channel_id=1, source_target_pairs={{0,1},{1,0},{2,3},{3,2},{4,5},{5,4},{6,7},{7,6},{8,9},{9,8},{10,11... | collective-permute-start | bytes 41480 | tf_op jit(solution)/shard_map/ppermute | solution.py:340
  7.2 3.0 %collective-permute-start.3 = (f32[8,384]{1,0:T(8,128)S(1)}, f32[8,384]{1,0:T(8,128)S(1)}, u32[]{:S(2)}, u32[]{:S(2)}) collective-permute-start(f32[8,384]{1,0:T(8,128)S(1)} %get-tuple-element.19), channel_id=1, source_target_pairs={{1,2},{2,1},{5,6},{6,5},{9,10},{10,9},{13,14},{14,13},{17,18},{18,... | collective-permute-start | bytes 36872 | tf_op jit(solution)/shard_map/ppermute | solution.py:341
  10.3 10.9 %collective-permute-start.6 = (bf16[128,384]{1,0:T(8,128)(2,1)S(1)}, bf16[128,384]{1,0:T(8,128)(2,1)S(1)}, u32[]{:S(2)}, u32[]{:S(2)}) collective-permute-start(bf16[128,384]{1,0:T(8,128)(2,1)S(1)} %get-tuple-element.20.refs_0_.refs_1_), channel_id=1, source_target_pairs={{0,12},{4,8},{8,4},{12,0},{1,13},{5,9},{9,5},{13,1},{2,14},{6,10},... | collective-permute-start | bytes 294920 | tf_op jit(solution)/shard_map/ppermute | solution.py:369
  14.4 7.3 %collective-permute-start.10 = (bf16[128,384]{1,0:T(8,128)(2,1)S(1)}, bf16[128,384]{1,0:T(8,128)(2,1)S(1)}, u32[]{:S(2)}, u32[]{:S(2)}) collective-permute-start(bf16[128,384]{1,0:T(8,128)(2,1)S(1)} %get-tuple-element.20.refs_0_.refs_1_), channel_id=1, source_target_pairs={{0,8},{4,12},{8,0},{12,4},{1,9},{5,13},{9,1},{13,5},{2,10},{6,14},... | collective-permute-start | bytes 294920 | tf_op jit(solution)/shard_map/ppermute | solution.py:369
  17.1 7.9 %collective-permute-start.8 = (bf16[128,384]{1,0:T(8,128)(2,1)S(1)}, bf16[128,384]{1,0:T(8,128)(2,1)S(1)}, u32[]{:S(2)}, u32[]{:S(2)}) collective-permute-start(bf16[128,384]{1,0:T(8,128)(2,1)S(1)} %get-tuple-element.20.refs_0_.refs_1_), channel_id=1, source_target_pairs={{0,4},{4,0},{8,12},{12,8},{1,5},{5,1},{9,13},{13,9},{2,6},{6,2},{1... | collective-permute-start | bytes 294920 | tf_op jit(solution)/shard_map/ppermute | solution.py:369
  17.6 7.4 %collective-permute-start.4 = (bf16[128,384]{1,0:T(8,128)(2,1)S(1)}, bf16[128,384]{1,0:T(8,128)(2,1)S(1)}, u32[]{:S(2)}, u32[]{:S(2)}) collective-permute-start(bf16[128,384]{1,0:T(8,128)(2,1)S(1)} %get-tuple-element.20.refs_0_.refs_1_), channel_id=1, source_target_pairs={{0,2},{1,3},{2,0},{3,1},{4,6},{5,7},{6,4},{7,5},{8,10},{9,11},{10,... | collective-permute-start | bytes 294920 | tf_op jit(solution)/shard_map/ppermute | solution.py:372
  21.3 4.4 %collective-permute-start.5 = (bf16[128,384]{1,0:T(8,128)(2,1)S(1)}, bf16[128,384]{1,0:T(8,128)(2,1)S(1)}, u32[]{:S(2)}, u32[]{:S(2)}) collective-permute-start(bf16[128,384]{1,0:T(8,128)(2,1)S(1)} %get-tuple-element.20.refs_0_.refs_1_), channel_id=1, source_target_pairs={{0,1},{1,0},{2,3},{3,2},{4,5},{5,4},{6,7},{7,6},{8,9},{9,8},{10,11... | collective-permute-start | bytes 294920 | tf_op jit(solution)/shard_map/ppermute | solution.py:375
  21.3 4.4 %collective-permute-start.7 = (bf16[128,384]{1,0:T(8,128)(2,1)S(1)}, bf16[128,384]{1,0:T(8,128)(2,1)S(1)}, u32[]{:S(2)}, u32[]{:S(2)}) collective-permute-start(bf16[128,384]{1,0:T(8,128)(2,1)S(1)} %collective-permute-done.6.refs_3_), channel_id=1, source_target_pairs={{0,1},{1,0},{2,3},{3,2},{4,5},{5,4},{6,7},{7,6},{8,9},{9,8},{10,11... | collective-permute-start | bytes 294920 | tf_op jit(solution)/shard_map/ppermute | solution.py:375
  21.8 5.0 %collective-permute-start.11 = (bf16[128,384]{1,0:T(8,128)(2,1)S(1)}, bf16[128,384]{1,0:T(8,128)(2,1)S(1)}, u32[]{:S(2)}, u32[]{:S(2)}) collective-permute-start(bf16[128,384]{1,0:T(8,128)(2,1)S(1)} %collective-permute-done.10.refs_6_), channel_id=1, source_target_pairs={{0,1},{1,0},{2,3},{3,2},{4,5},{5,4},{6,7},{7,6},{8,9},{9,8},{10,11... | collective-permute-start | bytes 294920 | tf_op jit(solution)/shard_map/ppermute | solution.py:375
  25.0 1.8 %collective-permute-start.9 = (bf16[128,384]{1,0:T(8,128)(2,1)S(1)}, bf16[128,384]{1,0:T(8,128)(2,1)S(1)}, u32[]{:S(2)}, u32[]{:S(2)}) collective-permute-start(bf16[128,384]{1,0:T(8,128)(2,1)S(1)} %collective-permute-done.8.refs_4_), channel_id=1, source_target_pairs={{0,1},{1,0},{2,3},{3,2},{4,5},{5,4},{6,7},{7,6},{8,9},{9,8},{10,11... | collective-permute-start | bytes 294920 | tf_op jit(solution)/shard_map/ppermute | solution.py:375
  27.6 6.2 %collective-permute-start.12 = (bf16[128,512]{1,0:T(8,128)(2,1)S(1)}, bf16[128,512]{1,0:T(8,128)(2,1)S(1)}, u32[]{:S(2)}, u32[]{:S(2)}) collective-permute-start(bf16[128,512]{1,0:T(8,128)(2,1)S(1)} %shard_map.142), channel_id=1, source_target_pairs={{2,0},{3,1},{0,2},{1,3},{6,4},{7,5},{4,6},{5,7},{10,8},{11,9},{8,1... | collective-permute-start | bytes 393224 | tf_op jit(solution)/shard_map/ppermute | solution.py:406

commit v5 on v4

--- a/solution.py
+++ b/solution.py
@@ -10,6 +10,7 @@
 
 norm_epsilon = 1e-06
 stat_lanes = 128
+stat_rows = 8
 f32 = jnp.float32
 bf16 = jnp.bfloat16
 
@@ -185,8 +186,9 @@
         at += rows
 
 
-def pack(values, log_sum):
-    lane = lax.broadcasted_iota(jnp.int32, (values.shape[0], stat_lanes), 1)
+def pack(out, values, log_sum):
+    count, channels = values.shape
+    lane = lax.broadcasted_iota(jnp.int32, (count, stat_lanes), 1)
     high = log_sum.astype(bf16).astype(f32)
     rest = log_sum - high
     middle = rest.astype(bf16).astype(f32)
@@ -194,7 +196,10 @@
     stats = jnp.where(
         lane == 0, high, jnp.where(lane == 1, middle, jnp.where(lane == 2, low, 0.0))
     )
-    return values.astype(bf16), stats.astype(bf16)
+    out[0:count, :] = values.astype(bf16)
+    flat = jnp.transpose(stats)[0:stat_rows, :]
+    fill = jnp.zeros((stat_rows, channels - count), f32)
+    out[count : count + stat_rows, :] = jnp.concatenate([flat, fill], axis=1).astype(bf16)
 
 
 def weigh(own, keys, state=None):
@@ -231,7 +236,6 @@
 def late_kernel(tile, blocks, first, *refs):
     queries, tops, totals, weights = refs[:4]
     keys, outs = refs[4 : 4 + blocks], list(refs[4 + blocks :])
-    channels = queries.shape[1]
     block = first
     while outs:
         rows = pl.ds(block * tile, tile)
@@ -243,18 +247,14 @@
             own[...] = mean
             own_log[...] = jnp.broadcast_to(log_sum, (tile, stat_lanes))
         else:
-            out = outs.pop(0)
-            values, stats = pack(mean, log_sum)
-            out[:, 0:channels] = values
-            out[:, channels : channels + stat_lanes] = stats
+            pack(outs.pop(0), mean, log_sum)
         block += 1
 
 
-def unpack(ref, rows):
-    channels = ref.shape[1] - stat_lanes
-    values = ref[rows, 0:channels].astype(f32)
-    log_sum = jnp.sum(ref[rows, channels : channels + stat_lanes].astype(f32), axis=1, keepdims=True)
-    return values, log_sum
+def unpack(ref, count):
+    flat = ref[count : count + stat_rows, 0:count].astype(f32)
+    stats = jnp.transpose(jnp.concatenate([flat] * (stat_lanes // stat_rows), axis=0))
+    return ref[0:count, :].astype(f32), jnp.sum(stats[:, 0:3], axis=1, keepdims=True)
 
 
 def merge(parts):
@@ -269,7 +269,7 @@
     own, own_log = refs[:2]
     received = refs[2 : 2 + others]
     mixed, value_weight, value_bias, out_weight, out_bias, decoded = refs[2 + others :]
-    parts = [(own[...], own_log[:, 0:1])] + [unpack(ref, pl.ds(0, tile)) for ref in received]
+    parts = [(own[...], own_log[:, 0:1])] + [unpack(ref, tile) for ref in received]
     mean, _ = merge(parts)
     attended = (
         jnp.dot(mean.astype(bf16), value_weight[...], preferred_element_type=f32) + line(value_bias)
@@ -392,7 +392,7 @@
         queries,
         *early,
     )
-    packed = pltpu.VMEM((tile, channels + stat_lanes), bf16)
+    packed = pltpu.VMEM((tile + stat_rows, channels), bf16)
     results = call(
         functools.partial(late_kernel, tile, len(late), 1),
         (packed,) * (chip_count - 1),

time: 35.2 us -> 35 us (level)
  starting transfers between devices: 21.9 us -> 18.3 us
  waiting for transfers between devices: 4.8 us -> 8.19 us
    ppermute x3, waiting for transfers between devices: 0.01 us -> 3.47 us  [per_device(): arrived[step] = lax.ppermute(normed, 'rows', far_pairs(row_count, step))]
    ppermute x4, starting transfers between devices: 3.72 us -> 1.02 us  [per_device(): keys[step] = [block, lax.ppermute(block, 'cols', partners)]]
    ppermute x1, starting transfers between devices: 2.49 us -> 1.56 us  [per_device(): lax.ppermute(result, 'cols', [(j, i) for i, j in far_pairs(chip_count, st...]
  transfers between devices with their start and end apart: 13 -> 13, of which waited for: 3 -> 4; matrix products, arithmetic and copies ran while one was open for 0% -> 0% of each run, Pallas kernels for 12% -> 12%
where the time goes in v5:
time: 35 us; the launch traced here: 34.8 us
  starting transfers between devices  18.3 us (52%)
  waiting for transfers between devices  8.19 us (23%)
  Pallas kernels  8.04 us (23%)
    ppermute x3, starting transfers between devices, per_device(): arrived[step] = lax.ppermute(normed, 'rows', far_pairs(row_count, step))  7.29 us
    pallas_call x8, Pallas kernels, call(): pl.pallas_call(kernel, out_shape=out_shape, in_specs=[VMEM] * len(operand...  7.02 us
    ppermute x1, starting transfers between devices, per_device(): lax.ppermute(normed, 'cols', far_pairs(chip_count, step, 2))  3.64 us
    ppermute x3, waiting for transfers between devices, per_device(): arrived[step] = lax.ppermute(normed, 'rows', far_pairs(row_count, step))  3.47 us
    ppermute x1, starting transfers between devices, per_device(): row_a = lax.ppermute(row_a, 'rows', near_pairs(row_count, 0))  3.13 us
    ppermute x1, waiting for transfers between devices, per_device(): lax.ppermute(result, 'cols', [(j, i) for i, j in far_pairs(chip_count, st...  2.83 us
    ppermute x1, starting transfers between devices, per_device(): lax.ppermute(result, 'cols', [(j, i) for i, j in far_pairs(chip_count, st...  1.56 us
    ppermute x1, waiting for transfers between devices, per_device(): row_a = lax.ppermute(row_a, 'rows', near_pairs(row_count, 0))  1.49 us
  transfers between devices with their start and end apart: 13, of which 4 were waited for; matrix products, arithmetic and copies ran while one was open for 0% of the time, Pallas kernels for 12%

profile of v5, /device:TPU:0, one launch (start us, length us, event | category | flops | bytes accessed | tf_op | source)
XLA Modules:
  0.0 34.8 jit_solution(7794025382979938609)
XLA Ops:
  0.0 0.0 copy-start.1
  0.0 0.0 copy-start.2
  0.0 0.0 copy-start.8
  0.0 0.0 copy-start
  0.0 1.0 %edge_rows.1 = (bf16[3,32,384]{2,1,0:T(8,128)(2,1)S(1)}, bf16[3,32,384]{2,1,0:T(8,128)(2,1)S(1)}) custom-call(bf16[1,2,4,32,384]{4,3,2,1,0:T(8,128)(2,1)} %cache.5, bf16[1,4,32,384]{3,2,1,0:T(8,128)(2,1)} %hidden.5), custom_call_target="tpu_custom_call" | custom-call | flops 10000000000 | bytes 10000000 | tf_op jit(solution)/shard_map/edge_rows/pallas_call | solution.py:315
  1.0 3.1 %collective-permute-start = (bf16[3,32,384]{2,1,0:T(8,128)(2,1)S(1)}, bf16[3,32,384]{2,1,0:T(8,128)(2,1)S(1)}, u32[]{:S(2)}, u32[]{:S(2)}) collective-permute-start(bf16[3,32,384]{2,1,0:T(8,128)(2,1)S(1)} %get-tuple-element.16), channel_id=1, source_target_pairs={{0,4},{4,0},{8,12},{12,8},{1,5},{5,1},{9,13},{13,9},{2,6},{6,2},{1... | collective-permute-start | bytes 221192 | tf_op jit(solution)/shard_map/ppermute | solution.py:325
  4.2 0.0 copy-start.7
  4.2 0.0 copy-start.9
  4.2 0.0 copy-start.10
  4.2 0.0 copy-start.5
  4.2 0.0 copy-start.6
  4.2 0.0 copy-start.11
  4.2 0.8 %collective-permute-start.1 = (bf16[3,32,384]{2,1,0:T(8,128)(2,1)S(1)}, bf16[3,32,384]{2,1,0:T(8,128)(2,1)S(1)}, u32[]{:S(2)}, u32[]{:S(2)}) collective-permute-start(bf16[3,32,384]{2,1,0:T(8,128)(2,1)S(1)} %get-tuple-element.17), channel_id=1, source_target_pairs={{4,8},{8,4},{5,9},{9,5},{6,10},{10,6},{7,11},{11,7},{20,24},{24,20... | collective-permute-start | bytes 221192 | tf_op jit(solution)/shard_map/ppermute | solution.py:326
  5.0 1.5 %collective-permute-done.row_a = bf16[3,32,384]{2,1,0:T(8,128)(2,1)S(1)} collective-permute-done((bf16[3,32,384]{2,1,0:T(8,128)(2,1)S(1)}, bf16[3,32,384]{2,1,0:T(8,128)(2,1)S(1)}, u32[]{:S(2)}, u32[]{:S(2)}) %collective-permute-start) | collective-permute-done | bytes 73760 | tf_op jit(solution)/shard_map/ppermute | solution.py:325
  6.5 0.0 collective-permute-done.1.row_b
  6.5 0.0 copy-done.1
  6.5 0.0 copy-done.2
  6.5 0.0 copy-done.8
  6.5 0.0 copy-done
  6.5 0.5 %shard_map.136 = (bf16[18,384]{1,0:T(8,128)(2,1)S(1)}, f32[8,384]{1,0:T(8,128)S(1)}) custom-call(bf16[1,2,4,32,384]{4,3,2,1,0:T(8,128)(2,1)S(1)} %copy-done.1, bf16[1,4,32,384]{3,2,1,0:T(8,128)(2,1)S(1)} %copy-done.2, bf16[3,32,384]{2,1,0:T(8,128)(2,1)S(1)} %collective-permute-done.row_a, bf16[3,32,384]{2,1,0:T(8,128)(2,1)S(1)} %collective-permute-done.1.row_b, ...), custom_call_target="tpu_custom_call" | custom-call | tf_op jit(solution)/shard_map/pallas_call | solution.py:282
  7.0 0.0 copy-start.3
  7.0 0.0 copy-start.4
  7.1 0.0 copy-start.12
  7.1 0.0 copy-start.13
  7.1 0.1 collective-permute-start.2
  7.2 0.8 %collective-permute-start.3 = (f32[8,384]{1,0:T(8,128)S(1)}, f32[8,384]{1,0:T(8,128)S(1)}, u32[]{:S(2)}, u32[]{:S(2)}) collective-permute-start(f32[8,384]{1,0:T(8,128)S(1)} %get-tuple-element.19), channel_id=1, source_target_pairs={{1,2},{2,1},{5,6},{6,5},{9,10},{10,9},{13,14},{14,13},{17,18},{18,... | collective-permute-start | bytes 36872 | tf_op jit(solution)/shard_map/ppermute | solution.py:341
  8.0 0.4 %collective-permute-done.2.inner = bf16[18,384]{1,0:T(8,128)(2,1)S(1)} collective-permute-done((bf16[18,384]{1,0:T(8,128)(2,1)S(1)}, bf16[18,384]{1,0:T(8,128)(2,1)S(1)}, u32[]{:S(2)}, u32[]{:S(2)}) %collective-permute-start.2) | collective-permute-done | bytes 13856 | tf_op jit(solution)/shard_map/ppermute | solution.py:340
  8.3 1.8 %shard_map.137.convolved = f32[128,384]{1,0:T(8,128)S(1)} custom-call(bf16[1,2,4,32,384]{4,3,2,1,0:T(8,128)(2,1)S(1)} %copy-done.1, bf16[1,4,32,384]{3,2,1,0:T(8,128)(2,1)S(1)} %copy-done.2, bf16[3,32,384]{2,1,0:T(8,128)(2,1)S(1)} %collective-permute-done.row_a, bf16[3,32,384]{2,1,0:T(8,128)(2,1)S(1)} %collective-permute-done.1.row_b, ...), custom_call_target="tpu_custom_call" | custom-call | tf_op jit(solution)/shard_map/pallas_call | solution.py:282
  10.1 0.0 collective-permute-done.3.outer
  10.1 0.0 copy-done.7
  10.1 0.0 copy-done.9
  10.2 0.0 copy-done.10
  10.2 0.2 shard_map.138
  10.3 4.1 %collective-permute-start.6 = (bf16[128,384]{1,0:T(8,128)(2,1)S(1)}, bf16[128,384]{1,0:T(8,128)(2,1)S(1)}, u32[]{:S(2)}, u32[]{:S(2)}) collective-permute-start(bf16[128,384]{1,0:T(8,128)(2,1)S(1)} %get-tuple-element.20.refs_0_.refs_1_), channel_id=1, source_target_pairs={{0,12},{4,8},{8,4},{12,0},{1,13},{5,9},{9,5},{13,1},{2,14},{6,10},... | collective-permute-start | bytes 294920 | tf_op jit(solution)/shard_map/ppermute | solution.py:369
  14.4 3.2 %collective-permute-start.8 = (bf16[128,384]{1,0:T(8,128)(2,1)S(1)}, bf16[128,384]{1,0:T(8,128)(2,1)S(1)}, u32[]{:S(2)}, u32[]{:S(2)}) collective-permute-start(bf16[128,384]{1,0:T(8,128)(2,1)S(1)} %get-tuple-element.20.refs_0_.refs_1_), channel_id=1, source_target_pairs={{0,4},{4,0},{8,12},{12,8},{1,5},{5,1},{9,13},{13,9},{2,6},{6,2},{1... | collective-permute-start | bytes 294920 | tf_op jit(solution)/shard_map/ppermute | solution.py:369
  17.6 0.0 collective-permute-start.10
  17.6 3.6 %collective-permute-start.4 = (bf16[128,384]{1,0:T(8,128)(2,1)S(1)}, bf16[128,384]{1,0:T(8,128)(2,1)S(1)}, u32[]{:S(2)}, u32[]{:S(2)}) collective-permute-start(bf16[128,384]{1,0:T(8,128)(2,1)S(1)} %get-tuple-element.20.refs_0_.refs_1_), channel_id=1, source_target_pairs={{0,2},{1,3},{2,0},{3,1},{4,6},{5,7},{6,4},{7,5},{8,10},{9,11},{10,... | collective-permute-start | bytes 294920 | tf_op jit(solution)/shard_map/ppermute | solution.py:372
  21.3 0.0 collective-permute-start.5
  21.3 0.0 collective-permute-done.6.refs_3_
  21.3 0.5 %collective-permute-start.7 = (bf16[128,384]{1,0:T(8,128)(2,1)S(1)}, bf16[128,384]{1,0:T(8,128)(2,1)S(1)}, u32[]{:S(2)}, u32[]{:S(2)}) collective-permute-start(bf16[128,384]{1,0:T(8,128)(2,1)S(1)} %collective-permute-done.6.refs_3_), channel_id=1, source_target_pairs={{0,1},{1,0},{2,3},{3,2},{4,5},{5,4},{6,7},{7,6},{8,9},{9,8},{10,11... | collective-permute-start | bytes 294920 | tf_op jit(solution)/shard_map/ppermute | solution.py:375
  21.8 0.0 collective-permute-done.8.refs_4_
  21.8 0.2 collective-permute-start.9
  22.0 3.5 %collective-permute-done.10.refs_6_ = bf16[128,384]{1,0:T(8,128)(2,1)S(1)} collective-permute-done((bf16[128,384]{1,0:T(8,128)(2,1)S(1)}, bf16[128,384]{1,0:T(8,128)(2,1)S(1)}, u32[]{:S(2)}, u32[]{:S(2)}) %collective-permute-start.10) | collective-permute-done | bytes 98336 | tf_op jit(solution)/shard_map/ppermute | solution.py:369
  25.4 0.3 collective-permute-start.11
  25.8 0.0 collective-permute-done.4.refs_1_
  25.8 0.0 copy-done.5
  25.8 0.0 copy-done.6
  25.8 0.0 copy-done.11
  25.8 0.6 %shard_map.139.refs_0_ = bf16[256,384]{1,0:T(8,128)(2,1)S(1)} custom-call(bf16[128,384]{1,0:T(8,128)(2,1)S(1)} %get-tuple-element.20.refs_0_.refs_1_, bf16[128,384]{1,0:T(8,128)(2,1)S(1)} %collective-permute-done.4.refs_1_, bf16[384,384]{1,0:T(8,128)(2,1)S(1)} %copy-done.5, f32[384]{0:T(512)S(1)} %copy-done.11, bf16[384,384]{1,0:T(8,128)(2,1)S(1)} %copy-done.6), custom_call_target="tpu_custom_call" | custom-call | tf_op jit(solution)/shard_map/pallas_call | solution.py:282
  26.4 0.0 collective-permute-done.5.refs_2_
  26.4 0.0 collective-permute-done.7.refs_4_
  26.4 1.1 %shard_map.140 = (f32[256,128]{1,0:T(8,128)S(1)}, f32[256,128]{1,0:T(8,128)S(1)}, f32[256,384]{1,0:T(8,128)S(1)}) custom-call(bf16[256,384]{1,0:T(8,128)(2,1)S(1)} %shard_map.139.refs_0_, bf16[128,384]{1,0:T(8,128)(2,1)S(1)} %get-tuple-element.20.refs_0_.refs_1_, bf16[128,384]{1,0:T(8,128)(2,1)S(1)} %collective-permute-done.5.refs_2_, ...), custom_call_target="tpu_custom_call" | custom-call | tf_op jit(solution)/shard_map/pallas_call | solution.py:282
  27.6 0.0 collective-permute-done.9.refs_5_
  27.6 0.0 collective-permute-done.11.refs_7_
  27.6 0.8 %shard_map.142 = bf16[136,384]{1,0:T(8,128)(2,1)S(1)} custom-call(bf16[256,384]{1,0:T(8,128)(2,1)S(1)} %shard_map.139.refs_0_, f32[256,128]{1,0:T(8,128)S(1)} %get-tuple-element.21.refs_1_, f32[256,128]{1,0:T(8,128)S(1)} %get-tuple-element.22.refs_2_, f32[256,384]{1,0:T(8,128)S(1)} %get-tuple-element.23.refs_3_, ...), custom_call_target="tpu_custom_call" | custom-call | tf_op jit(solution)/shard_map/pallas_call | solution.py:282
  28.4 1.6 %collective-permute-start.12 = (bf16[136,384]{1,0:T(8,128)(2,1)S(1)}, bf16[136,384]{1,0:T(8,128)(2,1)S(1)}, u32[]{:S(2)}, u32[]{:S(2)}) collective-permute-start(bf16[136,384]{1,0:T(8,128)(2,1)S(1)} %shard_map.142), channel_id=1, source_target_pairs={{2,0},{3,1},{0,2},{1,3},{6,4},{7,5},{4,6},{5,7},{10,8},{11,9},{8,1... | collective-permute-start | bytes 313352 | tf_op jit(solution)/shard_map/ppermute | solution.py:406
  29.9 0.8 %shard_map.141 = (f32[128,384]{1,0:T(8,128)S(1)}, f32[128,128]{1,0:T(8,128)S(1)}) custom-call(bf16[256,384]{1,0:T(8,128)(2,1)S(1)} %shard_map.139.refs_0_, f32[256,128]{1,0:T(8,128)S(1)} %get-tuple-element.21.refs_1_, f32[256,128]{1,0:T(8,128)S(1)} %get-tuple-element.22.refs_2_, f32[256,384]{1,0:T(8,128)S(1)} %get-tuple-element.23.refs_3_, ...), custom_call_target="tpu_custom_call" | custom-call | tf_op jit(solution)/shard_map/pallas_call | solution.py:282
  30.7 2.8 %collective-permute-done.12.refs_2_ = bf16[136,384]{1,0:T(8,128)(2,1)S(1)} collective-permute-done((bf16[136,384]{1,0:T(8,128)(2,1)S(1)}, bf16[136,384]{1,0:T(8,128)(2,1)S(1)}, u32[]{:S(2)}, u32[]{:S(2)}) %collective-permute-start.12) | collective-permute-done | bytes 104480 | tf_op jit(solution)/shard_map/ppermute | solution.py:406
  33.5 0.0 copy-done.3
  33.5 0.0 copy-done.4
  33.5 0.0 copy-done.12
  33.5 0.0 copy-done.13
  33.6 1.3 %shard_map.143 = bf16[128,384]{1,0:T(8,128)(2,1)} custom-call(f32[128,384]{1,0:T(8,128)S(1)} %get-tuple-element.24.refs_0_, f32[128,128]{1,0:T(8,128)S(1)} %get-tuple-element.25.refs_1_, bf16[136,384]{1,0:T(8,128)(2,1)S(1)} %collective-permute-done.12.refs_2_, bf16[128,384]{1,0:T(8,128)(2,1)S(1)} %get-tuple-element.26.refs_3_, ...), custom_call_target="tpu_custom_call" | custom-call | tf_op jit(solution)/shard_map/pallas_call | solution.py:282
Async XLA Ops:
  0.0 6.5 %copy-start.1 = (bf16[1,2,4,32,384]{4,3,2,1,0:T(8,128)(2,1)S(1)}, bf16[1,2,4,32,384]{4,3,2,1,0:T(8,128)(2,1)}, u32[]{:S(2)}) copy-start(bf16[1,2,4,32,384]{4,3,2,1,0:T(8,128)(2,1)} %cache.5) | copy-start | bytes 589828
  0.0 6.5 %copy-start.2 = (bf16[1,4,32,384]{3,2,1,0:T(8,128)(2,1)S(1)}, bf16[1,4,32,384]{3,2,1,0:T(8,128)(2,1)}, u32[]{:S(2)}) copy-start(bf16[1,4,32,384]{3,2,1,0:T(8,128)(2,1)} %hidden.5) | copy-start | bytes 294916
  0.0 6.5 %copy-start.8 = (f32[384]{0:T(512)S(1)}, f32[384]{0:T(512)}, u32[]{:S(2)}) copy-start(f32[384]{0:T(512)} %gain_one.3) | copy-start | bytes 4612
  0.0 6.5 %copy-start = (bf16[3,3,3,384,384]{4,3,2,1,0:T(8,128)(2,1)S(1)}, bf16[3,3,3,384,384]{4,3,2,1,0:T(8,128)(2,1)}, u32[]{:S(2)}) copy-start(bf16[3,3,3,384,384]{4,3,2,1,0:T(8,128)(2,1)} %weight.3) | copy-start | bytes 23887876
  1.0 5.5 %collective-permute-start = (bf16[3,32,384]{2,1,0:T(8,128)(2,1)S(1)}, bf16[3,32,384]{2,1,0:T(8,128)(2,1)S(1)}, u32[]{:S(2)}, u32[]{:S(2)}) collective-permute-start(bf16[3,32,384]{2,1,0:T(8,128)(2,1)S(1)} %get-tuple-element.16), channel_id=1, source_target_pairs={{0,4},{4,0},{8,12},{12,8},{1,5},{5,1},{9,13},{13,9},{2,6},{6,2},{1... | collective-permute-start | bytes 221192 | tf_op jit(solution)/shard_map/ppermute | solution.py:325
  4.2 6.0 %copy-start.7 = (bf16[1,4,32,384]{3,2,1,0:T(8,128)(2,1)S(1)}, bf16[1,4,32,384]{3,2,1,0:T(8,128)(2,1)}, u32[]{:S(2)}) copy-start(bf16[1,4,32,384]{3,2,1,0:T(8,128)(2,1)} %shortcut.1) | copy-start | bytes 294916
  4.2 6.0 %copy-start.9 = (f32[384]{0:T(512)S(1)}, f32[384]{0:T(512)}, u32[]{:S(2)}) copy-start(f32[384]{0:T(512)} %conv_bias.1) | copy-start | bytes 4612
  4.2 6.0 %copy-start.10 = (f32[384]{0:T(512)S(1)}, f32[384]{0:T(512)}, u32[]{:S(2)}) copy-start(f32[384]{0:T(512)} %gain_two.1) | copy-start | bytes 4612
  4.2 21.6 %copy-start.5 = (bf16[384,384]{1,0:T(8,128)(2,1)S(1)}, bf16[384,384]{1,0:T(8,128)(2,1)}, u32[]{:S(2)}) copy-start(bf16[384,384]{1,0:T(8,128)(2,1)} %refs_2_.1) | copy-start | bytes 884740
  4.2 21.6 %copy-start.6 = (bf16[384,384]{1,0:T(8,128)(2,1)S(1)}, bf16[384,384]{1,0:T(8,128)(2,1)}, u32[]{:S(2)}) copy-start(bf16[384,384]{1,0:T(8,128)(2,1)} %refs_4_.2) | copy-start | bytes 884740
  4.2 21.6 %copy-start.11 = (f32[384]{0:T(512)S(1)}, f32[384]{0:T(512)}, u32[]{:S(2)}) copy-start(f32[384]{0:T(512)} %refs_3_.1) | copy-start | bytes 4612
  4.2 2.3 %collective-permute-start.1 = (bf16[3,32,384]{2,1,0:T(8,128)(2,1)S(1)}, bf16[3,32,384]{2,1,0:T(8,128)(2,1)S(1)}, u32[]{:S(2)}, u32[]{:S(2)}) collective-permute-start(bf16[3,32,384]{2,1,0:T(8,128)(2,1)S(1)} %get-tuple-element.17), channel_id=1, source_target_pairs={{4,8},{8,4},{5,9},{9,5},{6,10},{10,6},{7,11},{11,7},{20,24},{24,20... | collective-permute-start | bytes 221192 | tf_op jit(solution)/shard_map/ppermute | solution.py:326
  7.0 26.5 %copy-start.3 = (bf16[384,384]{1,0:T(8,128)(2,1)S(1)}, bf16[384,384]{1,0:T(8,128)(2,1)}, u32[]{:S(2)}) copy-start(bf16[384,384]{1,0:T(8,128)(2,1)} %refs_4_.3) | copy-start | bytes 884740
  7.0 26.5 %copy-start.4 = (bf16[384,384]{1,0:T(8,128)(2,1)S(1)}, bf16[384,384]{1,0:T(8,128)(2,1)}, u32[]{:S(2)}) copy-start(bf16[384,384]{1,0:T(8,128)(2,1)} %refs_6_.1) | copy-start | bytes 884740
  7.1 26.5 %copy-start.12 = (f32[384]{0:T(512)S(1)}, f32[384]{0:T(512)}, u32[]{:S(2)}) copy-start(f32[384]{0:T(512)} %refs_5_.1) | copy-start | bytes 4612
  7.1 26.5 %copy-start.13 = (f32[384]{0:T(512)S(1)}, f32[384]{0:T(512)}, u32[]{:S(2)}) copy-start(f32[384]{0:T(512)} %refs_7_.1) | copy-start | bytes 4612
  7.1 1.3 %collective-permute-start.2 = (bf16[18,384]{1,0:T(8,128)(2,1)S(1)}, bf16[18,384]{1,0:T(8,128)(2,1)S(1)}, u32[]{:S(2)}, u32[]{:S(2)}) collective-permute-start(bf16[18,384]{1,0:T(8,128)(2,1)S(1)} %get-tuple-element.18), channel_id=1, source_target_pairs={{0,1},{1,0},{2,3},{3,2},{4,5},{5,4},{6,7},{7,6},{8,9},{9,8},{10,11... | collective-permute-start | bytes 41480 | tf_op jit(solution)/shard_map/ppermute | solution.py:340
  7.2 3.0 %collective-permute-start.3 = (f32[8,384]{1,0:T(8,128)S(1)}, f32[8,384]{1,0:T(8,128)S(1)}, u32[]{:S(2)}, u32[]{:S(2)}) collective-permute-start(f32[8,384]{1,0:T(8,128)S(1)} %get-tuple-element.19), channel_id=1, source_target_pairs={{1,2},{2,1},{5,6},{6,5},{9,10},{10,9},{13,14},{14,13},{17,18},{18,... | collective-permute-start | bytes 36872 | tf_op jit(solution)/shard_map/ppermute | solution.py:341
  10.3 10.9 %collective-permute-start.6 = (bf16[128,384]{1,0:T(8,128)(2,1)S(1)}, bf16[128,384]{1,0:T(8,128)(2,1)S(1)}, u32[]{:S(2)}, u32[]{:S(2)}) collective-permute-start(bf16[128,384]{1,0:T(8,128)(2,1)S(1)} %get-tuple-element.20.refs_0_.refs_1_), channel_id=1, source_target_pairs={{0,12},{4,8},{8,4},{12,0},{1,13},{5,9},{9,5},{13,1},{2,14},{6,10},... | collective-permute-start | bytes 294920 | tf_op jit(solution)/shard_map/ppermute | solution.py:369
  14.4 7.3 %collective-permute-start.8 = (bf16[128,384]{1,0:T(8,128)(2,1)S(1)}, bf16[128,384]{1,0:T(8,128)(2,1)S(1)}, u32[]{:S(2)}, u32[]{:S(2)}) collective-permute-start(bf16[128,384]{1,0:T(8,128)(2,1)S(1)} %get-tuple-element.20.refs_0_.refs_1_), channel_id=1, source_target_pairs={{0,4},{4,0},{8,12},{12,8},{1,5},{5,1},{9,13},{13,9},{2,6},{6,2},{1... | collective-permute-start | bytes 294920 | tf_op jit(solution)/shard_map/ppermute | solution.py:369
  17.6 7.8 %collective-permute-start.10 = (bf16[128,384]{1,0:T(8,128)(2,1)S(1)}, bf16[128,384]{1,0:T(8,128)(2,1)S(1)}, u32[]{:S(2)}, u32[]{:S(2)}) collective-permute-start(bf16[128,384]{1,0:T(8,128)(2,1)S(1)} %get-tuple-element.20.refs_0_.refs_1_), channel_id=1, source_target_pairs={{0,8},{4,12},{8,0},{12,4},{1,9},{5,13},{9,1},{13,5},{2,10},{6,14},... | collective-permute-start | bytes 294920 | tf_op jit(solution)/shard_map/ppermute | solution.py:369
  17.6 8.1 %collective-permute-start.4 = (bf16[128,384]{1,0:T(8,128)(2,1)S(1)}, bf16[128,384]{1,0:T(8,128)(2,1)S(1)}, u32[]{:S(2)}, u32[]{:S(2)}) collective-permute-start(bf16[128,384]{1,0:T(8,128)(2,1)S(1)} %get-tuple-element.20.refs_0_.refs_1_), channel_id=1, source_target_pairs={{0,2},{1,3},{2,0},{3,1},{4,6},{5,7},{6,4},{7,5},{8,10},{9,11},{10,... | collective-permute-start | bytes 294920 | tf_op jit(solution)/shard_map/ppermute | solution.py:372
  21.3 5.2 %collective-permute-start.5 = (bf16[128,384]{1,0:T(8,128)(2,1)S(1)}, bf16[128,384]{1,0:T(8,128)(2,1)S(1)}, u32[]{:S(2)}, u32[]{:S(2)}) collective-permute-start(bf16[128,384]{1,0:T(8,128)(2,1)S(1)} %get-tuple-element.20.refs_0_.refs_1_), channel_id=1, source_target_pairs={{0,1},{1,0},{2,3},{3,2},{4,5},{5,4},{6,7},{7,6},{8,9},{9,8},{10,11... | collective-permute-start | bytes 294920 | tf_op jit(solution)/shard_map/ppermute | solution.py:375
  21.3 5.2 %collective-permute-start.7 = (bf16[128,384]{1,0:T(8,128)(2,1)S(1)}, bf16[128,384]{1,0:T(8,128)(2,1)S(1)}, u32[]{:S(2)}, u32[]{:S(2)}) collective-permute-start(bf16[128,384]{1,0:T(8,128)(2,1)S(1)} %collective-permute-done.6.refs_3_), channel_id=1, source_target_pairs={{0,1},{1,0},{2,3},{3,2},{4,5},{5,4},{6,7},{7,6},{8,9},{9,8},{10,11... | collective-permute-start | bytes 294920 | tf_op jit(solution)/shard_map/ppermute | solution.py:375
  21.8 5.8 %collective-permute-start.9 = (bf16[128,384]{1,0:T(8,128)(2,1)S(1)}, bf16[128,384]{1,0:T(8,128)(2,1)S(1)}, u32[]{:S(2)}, u32[]{:S(2)}) collective-permute-start(bf16[128,384]{1,0:T(8,128)(2,1)S(1)} %collective-permute-done.8.refs_4_), channel_id=1, source_target_pairs={{0,1},{1,0},{2,3},{3,2},{4,5},{5,4},{6,7},{7,6},{8,9},{9,8},{10,11... | collective-permute-start | bytes 294920 | tf_op jit(solution)/shard_map/ppermute | solution.py:375
  25.4 2.1 %collective-permute-start.11 = (bf16[128,384]{1,0:T(8,128)(2,1)S(1)}, bf16[128,384]{1,0:T(8,128)(2,1)S(1)}, u32[]{:S(2)}, u32[]{:S(2)}) collective-permute-start(bf16[128,384]{1,0:T(8,128)(2,1)S(1)} %collective-permute-done.10.refs_6_), channel_id=1, source_target_pairs={{0,1},{1,0},{2,3},{3,2},{4,5},{5,4},{6,7},{7,6},{8,9},{9,8},{10,11... | collective-permute-start | bytes 294920 | tf_op jit(solution)/shard_map/ppermute | solution.py:375
  28.4 5.2 %collective-permute-start.12 = (bf16[136,384]{1,0:T(8,128)(2,1)S(1)}, bf16[136,384]{1,0:T(8,128)(2,1)S(1)}, u32[]{:S(2)}, u32[]{:S(2)}) collective-permute-start(bf16[136,384]{1,0:T(8,128)(2,1)S(1)} %shard_map.142), channel_id=1, source_target_pairs={{2,0},{3,1},{0,2},{1,3},{6,4},{7,5},{4,6},{5,7},{10,8},{11,9},{8,1... | collective-permute-start | bytes 313352 | tf_op jit(solution)/shard_map/ppermute | solution.py:406

commit v6 on v5

--- a/solution.py
+++ b/solution.py
@@ -233,6 +233,17 @@
         weights[rows, :] = weighted
 
 
+def fold_kernel(value_weight, value_bias, out_weight, out_bias, weight, bias):
+    weight[...] = jnp.dot(
+        value_weight[...], out_weight[...], preferred_element_type=f32
+    ).astype(bf16)
+    shift = jnp.broadcast_to(line(value_bias), bias.shape)
+    high = shift.astype(bf16)
+    low = (shift - high.astype(f32)).astype(bf16)
+    moved = sum(jnp.dot(v, out_weight[...], preferred_element_type=f32) for v in (high, low))
+    bias[...] = moved + line(out_bias)
+
+
 def late_kernel(tile, blocks, first, *refs):
     queries, tops, totals, weights = refs[:4]
     keys, outs = refs[4 : 4 + blocks], list(refs[4 + blocks :])
@@ -243,8 +254,8 @@
         top, total, weighted = weigh(queries[rows, :], keys, state)
         mean, log_sum = weighted / total, top + jnp.log(total)
         if block == 0:
-            own, own_log = outs.pop(0), outs.pop(0)
-            own[...] = mean
+            weight, own, own_log = outs.pop(0), outs.pop(0), outs.pop(0)
+            own[...] = jnp.dot(mean.astype(bf16), weight[...], preferred_element_type=f32)
             own_log[...] = jnp.broadcast_to(log_sum, (tile, stat_lanes))
         else:
             pack(outs.pop(0), mean, log_sum)
@@ -268,14 +279,14 @@
 def final_kernel(tile, others, *refs):
     own, own_log = refs[:2]
     received = refs[2 : 2 + others]
-    mixed, value_weight, value_bias, out_weight, out_bias, decoded = refs[2 + others :]
-    parts = [(own[...], own_log[:, 0:1])] + [unpack(ref, tile) for ref in received]
+    mixed, weight, bias, decoded = refs[2 + others :]
+    parts = [(own[...], own_log[:, 0:1])]
+    for ref in received:
+        values, log_sum = unpack(ref, tile)
+        projected = jnp.dot(values.astype(bf16), weight[...], preferred_element_type=f32)
+        parts.append((projected, log_sum))
     mean, _ = merge(parts)
-    attended = (
-        jnp.dot(mean.astype(bf16), value_weight[...], preferred_element_type=f32) + line(value_bias)
-    ).astype(bf16)
-    projected = jnp.dot(attended, out_weight[...], preferred_element_type=f32) + line(out_bias)
-    decoded[...] = (mixed[...].astype(f32) + projected).astype(bf16)
+    decoded[...] = (mixed[...].astype(f32) + (mean + bias[0:1, :])).astype(bf16)
 
 
 def call(kernel, out_shape, *operands, scratch_shapes=()):
@@ -363,6 +374,15 @@
         gain_two,
     )
 
+    weight, bias = call(
+        fold_kernel,
+        (pltpu.VMEM((channels, channels), bf16), pltpu.VMEM((8, channels), f32)),
+        value_weight,
+        value_bias,
+        out_weight,
+        out_bias,
+    )
+
     partners = near_pairs(col_count, 0)
     arrived = {0: normed}
     for step in range(row_count - 1, 0, -1):
@@ -373,8 +393,8 @@
     keys = {}
     for step, block in arrived.items():
         keys[step] = [block, lax.ppermute(block, "cols", partners)]
-    early = keys[0] + keys[row_count - 1]
-    late = [key for step in range(1, row_count - 1) for key in keys[step]]
+    early = keys[0]
+    late = [key for step in range(row_count - 1, 0, -1) for key in keys[step]]
 
     query_rows = chip_count * tile
     queries = call(
@@ -411,6 +431,7 @@
         queries,
         *state,
         *late,
+        weight,
     )
     decoded = call(
         functools.partial(final_kernel, tile, chip_count - 1),
@@ -419,10 +440,8 @@
         own_log,
         *returned,
         mixed,
-        value_weight,
-        value_bias,
-        out_weight,
-        out_bias,
+        weight,
+        bias,
     )
     return decoded.reshape(1, tile_rows, tile_cols, channels)
 

time: 35 us -> 35.9 us (1.026)
  starting transfers between devices: 18.3 us -> 23.1 us
  waiting for transfers between devices: 8.19 us -> 4.13 us
    ppermute x4, starting transfers between devices: 1.02 us -> 4.86 us  [per_device(): keys[step] = [block, lax.ppermute(block, 'cols', partners)]]
    ppermute x3, waiting for transfers between devices: 3.47 us -> 0.01 us  [per_device(): arrived[step] = lax.ppermute(normed, 'rows', far_pairs(row_count, step))]
    ppermute x3, starting transfers between devices: 7.29 us -> 8.19 us  [per_device(): arrived[step] = lax.ppermute(normed, 'rows', far_pairs(row_count, step))]
    ppermute x1, waiting for transfers between devices: 2.83 us -> 2.24 us  [per_device(): lax.ppermute(result, 'cols', [(j, i) for i, j in far_pairs(chip_count, st...]
    pallas_call x8 -> x9, Pallas kernels: 7.02 us -> 7.2 us  [call(): pl.pallas_call(kernel, out_shape=out_shape, in_specs=[VMEM] * len(operand...]
  transfers between devices with their start and end apart: 13 -> 13, of which waited for: 4 -> 3; matrix products, arithmetic and copies ran while one was open for 0% -> 0% of each run, Pallas kernels for 12% -> 13%
where the time goes in v6:
time: 35.9 us; the launch traced here: 35.8 us
  starting transfers between devices  23.1 us (64%)
  Pallas kernels  8.22 us (23%)
  waiting for transfers between devices  4.13 us (12%)
    ppermute x3, starting transfers between devices, per_device(): arrived[step] = lax.ppermute(normed, 'rows', far_pairs(row_count, step))  8.19 us
    pallas_call x9, Pallas kernels, call(): pl.pallas_call(kernel, out_shape=out_shape, in_specs=[VMEM] * len(operand...  7.2 us
    ppermute x4, starting transfers between devices, per_device(): keys[step] = [block, lax.ppermute(block, 'cols', partners)]  4.86 us
    ppermute x1, starting transfers between devices, per_device(): lax.ppermute(normed, 'cols', far_pairs(chip_count, step, 2))  3.64 us
    ppermute x1, starting transfers between devices, per_device(): row_a = lax.ppermute(row_a, 'rows', near_pairs(row_count, 0))  3.13 us
    ppermute x1, waiting for transfers between devices, per_device(): lax.ppermute(result, 'cols', [(j, i) for i, j in far_pairs(chip_count, st...  2.24 us
    ppermute x1, starting transfers between devices, per_device(): lax.ppermute(result, 'cols', [(j, i) for i, j in far_pairs(chip_count, st...  1.65 us
    ppermute x1, waiting for transfers between devices, per_device(): row_a = lax.ppermute(row_a, 'rows', near_pairs(row_count, 0))  1.49 us
  transfers between devices with their start and end apart: 13, of which 3 were waited for; matrix products, arithmetic and copies ran while one was open for 0% of the time, Pallas kernels for 13%

profile of v6, /device:TPU:0, one launch (start us, length us, event | category | flops | bytes accessed | tf_op | source)
XLA Modules:
  0.0 35.8 jit_solution(2360542987215945317)
XLA Ops:
  0.0 0.0 copy-start.1
  0.0 0.0 copy-start.2
  0.0 0.0 copy-start
  0.0 0.0 copy-start.8
  0.0 1.0 %edge_rows.1 = (bf16[3,32,384]{2,1,0:T(8,128)(2,1)S(1)}, bf16[3,32,384]{2,1,0:T(8,128)(2,1)S(1)}) custom-call(bf16[1,2,4,32,384]{4,3,2,1,0:T(8,128)(2,1)} %cache.5, bf16[1,4,32,384]{3,2,1,0:T(8,128)(2,1)} %hidden.5), custom_call_target="tpu_custom_call" | custom-call | flops 10000000000 | bytes 10000000 | tf_op jit(solution)/shard_map/edge_rows/pallas_call | solution.py:326
  1.0 3.1 %collective-permute-start = (bf16[3,32,384]{2,1,0:T(8,128)(2,1)S(1)}, bf16[3,32,384]{2,1,0:T(8,128)(2,1)S(1)}, u32[]{:S(2)}, u32[]{:S(2)}) collective-permute-start(bf16[3,32,384]{2,1,0:T(8,128)(2,1)S(1)} %get-tuple-element.18), channel_id=1, source_target_pairs={{0,4},{4,0},{8,12},{12,8},{1,5},{5,1},{9,13},{13,9},{2,6},{6,2},{1... | collective-permute-start | bytes 221192 | tf_op jit(solution)/shard_map/ppermute | solution.py:336
  4.2 0.0 copy-start.7
  4.2 0.0 copy-start.9
  4.2 0.0 copy-start.10
  4.2 0.0 copy-start.5
  4.2 0.0 copy-start.6
  4.2 0.0 copy-start.11
  4.2 0.8 %collective-permute-start.1 = (bf16[3,32,384]{2,1,0:T(8,128)(2,1)S(1)}, bf16[3,32,384]{2,1,0:T(8,128)(2,1)S(1)}, u32[]{:S(2)}, u32[]{:S(2)}) collective-permute-start(bf16[3,32,384]{2,1,0:T(8,128)(2,1)S(1)} %get-tuple-element.19), channel_id=1, source_target_pairs={{4,8},{8,4},{5,9},{9,5},{6,10},{10,6},{7,11},{11,7},{20,24},{24,20... | collective-permute-start | bytes 221192 | tf_op jit(solution)/shard_map/ppermute | solution.py:337
  5.0 1.5 %collective-permute-done.row_a = bf16[3,32,384]{2,1,0:T(8,128)(2,1)S(1)} collective-permute-done((bf16[3,32,384]{2,1,0:T(8,128)(2,1)S(1)}, bf16[3,32,384]{2,1,0:T(8,128)(2,1)S(1)}, u32[]{:S(2)}, u32[]{:S(2)}) %collective-permute-start) | collective-permute-done | bytes 73760 | tf_op jit(solution)/shard_map/ppermute | solution.py:336
  6.5 0.0 collective-permute-done.1.row_b
  6.5 0.0 copy-done.1
  6.5 0.0 copy-done.2
  6.5 0.0 copy-done
  6.5 0.0 copy-done.8
  6.5 0.5 %shard_map.136 = (bf16[18,384]{1,0:T(8,128)(2,1)S(1)}, f32[8,384]{1,0:T(8,128)S(1)}) custom-call(bf16[1,2,4,32,384]{4,3,2,1,0:T(8,128)(2,1)S(1)} %copy-done.1, bf16[1,4,32,384]{3,2,1,0:T(8,128)(2,1)S(1)} %copy-done.2, bf16[3,32,384]{2,1,0:T(8,128)(2,1)S(1)} %collective-permute-done.row_a, bf16[3,32,384]{2,1,0:T(8,128)(2,1)S(1)} %collective-permute-done.1.row_b, ...), custom_call_target="tpu_custom_call" | custom-call | tf_op jit(solution)/shard_map/pallas_call | solution.py:293
  7.0 0.0 copy-start.3
  7.0 0.0 copy-start.4
  7.1 0.0 copy-start.12
  7.1 0.0 copy-start.13
  7.1 0.1 collective-permute-start.2
  7.2 0.8 %collective-permute-start.3 = (f32[8,384]{1,0:T(8,128)S(1)}, f32[8,384]{1,0:T(8,128)S(1)}, u32[]{:S(2)}, u32[]{:S(2)}) collective-permute-start(f32[8,384]{1,0:T(8,128)S(1)} %get-tuple-element.21), channel_id=1, source_target_pairs={{1,2},{2,1},{5,6},{6,5},{9,10},{10,9},{13,14},{14,13},{17,18},{18,... | collective-permute-start | bytes 36872 | tf_op jit(solution)/shard_map/ppermute | solution.py:352
  8.0 0.4 %collective-permute-done.2.inner = bf16[18,384]{1,0:T(8,128)(2,1)S(1)} collective-permute-done((bf16[18,384]{1,0:T(8,128)(2,1)S(1)}, bf16[18,384]{1,0:T(8,128)(2,1)S(1)}, u32[]{:S(2)}, u32[]{:S(2)}) %collective-permute-start.2) | collective-permute-done | bytes 13856 | tf_op jit(solution)/shard_map/ppermute | solution.py:351
  8.3 1.8 %shard_map.137.convolved = f32[128,384]{1,0:T(8,128)S(1)} custom-call(bf16[1,2,4,32,384]{4,3,2,1,0:T(8,128)(2,1)S(1)} %copy-done.1, bf16[1,4,32,384]{3,2,1,0:T(8,128)(2,1)S(1)} %copy-done.2, bf16[3,32,384]{2,1,0:T(8,128)(2,1)S(1)} %collective-permute-done.row_a, bf16[3,32,384]{2,1,0:T(8,128)(2,1)S(1)} %collective-permute-done.1.row_b, ...), custom_call_target="tpu_custom_call" | custom-call | tf_op jit(solution)/shard_map/pallas_call | solution.py:293
  10.1 0.0 collective-permute-done.3.outer
  10.1 0.0 copy-done.7
  10.1 0.0 copy-done.9
  10.2 0.0 copy-done.10
  10.2 0.2 shard_map.138
  10.3 5.3 %collective-permute-start.10 = (bf16[128,384]{1,0:T(8,128)(2,1)S(1)}, bf16[128,384]{1,0:T(8,128)(2,1)S(1)}, u32[]{:S(2)}, u32[]{:S(2)}) collective-permute-start(bf16[128,384]{1,0:T(8,128)(2,1)S(1)} %get-tuple-element.22.refs_0_.refs_1_), channel_id=1, source_target_pairs={{0,4},{4,0},{8,12},{12,8},{1,5},{5,1},{9,13},{13,9},{2,6},{6,2},{1... | collective-permute-start | bytes 294920 | tf_op jit(solution)/shard_map/ppermute | solution.py:389
  15.6 1.5 %collective-permute-start.8 = (bf16[128,384]{1,0:T(8,128)(2,1)S(1)}, bf16[128,384]{1,0:T(8,128)(2,1)S(1)}, u32[]{:S(2)}, u32[]{:S(2)}) collective-permute-start(bf16[128,384]{1,0:T(8,128)(2,1)S(1)} %get-tuple-element.22.refs_0_.refs_1_), channel_id=1, source_target_pairs={{0,8},{4,12},{8,0},{12,4},{1,9},{5,13},{9,1},{13,5},{2,10},{6,14},... | collective-permute-start | bytes 294920 | tf_op jit(solution)/shard_map/ppermute | solution.py:389
  17.1 1.4 %collective-permute-start.6 = (bf16[128,384]{1,0:T(8,128)(2,1)S(1)}, bf16[128,384]{1,0:T(8,128)(2,1)S(1)}, u32[]{:S(2)}, u32[]{:S(2)}) collective-permute-start(bf16[128,384]{1,0:T(8,128)(2,1)S(1)} %get-tuple-element.22.refs_0_.refs_1_), channel_id=1, source_target_pairs={{0,12},{4,8},{8,4},{12,0},{1,13},{5,9},{9,5},{13,1},{2,14},{6,10},... | collective-permute-start | bytes 294920 | tf_op jit(solution)/shard_map/ppermute | solution.py:389
  18.5 3.6 %collective-permute-start.4 = (bf16[128,384]{1,0:T(8,128)(2,1)S(1)}, bf16[128,384]{1,0:T(8,128)(2,1)S(1)}, u32[]{:S(2)}, u32[]{:S(2)}) collective-permute-start(bf16[128,384]{1,0:T(8,128)(2,1)S(1)} %get-tuple-element.22.refs_0_.refs_1_), channel_id=1, source_target_pairs={{0,2},{1,3},{2,0},{3,1},{4,6},{5,7},{6,4},{7,5},{8,10},{9,11},{10,... | collective-permute-start | bytes 294920 | tf_op jit(solution)/shard_map/ppermute | solution.py:392
  22.2 0.0 collective-permute-start.5
  22.2 0.0 collective-permute-done.10.refs_8_
  22.2 0.5 %collective-permute-start.11 = (bf16[128,384]{1,0:T(8,128)(2,1)S(1)}, bf16[128,384]{1,0:T(8,128)(2,1)S(1)}, u32[]{:S(2)}, u32[]{:S(2)}) collective-permute-start(bf16[128,384]{1,0:T(8,128)(2,1)S(1)} %collective-permute-done.10.refs_8_), channel_id=1, source_target_pairs={{0,1},{1,0},{2,3},{3,2},{4,5},{5,4},{6,7},{7,6},{8,9},{9,8},{10,11... | collective-permute-start | bytes 294920 | tf_op jit(solution)/shard_map/ppermute | solution.py:395
  22.7 0.0 collective-permute-done.8.refs_6_
  22.7 4.3 %collective-permute-start.9 = (bf16[128,384]{1,0:T(8,128)(2,1)S(1)}, bf16[128,384]{1,0:T(8,128)(2,1)S(1)}, u32[]{:S(2)}, u32[]{:S(2)}) collective-permute-start(bf16[128,384]{1,0:T(8,128)(2,1)S(1)} %collective-permute-done.8.refs_6_), channel_id=1, source_target_pairs={{0,1},{1,0},{2,3},{3,2},{4,5},{5,4},{6,7},{7,6},{8,9},{9,8},{10,11... | collective-permute-start | bytes 294920 | tf_op jit(solution)/shard_map/ppermute | solution.py:395
  27.0 0.0 collective-permute-done.6.refs_4_
  27.0 0.0 collective-permute-start.7
  27.0 0.0 collective-permute-done.4.refs_1_
  27.0 0.0 copy-done.5
  27.0 0.0 copy-done.6
  27.0 0.0 copy-done.11
  27.1 0.6 %shard_map.139.refs_0_ = bf16[256,384]{1,0:T(8,128)(2,1)S(1)} custom-call(bf16[128,384]{1,0:T(8,128)(2,1)S(1)} %get-tuple-element.22.refs_0_.refs_1_, bf16[128,384]{1,0:T(8,128)(2,1)S(1)} %collective-permute-done.4.refs_1_, bf16[384,384]{1,0:T(8,128)(2,1)S(1)} %copy-done.5, f32[384]{0:T(512)S(1)} %copy-done.11, bf16[384,384]{1,0:T(8,128)(2,1)S(1)} %copy-done.6), custom_call_target="tpu_custom_call" | custom-call | tf_op jit(solution)/shard_map/pallas_call | solution.py:293
  27.7 0.0 collective-permute-done.5.refs_2_
  27.7 0.8 %shard_map.140 = (f32[256,128]{1,0:T(8,128)S(1)}, f32[256,128]{1,0:T(8,128)S(1)}, f32[256,384]{1,0:T(8,128)S(1)}) custom-call(bf16[256,384]{1,0:T(8,128)(2,1)S(1)} %shard_map.139.refs_0_, bf16[128,384]{1,0:T(8,128)(2,1)S(1)} %get-tuple-element.22.refs_0_.refs_1_, bf16[128,384]{1,0:T(8,128)(2,1)S(1)} %collective-permute-done.5.refs_2_), custom_call_target="tpu_custom_call" | custom-call | tf_op jit(solution)/shard_map/pallas_call | solution.py:293
  28.5 0.0 collective-permute-done.11.refs_9_
  28.5 0.0 collective-permute-done.9.refs_7_
  28.5 0.0 collective-permute-done.7.refs_5_
  28.5 0.9 %shard_map.143 = bf16[136,384]{1,0:T(8,128)(2,1)S(1)} custom-call(bf16[256,384]{1,0:T(8,128)(2,1)S(1)} %shard_map.139.refs_0_, f32[256,128]{1,0:T(8,128)S(1)} %get-tuple-element.23.refs_1_, f32[256,128]{1,0:T(8,128)S(1)} %get-tuple-element.24.refs_2_, f32[256,384]{1,0:T(8,128)S(1)} %get-tuple-element.25.refs_3_, ...), custom_call_target="tpu_custom_call" | custom-call | tf_op jit(solution)/shard_map/pallas_call | solution.py:293
  29.4 1.7 %collective-permute-start.12 = (bf16[136,384]{1,0:T(8,128)(2,1)S(1)}, bf16[136,384]{1,0:T(8,128)(2,1)S(1)}, u32[]{:S(2)}, u32[]{:S(2)}) collective-permute-start(bf16[136,384]{1,0:T(8,128)(2,1)S(1)} %shard_map.143), channel_id=1, source_target_pairs={{2,0},{3,1},{0,2},{1,3},{6,4},{7,5},{4,6},{5,7},{10,8},{11,9},{8,1... | collective-permute-start | bytes 313352 | tf_op jit(solution)/shard_map/ppermute | solution.py:426
  31.1 0.0 copy-done.3
  31.1 0.0 copy-done.4
  31.1 0.0 copy-done.12
  31.1 0.0 copy-done.13
  31.1 0.4 %shard_map.141 = (bf16[384,384]{1,0:T(8,128)(2,1)S(1)}, f32[8,384]{1,0:T(8,128)S(1)}) custom-call(bf16[384,384]{1,0:T(8,128)(2,1)S(1)} %copy-done.3, f32[384]{0:T(512)S(1)} %copy-done.12, bf16[384,384]{1,0:T(8,128)(2,1)S(1)} %copy-done.4, f32[384]{0:T(512)S(1)} %copy-done.13), custom_call_target="tpu_custom_call" | custom-call | tf_op jit(solution)/shard_map/pallas_call | solution.py:293
  31.5 1.1 %shard_map.142 = (f32[128,384]{1,0:T(8,128)S(1)}, f32[128,128]{1,0:T(8,128)S(1)}) custom-call(bf16[256,384]{1,0:T(8,128)(2,1)S(1)} %shard_map.139.refs_0_, f32[256,128]{1,0:T(8,128)S(1)} %get-tuple-element.23.refs_1_, f32[256,128]{1,0:T(8,128)S(1)} %get-tuple-element.24.refs_2_, f32[256,384]{1,0:T(8,128)S(1)} %get-tuple-element.25.refs_3_, ...), custom_call_target="tpu_custom_call" | custom-call | tf_op jit(solution)/shard_map/pallas_call | solution.py:293
  32.6 2.2 %collective-permute-done.12.refs_2_ = bf16[136,384]{1,0:T(8,128)(2,1)S(1)} collective-permute-done((bf16[136,384]{1,0:T(8,128)(2,1)S(1)}, bf16[136,384]{1,0:T(8,128)(2,1)S(1)}, u32[]{:S(2)}, u32[]{:S(2)}) %collective-permute-start.12) | collective-permute-done | bytes 104480 | tf_op jit(solution)/shard_map/ppermute | solution.py:426
  34.8 0.9 %shard_map.144 = bf16[128,384]{1,0:T(8,128)(2,1)} custom-call(f32[128,384]{1,0:T(8,128)S(1)} %get-tuple-element.27.refs_0_, f32[128,128]{1,0:T(8,128)S(1)} %get-tuple-element.28.refs_1_, bf16[136,384]{1,0:T(8,128)(2,1)S(1)} %collective-permute-done.12.refs_2_, bf16[128,384]{1,0:T(8,128)(2,1)S(1)} %get-tuple-element.29.refs_3_, ...), custom_call_target="tpu_custom_call" | custom-call | tf_op jit(solution)/shard_map/pallas_call | solution.py:293
Async XLA Ops:
  0.0 6.5 %copy-start.1 = (bf16[1,2,4,32,384]{4,3,2,1,0:T(8,128)(2,1)S(1)}, bf16[1,2,4,32,384]{4,3,2,1,0:T(8,128)(2,1)}, u32[]{:S(2)}) copy-start(bf16[1,2,4,32,384]{4,3,2,1,0:T(8,128)(2,1)} %cache.5) | copy-start | bytes 589828
  0.0 6.5 %copy-start.2 = (bf16[1,4,32,384]{3,2,1,0:T(8,128)(2,1)S(1)}, bf16[1,4,32,384]{3,2,1,0:T(8,128)(2,1)}, u32[]{:S(2)}) copy-start(bf16[1,4,32,384]{3,2,1,0:T(8,128)(2,1)} %hidden.5) | copy-start | bytes 294916
  0.0 6.5 %copy-start = (bf16[3,3,3,384,384]{4,3,2,1,0:T(8,128)(2,1)S(1)}, bf16[3,3,3,384,384]{4,3,2,1,0:T(8,128)(2,1)}, u32[]{:S(2)}) copy-start(bf16[3,3,3,384,384]{4,3,2,1,0:T(8,128)(2,1)} %weight.3) | copy-start | bytes 23887876
  0.0 6.5 %copy-start.8 = (f32[384]{0:T(512)S(1)}, f32[384]{0:T(512)}, u32[]{:S(2)}) copy-start(f32[384]{0:T(512)} %gain_one.3) | copy-start | bytes 4612
  1.0 5.5 %collective-permute-start = (bf16[3,32,384]{2,1,0:T(8,128)(2,1)S(1)}, bf16[3,32,384]{2,1,0:T(8,128)(2,1)S(1)}, u32[]{:S(2)}, u32[]{:S(2)}) collective-permute-start(bf16[3,32,384]{2,1,0:T(8,128)(2,1)S(1)} %get-tuple-element.18), channel_id=1, source_target_pairs={{0,4},{4,0},{8,12},{12,8},{1,5},{5,1},{9,13},{13,9},{2,6},{6,2},{1... | collective-permute-start | bytes 221192 | tf_op jit(solution)/shard_map/ppermute | solution.py:336
  4.2 6.0 %copy-start.7 = (bf16[1,4,32,384]{3,2,1,0:T(8,128)(2,1)S(1)}, bf16[1,4,32,384]{3,2,1,0:T(8,128)(2,1)}, u32[]{:S(2)}) copy-start(bf16[1,4,32,384]{3,2,1,0:T(8,128)(2,1)} %shortcut.1) | copy-start | bytes 294916
  4.2 6.0 %copy-start.9 = (f32[384]{0:T(512)S(1)}, f32[384]{0:T(512)}, u32[]{:S(2)}) copy-start(f32[384]{0:T(512)} %conv_bias.1) | copy-start | bytes 4612
  4.2 6.0 %copy-start.10 = (f32[384]{0:T(512)S(1)}, f32[384]{0:T(512)}, u32[]{:S(2)}) copy-start(f32[384]{0:T(512)} %gain_two.1) | copy-start | bytes 4612
  4.2 22.9 %copy-start.5 = (bf16[384,384]{1,0:T(8,128)(2,1)S(1)}, bf16[384,384]{1,0:T(8,128)(2,1)}, u32[]{:S(2)}) copy-start(bf16[384,384]{1,0:T(8,128)(2,1)} %refs_2_.1) | copy-start | bytes 884740
  4.2 22.9 %copy-start.6 = (bf16[384,384]{1,0:T(8,128)(2,1)S(1)}, bf16[384,384]{1,0:T(8,128)(2,1)}, u32[]{:S(2)}) copy-start(bf16[384,384]{1,0:T(8,128)(2,1)} %refs_4_.1) | copy-start | bytes 884740
  4.2 22.9 %copy-start.11 = (f32[384]{0:T(512)S(1)}, f32[384]{0:T(512)}, u32[]{:S(2)}) copy-start(f32[384]{0:T(512)} %refs_3_.1) | copy-start | bytes 4612
  4.2 2.3 %collective-permute-start.1 = (bf16[3,32,384]{2,1,0:T(8,128)(2,1)S(1)}, bf16[3,32,384]{2,1,0:T(8,128)(2,1)S(1)}, u32[]{:S(2)}, u32[]{:S(2)}) collective-permute-start(bf16[3,32,384]{2,1,0:T(8,128)(2,1)S(1)} %get-tuple-element.19), channel_id=1, source_target_pairs={{4,8},{8,4},{5,9},{9,5},{6,10},{10,6},{7,11},{11,7},{20,24},{24,20... | collective-permute-start | bytes 221192 | tf_op jit(solution)/shard_map/ppermute | solution.py:337
  7.0 24.1 %copy-start.3 = (bf16[384,384]{1,0:T(8,128)(2,1)S(1)}, bf16[384,384]{1,0:T(8,128)(2,1)}, u32[]{:S(2)}) copy-start(bf16[384,384]{1,0:T(8,128)(2,1)} %value_weight.1) | copy-start | bytes 884740
  7.0 24.1 %copy-start.4 = (bf16[384,384]{1,0:T(8,128)(2,1)S(1)}, bf16[384,384]{1,0:T(8,128)(2,1)}, u32[]{:S(2)}) copy-start(bf16[384,384]{1,0:T(8,128)(2,1)} %out_weight.1) | copy-start | bytes 884740
  7.1 24.1 %copy-start.12 = (f32[384]{0:T(512)S(1)}, f32[384]{0:T(512)}, u32[]{:S(2)}) copy-start(f32[384]{0:T(512)} %value_bias.1) | copy-start | bytes 4612
  7.1 24.0 %copy-start.13 = (f32[384]{0:T(512)S(1)}, f32[384]{0:T(512)}, u32[]{:S(2)}) copy-start(f32[384]{0:T(512)} %out_bias.1) | copy-start | bytes 4612
  7.1 1.3 %collective-permute-start.2 = (bf16[18,384]{1,0:T(8,128)(2,1)S(1)}, bf16[18,384]{1,0:T(8,128)(2,1)S(1)}, u32[]{:S(2)}, u32[]{:S(2)}) collective-permute-start(bf16[18,384]{1,0:T(8,128)(2,1)S(1)} %get-tuple-element.20), channel_id=1, source_target_pairs={{0,1},{1,0},{2,3},{3,2},{4,5},{5,4},{6,7},{7,6},{8,9},{9,8},{10,11... | collective-permute-start | bytes 41480 | tf_op jit(solution)/shard_map/ppermute | solution.py:351
  7.2 3.0 %collective-permute-start.3 = (f32[8,384]{1,0:T(8,128)S(1)}, f32[8,384]{1,0:T(8,128)S(1)}, u32[]{:S(2)}, u32[]{:S(2)}) collective-permute-start(f32[8,384]{1,0:T(8,128)S(1)} %get-tuple-element.21), channel_id=1, source_target_pairs={{1,2},{2,1},{5,6},{6,5},{9,10},{10,9},{13,14},{14,13},{17,18},{18,... | collective-permute-start | bytes 36872 | tf_op jit(solution)/shard_map/ppermute | solution.py:352
  10.3 11.8 %collective-permute-start.10 = (bf16[128,384]{1,0:T(8,128)(2,1)S(1)}, bf16[128,384]{1,0:T(8,128)(2,1)S(1)}, u32[]{:S(2)}, u32[]{:S(2)}) collective-permute-start(bf16[128,384]{1,0:T(8,128)(2,1)S(1)} %get-tuple-element.22.refs_0_.refs_1_), channel_id=1, source_target_pairs={{0,4},{4,0},{8,12},{12,8},{1,5},{5,1},{9,13},{13,9},{2,6},{6,2},{1... | collective-permute-start | bytes 294920 | tf_op jit(solution)/shard_map/ppermute | solution.py:389
  15.6 7.1 %collective-permute-start.8 = (bf16[128,384]{1,0:T(8,128)(2,1)S(1)}, bf16[128,384]{1,0:T(8,128)(2,1)S(1)}, u32[]{:S(2)}, u32[]{:S(2)}) collective-permute-start(bf16[128,384]{1,0:T(8,128)(2,1)S(1)} %get-tuple-element.22.refs_0_.refs_1_), channel_id=1, source_target_pairs={{0,8},{4,12},{8,0},{12,4},{1,9},{5,13},{9,1},{13,5},{2,10},{6,14},... | collective-permute-start | bytes 294920 | tf_op jit(solution)/shard_map/ppermute | solution.py:389
  17.1 9.9 %collective-permute-start.6 = (bf16[128,384]{1,0:T(8,128)(2,1)S(1)}, bf16[128,384]{1,0:T(8,128)(2,1)S(1)}, u32[]{:S(2)}, u32[]{:S(2)}) collective-permute-start(bf16[128,384]{1,0:T(8,128)(2,1)S(1)} %get-tuple-element.22.refs_0_.refs_1_), channel_id=1, source_target_pairs={{0,12},{4,8},{8,4},{12,0},{1,13},{5,9},{9,5},{13,1},{2,14},{6,10},... | collective-permute-start | bytes 294920 | tf_op jit(solution)/shard_map/ppermute | solution.py:389
  18.5 8.5 %collective-permute-start.4 = (bf16[128,384]{1,0:T(8,128)(2,1)S(1)}, bf16[128,384]{1,0:T(8,128)(2,1)S(1)}, u32[]{:S(2)}, u32[]{:S(2)}) collective-permute-start(bf16[128,384]{1,0:T(8,128)(2,1)S(1)} %get-tuple-element.22.refs_0_.refs_1_), channel_id=1, source_target_pairs={{0,2},{1,3},{2,0},{3,1},{4,6},{5,7},{6,4},{7,5},{8,10},{9,11},{10,... | collective-permute-start | bytes 294920 | tf_op jit(solution)/shard_map/ppermute | solution.py:392
  22.2 5.5 %collective-permute-start.5 = (bf16[128,384]{1,0:T(8,128)(2,1)S(1)}, bf16[128,384]{1,0:T(8,128)(2,1)S(1)}, u32[]{:S(2)}, u32[]{:S(2)}) collective-permute-start(bf16[128,384]{1,0:T(8,128)(2,1)S(1)} %get-tuple-element.22.refs_0_.refs_1_), channel_id=1, source_target_pairs={{0,1},{1,0},{2,3},{3,2},{4,5},{5,4},{6,7},{7,6},{8,9},{9,8},{10,11... | collective-permute-start | bytes 294920 | tf_op jit(solution)/shard_map/ppermute | solution.py:395
  22.2 6.4 %collective-permute-start.11 = (bf16[128,384]{1,0:T(8,128)(2,1)S(1)}, bf16[128,384]{1,0:T(8,128)(2,1)S(1)}, u32[]{:S(2)}, u32[]{:S(2)}) collective-permute-start(bf16[128,384]{1,0:T(8,128)(2,1)S(1)} %collective-permute-done.10.refs_8_), channel_id=1, source_target_pairs={{0,1},{1,0},{2,3},{3,2},{4,5},{5,4},{6,7},{7,6},{8,9},{9,8},{10,11... | collective-permute-start | bytes 294920 | tf_op jit(solution)/shard_map/ppermute | solution.py:395
  22.7 5.9 %collective-permute-start.9 = (bf16[128,384]{1,0:T(8,128)(2,1)S(1)}, bf16[128,384]{1,0:T(8,128)(2,1)S(1)}, u32[]{:S(2)}, u32[]{:S(2)}) collective-permute-start(bf16[128,384]{1,0:T(8,128)(2,1)S(1)} %collective-permute-done.8.refs_6_), channel_id=1, source_target_pairs={{0,1},{1,0},{2,3},{3,2},{4,5},{5,4},{6,7},{7,6},{8,9},{9,8},{10,11... | collective-permute-start | bytes 294920 | tf_op jit(solution)/shard_map/ppermute | solution.py:395
  27.0 1.5 %collective-permute-start.7 = (bf16[128,384]{1,0:T(8,128)(2,1)S(1)}, bf16[128,384]{1,0:T(8,128)(2,1)S(1)}, u32[]{:S(2)}, u32[]{:S(2)}) collective-permute-start(bf16[128,384]{1,0:T(8,128)(2,1)S(1)} %collective-permute-done.6.refs_4_), channel_id=1, source_target_pairs={{0,1},{1,0},{2,3},{3,2},{4,5},{5,4},{6,7},{7,6},{8,9},{9,8},{10,11... | collective-permute-start | bytes 294920 | tf_op jit(solution)/shard_map/ppermute | solution.py:395
  29.4 5.4 %collective-permute-start.12 = (bf16[136,384]{1,0:T(8,128)(2,1)S(1)}, bf16[136,384]{1,0:T(8,128)(2,1)S(1)}, u32[]{:S(2)}, u32[]{:S(2)}) collective-permute-start(bf16[136,384]{1,0:T(8,128)(2,1)S(1)} %shard_map.143), channel_id=1, source_target_pairs={{2,0},{3,1},{0,2},{1,3},{6,4},{7,5},{4,6},{5,7},{10,8},{11,9},{8,1... | collective-permute-start | bytes 313352 | tf_op jit(solution)/shard_map/ppermute | solution.py:426

commit v7 on v6

--- a/solution.py
+++ b/solution.py
@@ -244,6 +244,18 @@
     bias[...] = moved + line(out_bias)
 
 
+def middle_kernel(tile, blocks, *refs):
+    queries, tops, totals, weights = refs[:4]
+    keys, outs = refs[4 : 4 + blocks], refs[4 + blocks :]
+    for at in range(0, queries.shape[0], tile):
+        rows = pl.ds(at, tile)
+        state = (tops[rows, 0:1], totals[rows, 0:1], weights[rows, :])
+        top, total, weighted = weigh(queries[rows, :], keys, state)
+        outs[0][rows, :] = jnp.broadcast_to(top, (tile, stat_lanes))
+        outs[1][rows, :] = jnp.broadcast_to(total, (tile, stat_lanes))
+        outs[2][rows, :] = weighted
+
+
 def late_kernel(tile, blocks, first, *refs):
     queries, tops, totals, weights = refs[:4]
     keys, outs = refs[4 : 4 + blocks], list(refs[4 + blocks :])
@@ -394,7 +406,8 @@
     for step, block in arrived.items():
         keys[step] = [block, lax.ppermute(block, "cols", partners)]
     early = keys[0]
-    late = [key for step in range(row_count - 1, 0, -1) for key in keys[step]]
+    middle = keys[row_count - 1]
+    late = [key for step in range(row_count - 2, 0, -1) for key in keys[step]]
 
     query_rows = chip_count * tile
     queries = call(
@@ -411,6 +424,13 @@
         (stat, stat, pltpu.VMEM((query_rows, channels), f32)),
         queries,
         *early,
+    )
+    state = call(
+        functools.partial(middle_kernel, tile, len(middle)),
+        (stat, stat, pltpu.VMEM((query_rows, channels), f32)),
+        queries,
+        *state,
+        *middle,
     )
     packed = pltpu.VMEM((tile + stat_rows, channels), bf16)
     results = call(

time: 35.9 us -> 35 us (0.975)
  starting transfers between devices: 23.1 us -> 21.9 us
  Pallas kernels: 8.22 us -> 8.95 us
  waiting for transfers between devices: 4.13 us -> 3.67 us
    ppermute x4, starting transfers between devices: 4.86 us -> 3.72 us  [per_device(): keys[step] = [block, lax.ppermute(block, 'cols', partners)]]
    ppermute x3, starting transfers between devices: 8.19 us -> 7.29 us  [per_device(): arrived[step] = lax.ppermute(normed, 'rows', far_pairs(row_count, step))]
    ppermute x1, starting transfers between devices: 1.65 us -> 2.48 us  [per_device(): lax.ppermute(result, 'cols', [(j, i) for i, j in far_pairs(chip_count, st...]
    pallas_call x9 -> x10, Pallas kernels: 7.2 us -> 7.93 us  [call(): pl.pallas_call(kernel, out_shape=out_shape, in_specs=[VMEM] * len(operand...]
    ppermute x1, waiting for transfers between devices: 2.24 us -> 1.78 us  [per_device(): lax.ppermute(result, 'cols', [(j, i) for i, j in far_pairs(chip_count, st...]
  transfers between devices with their start and end apart: 13 -> 13, of which waited for: 3 -> 3; matrix products, arithmetic and copies ran while one was open for 0% -> 0% of each run, Pallas kernels for 13% -> 16%
where the time goes in v7:
time: 35 us; the launch traced here: 34.8 us
  starting transfers between devices  21.9 us (63%)
  Pallas kernels  8.95 us (26%)
  waiting for transfers between devices  3.67 us (10%)
    pallas_call x10, Pallas kernels, call(): pl.pallas_call(kernel, out_shape=out_shape, in_specs=[VMEM] * len(operand...  7.93 us
    ppermute x3, starting transfers between devices, per_device(): arrived[step] = lax.ppermute(normed, 'rows', far_pairs(row_count, step))  7.29 us
    ppermute x4, starting transfers between devices, per_device(): keys[step] = [block, lax.ppermute(block, 'cols', partners)]  3.72 us
    ppermute x1, starting transfers between devices, per_device(): lax.ppermute(normed, 'cols', far_pairs(chip_count, step, 2))  3.64 us
    ppermute x1, starting transfers between devices, per_device(): row_a = lax.ppermute(row_a, 'rows', near_pairs(row_count, 0))  3.13 us
    ppermute x1, starting transfers between devices, per_device(): lax.ppermute(result, 'cols', [(j, i) for i, j in far_pairs(chip_count, st...  2.48 us
    ppermute x1, waiting for transfers between devices, per_device(): lax.ppermute(result, 'cols', [(j, i) for i, j in far_pairs(chip_count, st...  1.78 us
    ppermute x1, waiting for transfers between devices, per_device(): row_a = lax.ppermute(row_a, 'rows', near_pairs(row_count, 0))  1.49 us
  transfers between devices with their start and end apart: 13, of which 3 were waited for; matrix products, arithmetic and copies ran while one was open for 0% of the time, Pallas kernels for 16%

profile of v7, /device:TPU:0, one launch (start us, length us, event | category | flops | bytes accessed | tf_op | source)
XLA Modules:
  0.0 34.8 jit_solution(15226369393465252170)
XLA Ops:
  0.0 0.0 copy-start.1
  0.0 0.0 copy-start.2
  0.0 0.0 copy-start.8
  0.0 0.0 copy-start
  0.0 1.0 %edge_rows.1 = (bf16[3,32,384]{2,1,0:T(8,128)(2,1)S(1)}, bf16[3,32,384]{2,1,0:T(8,128)(2,1)S(1)}) custom-call(bf16[1,2,4,32,384]{4,3,2,1,0:T(8,128)(2,1)} %cache.5, bf16[1,4,32,384]{3,2,1,0:T(8,128)(2,1)} %hidden.5), custom_call_target="tpu_custom_call" | custom-call | flops 10000000000 | bytes 10000000 | tf_op jit(solution)/shard_map/edge_rows/pallas_call | solution.py:338
  1.0 3.1 %collective-permute-start = (bf16[3,32,384]{2,1,0:T(8,128)(2,1)S(1)}, bf16[3,32,384]{2,1,0:T(8,128)(2,1)S(1)}, u32[]{:S(2)}, u32[]{:S(2)}) collective-permute-start(bf16[3,32,384]{2,1,0:T(8,128)(2,1)S(1)} %get-tuple-element.21), channel_id=1, source_target_pairs={{0,4},{4,0},{8,12},{12,8},{1,5},{5,1},{9,13},{13,9},{2,6},{6,2},{1... | collective-permute-start | bytes 221192 | tf_op jit(solution)/shard_map/ppermute | solution.py:348
  4.2 0.0 copy-start.7
  4.2 0.0 copy-start.9
  4.2 0.0 copy-start.10
  4.2 0.0 copy-start.5
  4.2 0.0 copy-start.6
  4.2 0.0 copy-start.11
  4.2 0.8 %collective-permute-start.1 = (bf16[3,32,384]{2,1,0:T(8,128)(2,1)S(1)}, bf16[3,32,384]{2,1,0:T(8,128)(2,1)S(1)}, u32[]{:S(2)}, u32[]{:S(2)}) collective-permute-start(bf16[3,32,384]{2,1,0:T(8,128)(2,1)S(1)} %get-tuple-element.22), channel_id=1, source_target_pairs={{4,8},{8,4},{5,9},{9,5},{6,10},{10,6},{7,11},{11,7},{20,24},{24,20... | collective-permute-start | bytes 221192 | tf_op jit(solution)/shard_map/ppermute | solution.py:349
  5.0 1.5 %collective-permute-done.row_a = bf16[3,32,384]{2,1,0:T(8,128)(2,1)S(1)} collective-permute-done((bf16[3,32,384]{2,1,0:T(8,128)(2,1)S(1)}, bf16[3,32,384]{2,1,0:T(8,128)(2,1)S(1)}, u32[]{:S(2)}, u32[]{:S(2)}) %collective-permute-start) | collective-permute-done | bytes 73760 | tf_op jit(solution)/shard_map/ppermute | solution.py:348
  6.5 0.0 collective-permute-done.1.row_b
  6.5 0.0 copy-done.1
  6.5 0.0 copy-done.2
  6.5 0.0 copy-done.8
  6.5 0.0 copy-done
  6.5 0.5 %shard_map.136 = (bf16[18,384]{1,0:T(8,128)(2,1)S(1)}, f32[8,384]{1,0:T(8,128)S(1)}) custom-call(bf16[1,2,4,32,384]{4,3,2,1,0:T(8,128)(2,1)S(1)} %copy-done.1, bf16[1,4,32,384]{3,2,1,0:T(8,128)(2,1)S(1)} %copy-done.2, bf16[3,32,384]{2,1,0:T(8,128)(2,1)S(1)} %collective-permute-done.row_a, bf16[3,32,384]{2,1,0:T(8,128)(2,1)S(1)} %collective-permute-done.1.row_b, ...), custom_call_target="tpu_custom_call" | custom-call | tf_op jit(solution)/shard_map/pallas_call | solution.py:305
  7.0 0.0 copy-start.3
  7.0 0.0 copy-start.12
  7.1 0.0 copy-start.13
  7.1 0.1 collective-permute-start.2
  7.2 0.8 %collective-permute-start.3 = (f32[8,384]{1,0:T(8,128)S(1)}, f32[8,384]{1,0:T(8,128)S(1)}, u32[]{:S(2)}, u32[]{:S(2)}) collective-permute-start(f32[8,384]{1,0:T(8,128)S(1)} %get-tuple-element.24), channel_id=1, source_target_pairs={{1,2},{2,1},{5,6},{6,5},{9,10},{10,9},{13,14},{14,13},{17,18},{18,... | collective-permute-start | bytes 36872 | tf_op jit(solution)/shard_map/ppermute | solution.py:364
  8.0 0.4 %collective-permute-done.2.inner = bf16[18,384]{1,0:T(8,128)(2,1)S(1)} collective-permute-done((bf16[18,384]{1,0:T(8,128)(2,1)S(1)}, bf16[18,384]{1,0:T(8,128)(2,1)S(1)}, u32[]{:S(2)}, u32[]{:S(2)}) %collective-permute-start.2) | collective-permute-done | bytes 13856 | tf_op jit(solution)/shard_map/ppermute | solution.py:363
  8.3 1.8 %shard_map.137.convolved = f32[128,384]{1,0:T(8,128)S(1)} custom-call(bf16[1,2,4,32,384]{4,3,2,1,0:T(8,128)(2,1)S(1)} %copy-done.1, bf16[1,4,32,384]{3,2,1,0:T(8,128)(2,1)S(1)} %copy-done.2, bf16[3,32,384]{2,1,0:T(8,128)(2,1)S(1)} %collective-permute-done.row_a, bf16[3,32,384]{2,1,0:T(8,128)(2,1)S(1)} %collective-permute-done.1.row_b, ...), custom_call_target="tpu_custom_call" | custom-call | tf_op jit(solution)/shard_map/pallas_call | solution.py:305
  10.1 0.0 collective-permute-done.3.outer
  10.1 0.0 copy-done.7
  10.1 0.0 copy-done.9
  10.2 0.0 copy-done.10
  10.2 0.2 shard_map.138
  10.3 4.1 %collective-permute-start.6 = (bf16[128,384]{1,0:T(8,128)(2,1)S(1)}, bf16[128,384]{1,0:T(8,128)(2,1)S(1)}, u32[]{:S(2)}, u32[]{:S(2)}) collective-permute-start(bf16[128,384]{1,0:T(8,128)(2,1)S(1)} %get-tuple-element.25.refs_0_.refs_1_), channel_id=1, source_target_pairs={{0,12},{4,8},{8,4},{12,0},{1,13},{5,9},{9,5},{13,1},{2,14},{6,10},... | collective-permute-start | bytes 294920 | tf_op jit(solution)/shard_map/ppermute | solution.py:401
  14.4 2.7 %collective-permute-start.8 = (bf16[128,384]{1,0:T(8,128)(2,1)S(1)}, bf16[128,384]{1,0:T(8,128)(2,1)S(1)}, u32[]{:S(2)}, u32[]{:S(2)}) collective-permute-start(bf16[128,384]{1,0:T(8,128)(2,1)S(1)} %get-tuple-element.25.refs_0_.refs_1_), channel_id=1, source_target_pairs={{0,8},{4,12},{8,0},{12,4},{1,9},{5,13},{9,1},{13,5},{2,10},{6,14},... | collective-permute-start | bytes 294920 | tf_op jit(solution)/shard_map/ppermute | solution.py:401
  17.1 0.5 %collective-permute-start.10 = (bf16[128,384]{1,0:T(8,128)(2,1)S(1)}, bf16[128,384]{1,0:T(8,128)(2,1)S(1)}, u32[]{:S(2)}, u32[]{:S(2)}) collective-permute-start(bf16[128,384]{1,0:T(8,128)(2,1)S(1)} %get-tuple-element.25.refs_0_.refs_1_), channel_id=1, source_target_pairs={{0,4},{4,0},{8,12},{12,8},{1,5},{5,1},{9,13},{13,9},{2,6},{6,2},{1... | collective-permute-start | bytes 294920 | tf_op jit(solution)/shard_map/ppermute | solution.py:401
  17.6 3.6 %collective-permute-start.4 = (bf16[128,384]{1,0:T(8,128)(2,1)S(1)}, bf16[128,384]{1,0:T(8,128)(2,1)S(1)}, u32[]{:S(2)}, u32[]{:S(2)}) collective-permute-start(bf16[128,384]{1,0:T(8,128)(2,1)S(1)} %get-tuple-element.25.refs_0_.refs_1_), channel_id=1, source_target_pairs={{0,2},{1,3},{2,0},{3,1},{4,6},{5,7},{6,4},{7,5},{8,10},{9,11},{10,... | collective-permute-start | bytes 294920 | tf_op jit(solution)/shard_map/ppermute | solution.py:404
  21.3 0.0 collective-permute-start.5
  21.3 0.0 collective-permute-done.6.refs_4_
  21.3 0.5 %collective-permute-start.7 = (bf16[128,384]{1,0:T(8,128)(2,1)S(1)}, bf16[128,384]{1,0:T(8,128)(2,1)S(1)}, u32[]{:S(2)}, u32[]{:S(2)}) collective-permute-start(bf16[128,384]{1,0:T(8,128)(2,1)S(1)} %collective-permute-done.6.refs_4_), channel_id=1, source_target_pairs={{0,1},{1,0},{2,3},{3,2},{4,5},{5,4},{6,7},{7,6},{8,9},{9,8},{10,11... | collective-permute-start | bytes 294920 | tf_op jit(solution)/shard_map/ppermute | solution.py:407
  21.8 0.0 collective-permute-done.8.refs_4_
  21.8 3.2 %collective-permute-start.9 = (bf16[128,384]{1,0:T(8,128)(2,1)S(1)}, bf16[128,384]{1,0:T(8,128)(2,1)S(1)}, u32[]{:S(2)}, u32[]{:S(2)}) collective-permute-start(bf16[128,384]{1,0:T(8,128)(2,1)S(1)} %collective-permute-done.8.refs_4_), channel_id=1, source_target_pairs={{0,1},{1,0},{2,3},{3,2},{4,5},{5,4},{6,7},{7,6},{8,9},{9,8},{10,11... | collective-permute-start | bytes 294920 | tf_op jit(solution)/shard_map/ppermute | solution.py:407
  25.0 0.0 collective-permute-done.10.refs_6_
  25.0 0.0 collective-permute-start.11
  25.0 0.0 collective-permute-done.4.refs_1_
  25.0 0.0 copy-done.5
  25.0 0.0 copy-done.6
  25.0 0.0 copy-done.11
  25.0 0.6 %shard_map.139.refs_0_ = bf16[256,384]{1,0:T(8,128)(2,1)S(1)} custom-call(bf16[128,384]{1,0:T(8,128)(2,1)S(1)} %get-tuple-element.25.refs_0_.refs_1_, bf16[128,384]{1,0:T(8,128)(2,1)S(1)} %collective-permute-done.4.refs_1_, bf16[384,384]{1,0:T(8,128)(2,1)S(1)} %copy-done.5, f32[384]{0:T(512)S(1)} %copy-done.11, bf16[384,384]{1,0:T(8,128)(2,1)S(1)} %copy-done.6), custom_call_target="tpu_custom_call" | custom-call | tf_op jit(solution)/shard_map/pallas_call | solution.py:305
  25.7 0.0 collective-permute-done.5.refs_2_
  25.7 0.8 %shard_map.140 = (f32[256,128]{1,0:T(8,128)S(1)}, f32[256,128]{1,0:T(8,128)S(1)}, f32[256,384]{1,0:T(8,128)S(1)}) custom-call(bf16[256,384]{1,0:T(8,128)(2,1)S(1)} %shard_map.139.refs_0_, bf16[128,384]{1,0:T(8,128)(2,1)S(1)} %get-tuple-element.25.refs_0_.refs_1_, bf16[128,384]{1,0:T(8,128)(2,1)S(1)} %collective-permute-done.5.refs_2_), custom_call_target="tpu_custom_call" | custom-call | tf_op jit(solution)/shard_map/pallas_call | solution.py:305
  26.5 0.0 collective-permute-done.7.refs_5_
  26.5 1.0 %shard_map.141 = (f32[256,128]{1,0:T(8,128)S(1)}, f32[256,128]{1,0:T(8,128)S(1)}, f32[256,384]{1,0:T(8,128)S(1)}) custom-call(bf16[256,384]{1,0:T(8,128)(2,1)S(1)} %shard_map.139.refs_0_, f32[256,128]{1,0:T(8,128)S(1)} %get-tuple-element.26.refs_1_, f32[256,128]{1,0:T(8,128)S(1)} %get-tuple-element.27.refs_2_, f32[256,384]{1,0:T(8,128)S(1)} %get-tuple-element.28.refs_3_, ...), custom_call_target="tpu_custom_call" | custom-call | tf_op jit(solution)/shard_map/pallas_call | solution.py:305
  27.5 0.0 collective-permute-done.9.refs_5_
  27.5 0.0 collective-permute-done.11.refs_7_
  27.5 0.8 %shard_map.144 = bf16[136,384]{1,0:T(8,128)(2,1)S(1)} custom-call(bf16[256,384]{1,0:T(8,128)(2,1)S(1)} %shard_map.139.refs_0_, f32[256,128]{1,0:T(8,128)S(1)} %get-tuple-element.29.refs_1_, f32[256,128]{1,0:T(8,128)S(1)} %get-tuple-element.30.refs_2_, f32[256,384]{1,0:T(8,128)S(1)} %get-tuple-element.31.refs_3_, ...), custom_call_target="tpu_custom_call" | custom-call | tf_op jit(solution)/shard_map/pallas_call | solution.py:305
  28.3 2.5 %collective-permute-start.12 = (bf16[136,384]{1,0:T(8,128)(2,1)S(1)}, bf16[136,384]{1,0:T(8,128)(2,1)S(1)}, u32[]{:S(2)}, u32[]{:S(2)}) collective-permute-start(bf16[136,384]{1,0:T(8,128)(2,1)S(1)} %shard_map.144), channel_id=1, source_target_pairs={{2,0},{3,1},{0,2},{1,3},{6,4},{7,5},{4,6},{5,7},{10,8},{11,9},{8,1... | collective-permute-start | bytes 313352 | tf_op jit(solution)/shard_map/ppermute | solution.py:446
  30.8 0.0 copy-done.3
  30.8 0.0 copy-done.4
  30.8 0.0 copy-done.12
  30.8 0.0 copy-done.13
  30.8 0.4 %shard_map.142 = (bf16[384,384]{1,0:T(8,128)(2,1)S(1)}, f32[8,384]{1,0:T(8,128)S(1)}) custom-call(bf16[384,384]{1,0:T(8,128)(2,1)S(1)} %copy-done.3, f32[384]{0:T(512)S(1)} %copy-done.12, bf16[384,384]{1,0:T(8,128)(2,1)S(1)} %copy-done.4, f32[384]{0:T(512)S(1)} %copy-done.13), custom_call_target="tpu_custom_call" | custom-call | tf_op jit(solution)/shard_map/pallas_call | solution.py:305
  31.2 0.9 %shard_map.143 = (f32[128,384]{1,0:T(8,128)S(1)}, f32[128,128]{1,0:T(8,128)S(1)}) custom-call(bf16[256,384]{1,0:T(8,128)(2,1)S(1)} %shard_map.139.refs_0_, f32[256,128]{1,0:T(8,128)S(1)} %get-tuple-element.29.refs_1_, f32[256,128]{1,0:T(8,128)S(1)} %get-tuple-element.30.refs_2_, f32[256,384]{1,0:T(8,128)S(1)} %get-tuple-element.31.refs_3_, ...), custom_call_target="tpu_custom_call" | custom-call | tf_op jit(solution)/shard_map/pallas_call | solution.py:305
  32.1 1.8 %collective-permute-done.12.refs_2_ = bf16[136,384]{1,0:T(8,128)(2,1)S(1)} collective-permute-done((bf16[136,384]{1,0:T(8,128)(2,1)S(1)}, bf16[136,384]{1,0:T(8,128)(2,1)S(1)}, u32[]{:S(2)}, u32[]{:S(2)}) %collective-permute-start.12) | collective-permute-done | bytes 104480 | tf_op jit(solution)/shard_map/ppermute | solution.py:446
  33.9 0.9 %shard_map.145 = bf16[128,384]{1,0:T(8,128)(2,1)} custom-call(f32[128,384]{1,0:T(8,128)S(1)} %get-tuple-element.33.refs_0_, f32[128,128]{1,0:T(8,128)S(1)} %get-tuple-element.34.refs_1_, bf16[136,384]{1,0:T(8,128)(2,1)S(1)} %collective-permute-done.12.refs_2_, bf16[128,384]{1,0:T(8,128)(2,1)S(1)} %get-tuple-element.35.refs_3_, ...), custom_call_target="tpu_custom_call" | custom-call | tf_op jit(solution)/shard_map/pallas_call | solution.py:305
  (1 shorter events, 0.0 us)
Async XLA Ops:
  0.0 6.5 %copy-start.1 = (bf16[1,2,4,32,384]{4,3,2,1,0:T(8,128)(2,1)S(1)}, bf16[1,2,4,32,384]{4,3,2,1,0:T(8,128)(2,1)}, u32[]{:S(2)}) copy-start(bf16[1,2,4,32,384]{4,3,2,1,0:T(8,128)(2,1)} %cache.5) | copy-start | bytes 589828
  0.0 6.5 %copy-start.2 = (bf16[1,4,32,384]{3,2,1,0:T(8,128)(2,1)S(1)}, bf16[1,4,32,384]{3,2,1,0:T(8,128)(2,1)}, u32[]{:S(2)}) copy-start(bf16[1,4,32,384]{3,2,1,0:T(8,128)(2,1)} %hidden.5) | copy-start | bytes 294916
  0.0 6.5 %copy-start.8 = (f32[384]{0:T(512)S(1)}, f32[384]{0:T(512)}, u32[]{:S(2)}) copy-start(f32[384]{0:T(512)} %gain_one.3) | copy-start | bytes 4612
  0.0 6.5 %copy-start = (bf16[3,3,3,384,384]{4,3,2,1,0:T(8,128)(2,1)S(1)}, bf16[3,3,3,384,384]{4,3,2,1,0:T(8,128)(2,1)}, u32[]{:S(2)}) copy-start(bf16[3,3,3,384,384]{4,3,2,1,0:T(8,128)(2,1)} %weight.3) | copy-start | bytes 23887876
  1.0 5.5 %collective-permute-start = (bf16[3,32,384]{2,1,0:T(8,128)(2,1)S(1)}, bf16[3,32,384]{2,1,0:T(8,128)(2,1)S(1)}, u32[]{:S(2)}, u32[]{:S(2)}) collective-permute-start(bf16[3,32,384]{2,1,0:T(8,128)(2,1)S(1)} %get-tuple-element.21), channel_id=1, source_target_pairs={{0,4},{4,0},{8,12},{12,8},{1,5},{5,1},{9,13},{13,9},{2,6},{6,2},{1... | collective-permute-start | bytes 221192 | tf_op jit(solution)/shard_map/ppermute | solution.py:348
  4.2 6.0 %copy-start.7 = (bf16[1,4,32,384]{3,2,1,0:T(8,128)(2,1)S(1)}, bf16[1,4,32,384]{3,2,1,0:T(8,128)(2,1)}, u32[]{:S(2)}) copy-start(bf16[1,4,32,384]{3,2,1,0:T(8,128)(2,1)} %shortcut.1) | copy-start | bytes 294916
  4.2 6.0 %copy-start.9 = (f32[384]{0:T(512)S(1)}, f32[384]{0:T(512)}, u32[]{:S(2)}) copy-start(f32[384]{0:T(512)} %conv_bias.1) | copy-start | bytes 4612
  4.2 6.0 %copy-start.10 = (f32[384]{0:T(512)S(1)}, f32[384]{0:T(512)}, u32[]{:S(2)}) copy-start(f32[384]{0:T(512)} %gain_two.1) | copy-start | bytes 4612
  4.2 20.8 %copy-start.5 = (bf16[384,384]{1,0:T(8,128)(2,1)S(1)}, bf16[384,384]{1,0:T(8,128)(2,1)}, u32[]{:S(2)}) copy-start(bf16[384,384]{1,0:T(8,128)(2,1)} %refs_2_.1) | copy-start | bytes 884740
  4.2 20.8 %copy-start.6 = (bf16[384,384]{1,0:T(8,128)(2,1)S(1)}, bf16[384,384]{1,0:T(8,128)(2,1)}, u32[]{:S(2)}) copy-start(bf16[384,384]{1,0:T(8,128)(2,1)} %refs_4_.1) | copy-start | bytes 884740
  4.2 20.8 %copy-start.11 = (f32[384]{0:T(512)S(1)}, f32[384]{0:T(512)}, u32[]{:S(2)}) copy-start(f32[384]{0:T(512)} %refs_3_.1) | copy-start | bytes 4612
  4.2 2.3 %collective-permute-start.1 = (bf16[3,32,384]{2,1,0:T(8,128)(2,1)S(1)}, bf16[3,32,384]{2,1,0:T(8,128)(2,1)S(1)}, u32[]{:S(2)}, u32[]{:S(2)}) collective-permute-start(bf16[3,32,384]{2,1,0:T(8,128)(2,1)S(1)} %get-tuple-element.22), channel_id=1, source_target_pairs={{4,8},{8,4},{5,9},{9,5},{6,10},{10,6},{7,11},{11,7},{20,24},{24,20... | collective-permute-start | bytes 221192 | tf_op jit(solution)/shard_map/ppermute | solution.py:349
  7.0 23.7 %copy-start.3 = (bf16[384,384]{1,0:T(8,128)(2,1)S(1)}, bf16[384,384]{1,0:T(8,128)(2,1)}, u32[]{:S(2)}) copy-start(bf16[384,384]{1,0:T(8,128)(2,1)} %value_weight.1) | copy-start | bytes 884740
  7.0 23.7 %copy-start.4 = (bf16[384,384]{1,0:T(8,128)(2,1)S(1)}, bf16[384,384]{1,0:T(8,128)(2,1)}, u32[]{:S(2)}) copy-start(bf16[384,384]{1,0:T(8,128)(2,1)} %out_weight.1) | copy-start | bytes 884740
  7.0 23.7 %copy-start.12 = (f32[384]{0:T(512)S(1)}, f32[384]{0:T(512)}, u32[]{:S(2)}) copy-start(f32[384]{0:T(512)} %value_bias.1) | copy-start | bytes 4612
  7.1 23.7 %copy-start.13 = (f32[384]{0:T(512)S(1)}, f32[384]{0:T(512)}, u32[]{:S(2)}) copy-start(f32[384]{0:T(512)} %out_bias.1) | copy-start | bytes 4612
  7.1 1.3 %collective-permute-start.2 = (bf16[18,384]{1,0:T(8,128)(2,1)S(1)}, bf16[18,384]{1,0:T(8,128)(2,1)S(1)}, u32[]{:S(2)}, u32[]{:S(2)}) collective-permute-start(bf16[18,384]{1,0:T(8,128)(2,1)S(1)} %get-tuple-element.23), channel_id=1, source_target_pairs={{0,1},{1,0},{2,3},{3,2},{4,5},{5,4},{6,7},{7,6},{8,9},{9,8},{10,11... | collective-permute-start | bytes 41480 | tf_op jit(solution)/shard_map/ppermute | solution.py:363
  7.2 3.0 %collective-permute-start.3 = (f32[8,384]{1,0:T(8,128)S(1)}, f32[8,384]{1,0:T(8,128)S(1)}, u32[]{:S(2)}, u32[]{:S(2)}) collective-permute-start(f32[8,384]{1,0:T(8,128)S(1)} %get-tuple-element.24), channel_id=1, source_target_pairs={{1,2},{2,1},{5,6},{6,5},{9,10},{10,9},{13,14},{14,13},{17,18},{18,... | collective-permute-start | bytes 36872 | tf_op jit(solution)/shard_map/ppermute | solution.py:364
  10.3 10.9 %collective-permute-start.6 = (bf16[128,384]{1,0:T(8,128)(2,1)S(1)}, bf16[128,384]{1,0:T(8,128)(2,1)S(1)}, u32[]{:S(2)}, u32[]{:S(2)}) collective-permute-start(bf16[128,384]{1,0:T(8,128)(2,1)S(1)} %get-tuple-element.25.refs_0_.refs_1_), channel_id=1, source_target_pairs={{0,12},{4,8},{8,4},{12,0},{1,13},{5,9},{9,5},{13,1},{2,14},{6,10},... | collective-permute-start | bytes 294920 | tf_op jit(solution)/shard_map/ppermute | solution.py:401
  14.4 7.3 %collective-permute-start.8 = (bf16[128,384]{1,0:T(8,128)(2,1)S(1)}, bf16[128,384]{1,0:T(8,128)(2,1)S(1)}, u32[]{:S(2)}, u32[]{:S(2)}) collective-permute-start(bf16[128,384]{1,0:T(8,128)(2,1)S(1)} %get-tuple-element.25.refs_0_.refs_1_), channel_id=1, source_target_pairs={{0,8},{4,12},{8,0},{12,4},{1,9},{5,13},{9,1},{13,5},{2,10},{6,14},... | collective-permute-start | bytes 294920 | tf_op jit(solution)/shard_map/ppermute | solution.py:401
  17.1 7.9 %collective-permute-start.10 = (bf16[128,384]{1,0:T(8,128)(2,1)S(1)}, bf16[128,384]{1,0:T(8,128)(2,1)S(1)}, u32[]{:S(2)}, u32[]{:S(2)}) collective-permute-start(bf16[128,384]{1,0:T(8,128)(2,1)S(1)} %get-tuple-element.25.refs_0_.refs_1_), channel_id=1, source_target_pairs={{0,4},{4,0},{8,12},{12,8},{1,5},{5,1},{9,13},{13,9},{2,6},{6,2},{1... | collective-permute-start | bytes 294920 | tf_op jit(solution)/shard_map/ppermute | solution.py:401
  17.6 7.4 %collective-permute-start.4 = (bf16[128,384]{1,0:T(8,128)(2,1)S(1)}, bf16[128,384]{1,0:T(8,128)(2,1)S(1)}, u32[]{:S(2)}, u32[]{:S(2)}) collective-permute-start(bf16[128,384]{1,0:T(8,128)(2,1)S(1)} %get-tuple-element.25.refs_0_.refs_1_), channel_id=1, source_target_pairs={{0,2},{1,3},{2,0},{3,1},{4,6},{5,7},{6,4},{7,5},{8,10},{9,11},{10,... | collective-permute-start | bytes 294920 | tf_op jit(solution)/shard_map/ppermute | solution.py:404
  21.3 4.4 %collective-permute-start.5 = (bf16[128,384]{1,0:T(8,128)(2,1)S(1)}, bf16[128,384]{1,0:T(8,128)(2,1)S(1)}, u32[]{:S(2)}, u32[]{:S(2)}) collective-permute-start(bf16[128,384]{1,0:T(8,128)(2,1)S(1)} %get-tuple-element.25.refs_0_.refs_1_), channel_id=1, source_target_pairs={{0,1},{1,0},{2,3},{3,2},{4,5},{5,4},{6,7},{7,6},{8,9},{9,8},{10,11... | collective-permute-start | bytes 294920 | tf_op jit(solution)/shard_map/ppermute | solution.py:407
  21.3 5.2 %collective-permute-start.7 = (bf16[128,384]{1,0:T(8,128)(2,1)S(1)}, bf16[128,384]{1,0:T(8,128)(2,1)S(1)}, u32[]{:S(2)}, u32[]{:S(2)}) collective-permute-start(bf16[128,384]{1,0:T(8,128)(2,1)S(1)} %collective-permute-done.6.refs_4_), channel_id=1, source_target_pairs={{0,1},{1,0},{2,3},{3,2},{4,5},{5,4},{6,7},{7,6},{8,9},{9,8},{10,11... | collective-permute-start | bytes 294920 | tf_op jit(solution)/shard_map/ppermute | solution.py:407
  21.8 5.7 %collective-permute-start.9 = (bf16[128,384]{1,0:T(8,128)(2,1)S(1)}, bf16[128,384]{1,0:T(8,128)(2,1)S(1)}, u32[]{:S(2)}, u32[]{:S(2)}) collective-permute-start(bf16[128,384]{1,0:T(8,128)(2,1)S(1)} %collective-permute-done.8.refs_4_), channel_id=1, source_target_pairs={{0,1},{1,0},{2,3},{3,2},{4,5},{5,4},{6,7},{7,6},{8,9},{9,8},{10,11... | collective-permute-start | bytes 294920 | tf_op jit(solution)/shard_map/ppermute | solution.py:407
  25.0 2.5 %collective-permute-start.11 = (bf16[128,384]{1,0:T(8,128)(2,1)S(1)}, bf16[128,384]{1,0:T(8,128)(2,1)S(1)}, u32[]{:S(2)}, u32[]{:S(2)}) collective-permute-start(bf16[128,384]{1,0:T(8,128)(2,1)S(1)} %collective-permute-done.10.refs_6_), channel_id=1, source_target_pairs={{0,1},{1,0},{2,3},{3,2},{4,5},{5,4},{6,7},{7,6},{8,9},{9,8},{10,11... | collective-permute-start | bytes 294920 | tf_op jit(solution)/shard_map/ppermute | solution.py:407
  28.3 5.6 %collective-permute-start.12 = (bf16[136,384]{1,0:T(8,128)(2,1)S(1)}, bf16[136,384]{1,0:T(8,128)(2,1)S(1)}, u32[]{:S(2)}, u32[]{:S(2)}) collective-permute-start(bf16[136,384]{1,0:T(8,128)(2,1)S(1)} %shard_map.144), channel_id=1, source_target_pairs={{2,0},{3,1},{0,2},{1,3},{6,4},{7,5},{4,6},{5,7},{10,8},{11,9},{8,1... | collective-permute-start | bytes 313352 | tf_op jit(solution)/shard_map/ppermute | solution.py:446
